TPU v7x, 32 devices: a whole 2x2x4 slice. The times are simulated.
32 devices in a mesh: groups: 2 (over x), tile: 16 (over z, y, core).
Axes of the slice: x: 2, y: 2, z: 4, core: 2. Of those that a mesh axis runs over, the one named last changes fastest.
Arguments:
- queries: bfloat16 [2048, 4096], P(('groups', 'tile')), parts along dimension 0, may hold values from -8 to 8
- key_rows: bfloat16 [2048, 4096], P(('groups', 'tile')), parts along dimension 0, may hold values from -8 to 8
- values: bfloat16 [2048, 4096], P(('groups', 'tile')), parts along dimension 0, may hold values from -6 to 6
- modulation: float32 [6, 4096], P('groups'), parts along dimension 0, may hold values from -3 to 3
- expert_in: bfloat16 [4096, 8192], P(None, 'tile'), may hold values from -0.09375 to 0.09375
- expert_out: bfloat16 [8192, 4096], P('tile'), may hold values from -0.125 to 0.125
- routes: int32 [2048, 2], P(('groups', 'tile')), parts along dimension 0, may hold values from 0 to 3, all different within a row; in each aligned block of 64 rows (0 to 63, 64 to 127, ...) at most 48 rows name the same one
- gate_fixed: int32 [2048, 2], P(('groups', 'tile')), parts along dimension 0, may hold values from 64 to 1023
Outputs:
- layer_out: bfloat16 [2048, 4096], P(('groups', 'tile')), parts along dimension 0
There are 2 independent parts, one for each index of `groups`. A program takes and returns all parts, laid end to end along the dimension named above; an argument that names none is the same for every part. Nothing has to cross between parts.
Inputs may be any that keep to these rules, and one draw needn't show every extreme that they name: `routes`: the two experts of a token differ; among the 64 tokens of one tile no expert is named more than 48 times.
All inputs are finite; a program needn't handle non-finite values.
Results may differ from a plain program's by a relative error of at most 0.011.
Values may be sent and summed in bfloat16 or wider, within the bound.
No kernel may reach another device: no remote copies, remote signals or barrier semaphores. Data moves between devices by JAX's collectives and lax.ppermute only.
A program may use at most 128 MiB of HBM per device.

v0:
```python
import functools
import math

import jax
import jax.numpy as jnp
from jax import lax
from jax.experimental import pallas as pl
from jax.experimental.pallas import tpu as pltpu
from jax.sharding import PartitionSpec as P


HEAD_DIM = 128
SPLIT = 4
TILE_COLS = 8
CORES = 2
EPSILON = 1e-06
MASKED = -1e30
HEADS = (12, 12, 8)
HEAD_GROUP = 4
HIDDEN_STEP = 256
KERNEL_VMEM = 40 * 2**20


def permute(x, pairs):
    return lax.ppermute(x, "tile", pairs)


def band_pairs(devices):
    rotation = TILE_COLS // 2
    grid_rows = devices // TILE_COLS
    device = lambda tile: (tile - rotation) % devices
    vertical = []
    if grid_rows == 2:
        vertical.append([(device(g), device((g + TILE_COLS) % devices)) for g in range(devices)])
    elif grid_rows > 2:
        for step in (TILE_COLS, -TILE_COLS):
            vertical.append(
                [
                    (device(g - step), device(g))
                    for g in range(devices)
                    if 0 <= g - step < devices
                ]
            )
    sides = []
    for step in (1, -1):
        pairs = []
        for g in range(devices):
            column = g % TILE_COLS
            if not 0 <= column - step < TILE_COLS:
                continue
            source = g - step
            if grid_rows == 2 and {column, column - step} == {rotation - 1, rotation}:
                source = (source + TILE_COLS) % devices
            pairs.append((device(source), device(g)))
        sides.append(pairs)
    return vertical, sides


def attention_kernel(heads, sources, last, flags_ref, q_ref, k_ref, v_ref, *refs):
    around = refs[: sources - 1]
    rest = refs[sources - 1 :]
    if last:
        modulation_ref = rest[0]
        before = rest[1:-2]
        out_ref, normed_ref = rest[-2:]
    else:
        (out_ref,) = rest
    rows = q_ref.shape[0]
    lane = lax.broadcasted_iota(jnp.int32, (1, sources * rows), 1)
    bias = jnp.zeros((1, sources * rows), jnp.float32)
    for j in range(sources):
        closed = jnp.where(flags_ref[j] > 0, 0.0, MASKED).astype(jnp.float32)
        bias = jnp.where((lane >= j * rows) & (lane < (j + 1) * rows), closed, bias)
    scale = 1.0 / math.sqrt(HEAD_DIM)
    for first in range(0, heads, HEAD_GROUP):
        cols = [
            slice(h * HEAD_DIM, (h + 1) * HEAD_DIM)
            for h in range(first, min(heads, first + HEAD_GROUP))
        ]
        keys = [jnp.concatenate([k_ref[:, c]] + [r[0, :, c] for r in around], axis=0) for c in cols]
        scores = [
            lax.dot_general(
                q_ref[:, c], k, (((1,), (1,)), ((), ())), preferred_element_type=jnp.float32
            )
            for c, k in zip(cols, keys)
        ]
        scores = [jnp.where(bias < 0.0, MASKED, x * scale) for x in scores]
        highest = [jnp.max(x, axis=-1, keepdims=True) for x in scores]
        raised = [jnp.exp(x - m) for x, m in zip(scores, highest)]
        total = [jnp.sum(x, axis=-1, keepdims=True) for x in raised]
        probs = [(x / t).astype(jnp.bfloat16) for x, t in zip(raised, total)]
        vals = [jnp.concatenate([v_ref[:, c]] + [r[1, :, c] for r in around], axis=0) for c in cols]
        pieces = [jnp.dot(p, v, preferred_element_type=jnp.float32) for p, v in zip(probs, vals)]
        for c, piece in zip(cols, pieces):
            out_ref[:, c] = piece.astype(jnp.bfloat16)
    if last:
        blocks = [ref[...] for ref in before] + [out_ref[...]]
        count = sum(block.shape[1] for block in blocks)
        wide = [block.astype(jnp.float32) for block in blocks]
        center = sum(jnp.sum(w, axis=-1, keepdims=True) for w in wide) / count
        spread = sum(jnp.sum(jnp.square(w - center), axis=-1, keepdims=True) for w in wide) / count
        factor = lax.rsqrt(spread + EPSILON)
        start = 0
        for w in wide:
            cols = slice(start, start + w.shape[1])
            start += w.shape[1]
            normed_ref[:, cols] = (
                (w - center) * factor * (1.0 + modulation_ref[1:2, cols])
                + modulation_ref[0:1, cols]
            ).astype(jnp.bfloat16)


def attend_chunk(start, part, flags, queries, key_rows, values, around, before, modulation):
    rows, width = queries.shape
    sources = 1 + len(around)
    last = modulation is not None
    window = start // part
    flat = pl.BlockSpec((rows, part), lambda i, f: (0, window))
    deep = pl.BlockSpec((2, rows, part), lambda i, f: (0, 0, window))
    whole = lambda x: pl.BlockSpec(x.shape, lambda i, f: (0,) * x.ndim)
    operands = [queries, key_rows, values] + around
    specs = [flat] * 3 + [deep if x.shape[2] == width else whole(x) for x in around]
    out_shape = [jax.ShapeDtypeStruct((rows, part), jnp.bfloat16)]
    if last:
        operands += [modulation] + before
        specs += [whole(x) for x in [modulation] + before]
        out_shape.append(jax.ShapeDtypeStruct((rows, width), jnp.bfloat16))
    return pl.pallas_call(
        functools.partial(attention_kernel, part // HEAD_DIM, sources, last),
        out_shape=out_shape,
        grid_spec=pltpu.PrefetchScalarGridSpec(
            num_scalar_prefetch=1,
            grid=(1,),
            in_specs=specs,
            out_specs=[whole(x) for x in out_shape],
        ),
        compiler_params=pltpu.CompilerParams(vmem_limit_bytes=KERNEL_VMEM),
        cost_estimate=pl.CostEstimate(
            flops=4 * rows * sources * rows * part,
            bytes_accessed=(2 * sources + 2) * rows * part * 2,
            transcendentals=rows * rows * sources * part // HEAD_DIM,
        ),
        name="attend_last" if last else "attend",
    )(flags, *operands)


def experts_kernel(shifts, pieces, mine_ref, index_ref, meta_ref, *refs):
    blocks = len(shifts)
    inputs = refs[: sum(pieces)]
    in_a, in_b, out_a, out_b = refs[sum(pieces) : sum(pieces) + 4]
    outs = refs[sum(pieces) + 4 : sum(pieces) + 4 + blocks]
    x_ref, total_ref, first_ref, second_ref, first_sem, second_sem = refs[
        sum(pieces) + 4 + blocks :
    ]
    steps, _, step = first_ref.shape
    for j in range(steps):
        source_in, source_out = (in_a, out_a) if j < steps // 2 else (in_b, out_b)
        span = pl.ds(j % (steps // 2) * step, step)
        pltpu.make_async_copy(source_in.at[:, span], first_ref.at[j], first_sem.at[j]).start()
        pltpu.make_async_copy(source_out.at[span], second_ref.at[j], second_sem.at[j]).start()
    start = 0
    for ref in inputs:
        x_ref[start : start + ref.shape[0], :] = ref[...]
        start += ref.shape[0]
    rows = start // blocks
    total_ref[...] = jnp.zeros_like(total_ref)

    def body(j, carry):
        first, second = first_ref.at[j], second_ref.at[j]
        pltpu.make_async_copy(first, first, first_sem.at[j]).wait()
        wide = jnp.dot(x_ref[...], first[...], preferred_element_type=jnp.float32)
        hidden = jax.nn.gelu(wide, approximate=True).astype(jnp.bfloat16)
        pltpu.make_async_copy(second, second, second_sem.at[j]).wait()
        total_ref[...] += jnp.dot(hidden, second[...], preferred_element_type=jnp.float32)
        return carry

    lax.fori_loop(0, steps, body, 0)
    for i, out in enumerate(outs):
        block = meta_ref[index_ref[shifts[i]]]
        chosen = jnp.where(block[:, :2] == mine_ref[0], block[:, 2:], 0)
        gate = jnp.sum(chosen, axis=1, keepdims=True).astype(jnp.float32) / 1024.0
        out[...] = (total_ref[i * rows : (i + 1) * rows, :] * gate).astype(jnp.bfloat16)


def run_experts(shifts, blocks, weights, mine, index, meta):
    pieces = [len(block) for block in blocks]
    rows = sum(x.shape[0] for x in blocks[0])
    flat = [x for block in blocks for x in block]
    width = flat[0].shape[1]
    count = len(blocks)
    hidden = sum(w.shape[1] for w in weights[:2])
    step = min(HIDDEN_STEP, weights[0].shape[1])
    steps = hidden // step
    resident = pl.BlockSpec(memory_space=pltpu.VMEM)
    scalar = pl.BlockSpec(memory_space=pltpu.SMEM)
    return pl.pallas_call(
        functools.partial(experts_kernel, shifts, pieces),
        out_shape=[jax.ShapeDtypeStruct((rows, width), jnp.bfloat16)] * count,
        in_specs=[scalar, scalar] + [resident] * (1 + len(flat)) + [pl.BlockSpec(memory_space=pl.ANY)] * 4,
        out_specs=[resident] * count,
        scratch_shapes=[
            pltpu.VMEM((count * rows, width), jnp.bfloat16),
            pltpu.VMEM((count * rows, width), jnp.float32),
            pltpu.VMEM((steps, width, step), jnp.bfloat16),
            pltpu.VMEM((steps, step, width), jnp.bfloat16),
            pltpu.SemaphoreType.DMA((steps,)),
            pltpu.SemaphoreType.DMA((steps,)),
        ],
        compiler_params=pltpu.CompilerParams(vmem_limit_bytes=KERNEL_VMEM),
        cost_estimate=pl.CostEstimate(
            flops=4 * count * rows * width * hidden,
            bytes_accessed=4 * width * hidden,
            transcendentals=count * rows * hidden,
        ),
        name="experts",
    )(mine, index, meta, *flat, *weights)


def ring_order(chips, grid_rows):
    if grid_rows == 2:
        return list(range(0, chips, 2)) + list(range(chips - 1, 0, -2))
    return list(range(chips))


def block(queries, key_rows, values, modulation, expert_in, expert_out, routes, gate_fixed):
    rows, width = queries.shape
    devices = lax.axis_size("tile")
    position = lax.axis_index("tile")
    grid_rows = devices // TILE_COLS
    tile = (position + TILE_COLS // 2) % devices
    grid_row, grid_col = tile // TILE_COLS, tile % TILE_COLS
    vertical, sides = band_pairs(devices)

    parts = [width * heads // sum(HEADS) for heads in HEADS]
    starts = [sum(parts[:c]) for c in range(len(parts))]
    kv = [
        jnp.stack([a[:, s : s + p] for a in (key_rows, values)]) for s, p in zip(starts, parts)
    ]
    above = [[permute(x, pairs) for pairs in vertical] for x in kv]
    own = jnp.stack([key_rows, values])
    beside = [permute(own, pairs) for pairs in sides]
    beyond = [[[permute(x, pairs) for pairs in sides] for x in above[c]] for c in range(len(parts))]

    swap = [(i, i ^ 1) for i in range(devices)]
    weights = [expert_in, permute(expert_in, swap), expert_out, permute(expert_out, swap)]
    chips = devices // CORES
    meta = jnp.concatenate([routes, gate_fixed], axis=1)[None]
    reach = 1
    while reach < chips:
        pairs = [(i, i ^ (reach * CORES)) for i in range(devices)]
        meta = jnp.concatenate([meta, permute(meta, pairs)])
        reach *= 2

    one = jnp.ones((), jnp.bool_)
    cols_ok = [one, grid_col > 0, grid_col < TILE_COLS - 1]
    if len(vertical) == 2:
        rows_ok = [one, grid_row > 0, grid_row < grid_rows - 1]
    else:
        rows_ok = [one] * (1 + len(vertical))
    flags = jnp.stack([r & c for r in rows_ok for c in cols_ok]).astype(jnp.int32)
    attended = []
    for c, (start, part) in enumerate(zip(starts, parts)):
        around = list(beside)
        for center, sideways in zip(above[c], beyond[c]):
            around += [center] + sideways
        last = c == len(parts) - 1
        got = attend_chunk(
            start,
            part,
            flags,
            queries,
            key_rows,
            values,
            around,
            attended,
            modulation if last else None,
        )
        attended = attended + [got[0]]
    normed = got[1]

    order = ring_order(chips, grid_rows)
    place = {chip: i for i, chip in enumerate(order)}
    forward = [
        (order[i] * CORES + k, order[(i + 1) % chips] * CORES + k)
        for i in range(chips)
        for k in range(CORES)
    ]
    backward = [(b, a) for a, b in forward]
    half = rows // 2
    far = chips // 2
    upper, lower = slice(0, half), slice(half, rows)
    ahead, behind = [normed], [normed]
    for _ in range(1, far):
        behind.append(permute(behind[-1], forward))
        ahead.append(permute(ahead[-1], backward))
    far_upper = permute(behind[-1][upper], forward)
    far_lower = permute(ahead[-1][lower], backward)

    my_chip = position // CORES
    mine = (position // SPLIT).astype(jnp.int32).reshape(1)
    places = jnp.array([place[c] for c in range(chips)], jnp.int32)
    orders = jnp.array(order, jnp.int32)
    my_place = places[my_chip]

    index = orders[(my_place + jnp.arange(chips, dtype=jnp.int32)) % chips] ^ my_chip

    def share(shifts, blocks):
        ring = [shift % chips for shift in shifts]
        got = run_experts(ring, blocks, weights, mine, index, meta)
        return dict(zip(shifts, got))

    partial = share([0, 1, -1], [[normed], [ahead[1]], [behind[1]]])
    for s in range(2, far):
        partial.update(share([s, -s], [[ahead[s]], [behind[s]]]))
    partial.update(share([far], [[far_upper, far_lower]]))

    wide = lambda a: a.astype(jnp.float32)
    add = lambda a, b: (wide(a) + wide(b)).astype(jnp.bfloat16)
    up = permute(partial[far][upper], forward)
    down = permute(partial[far][lower], backward)
    for s in range(far - 1, 0, -1):
        up_sum, down_sum = partial[s], partial[-s]
        if s == far - 1:
            up_sum = jnp.concatenate([add(up_sum[upper], up), up_sum[lower]], axis=0)
            down_sum = jnp.concatenate([down_sum[upper], add(down_sum[lower], down)], axis=0)
        else:
            up_sum, down_sum = add(up_sum, up), add(down_sum, down)
        up = permute(up_sum, forward)
        down = permute(down_sum, backward)
    mixture = wide(up) + wide(down) + wide(partial[0])
    attended = wide(jnp.concatenate(attended, axis=1))
    return (attended + modulation[2] * mixture).astype(jnp.bfloat16)


def solution(mesh):
    placed = (
        P(("groups", "tile"), None),
        P(("groups", "tile"), None),
        P(("groups", "tile"), None),
        P("groups", None),
        P(None, "tile"),
        P("tile", None),
        P(("groups", "tile"), None),
        P(("groups", "tile"), None),
    )
    return jax.shard_map(
        block, mesh=mesh, in_specs=placed, out_specs=P(("groups", "tile"), None), check_vma=False
    )
```

profile of v0, /device:TPU:0, one launch (start us, length us, event | category | flops | bytes accessed | tf_op | source)
XLA Modules:
  0.0 253.9 jit_solution(9785719448950348898)
XLA Ops:
  0.0 1.4 slice_bitcast_fusion
  1.4 4.1 %collective-permute-start.5 = (bf16[2,64,1536]{2,1,0:T(8,128)(2,1)S(1)}, bf16[2,64,1536]{2,1,0:T(8,128)(2,1)S(1)}, u32[]{:S(2)}, u32[]{:S(2)}) collective-permute-start(bf16[2,64,1536]{2,1,0:T(8,128)(2,1)S(1)} %pad_maximum_fusion.4), channel_id=1, source_target_pairs={{12,4},{13,5},{14,6},{15,7},{0,8},{1,9},{2,10},{3,11},{4,12},{5,13... | collective-permute-start | bytes 1179656 | tf_op jit(solution)/shard_map/ppermute | solution.py:25
  7.3 2.9 %collective-permute-start.8 = (bf16[2,64,1024]{2,1,0:T(8,128)(2,1)S(1)}, bf16[2,64,1024]{2,1,0:T(8,128)(2,1)}, u32[]{:S(2)}, u32[]{:S(2)}) collective-permute-start(bf16[2,64,1024]{2,1,0:T(8,128)(2,1)S(1)} %pad_maximum_fusion.5), channel_id=1, source_target_pairs={{12,4},{13,5},{14,6},{15,7},{0,8},{1,9},{2,10},{3,11},{4,12},{5,13... | collective-permute-start | bytes 786440 | tf_op jit(solution)/shard_map/ppermute | solution.py:25
  10.2 27.8 %collective-permute-done.5.refs_2_ = bf16[2,64,1536]{2,1,0:T(8,128)(2,1)S(1)} collective-permute-done((bf16[2,64,1536]{2,1,0:T(8,128)(2,1)S(1)}, bf16[2,64,1536]{2,1,0:T(8,128)(2,1)S(1)}, u32[]{:S(2)}, u32[]{:S(2)}) %collective-permute-start.5) | collective-permute-done | bytes 393248 | tf_op jit(solution)/shard_map/ppermute | solution.py:25
  38.0 1.9 collective-permute-start.6
  40.0 11.3 %collective-permute-done.8.refs_2_ = bf16[2,64,1024]{2,1,0:T(8,128)(2,1)} collective-permute-done((bf16[2,64,1024]{2,1,0:T(8,128)(2,1)S(1)}, bf16[2,64,1024]{2,1,0:T(8,128)(2,1)}, u32[]{:S(2)}, u32[]{:S(2)}) %collective-permute-start.8) | collective-permute-done | bytes 262176 | tf_op jit(solution)/shard_map/ppermute | solution.py:25
  51.3 1.9 collective-permute-start
  53.2 4.5 %collective-permute-start.1 = (bf16[2,64,4096]{2,1,0:T(8,128)(2,1)S(1)}, bf16[2,64,4096]{2,1,0:T(8,128)(2,1)S(1)}, u32[]{:S(2)}, u32[]{:S(2)}) collective-permute-start(bf16[2,64,4096]{2,1,0:T(8,128)(2,1)S(1)} %pad_maximum_fusion), channel_id=1, source_target_pairs={{13,12},{14,13},{15,14},{8,15},{1,0},{2,1},{3,2},{5,4},{6,5},{7,6}... | collective-permute-start | bytes 3145736 | tf_op jit(solution)/shard_map/ppermute | solution.py:25
  58.5 1.9 collective-permute-start.7
  60.4 13.9 %collective-permute-done.7.refs_4_ = bf16[2,64,1536]{2,1,0:T(8,128)(2,1)S(1)} collective-permute-done((bf16[2,64,1536]{2,1,0:T(8,128)(2,1)S(1)}, bf16[2,64,1536]{2,1,0:T(8,128)(2,1)S(1)}, u32[]{:S(2)}, u32[]{:S(2)}) %collective-permute-start.7) | collective-permute-done | bytes 393248 | tf_op jit(solution)/shard_map/ppermute | solution.py:25
  75.1 15.4 %collective-permute-start.3 = (bf16[2,64,1536]{2,1,0:T(8,128)(2,1)}, bf16[2,64,1536]{2,1,0:T(8,128)(2,1)S(1)}, u32[]{:S(2)}, u32[]{:S(2)}) collective-permute-start(bf16[2,64,1536]{2,1,0:T(8,128)(2,1)} %collective-permute-done.2.refs_2_), channel_id=1, source_target_pairs={{12,13},{13,14},{14,15},{7,0},{0,1},{1,2},{2,3},{4,5},{5,6},{6,7},... | collective-permute-start | bytes 1179656 | tf_op jit(solution)/shard_map/ppermute | solution.py:25
  90.4 1.5 collective-permute-done.3.refs_3_
  92.7 1.9 collective-permute-start.4
  94.6 1.9 collective-permute-start.10
  96.6 5.4 %collective-permute-start.9 = (bf16[2,64,1024]{2,1,0:T(8,128)(2,1)}, bf16[2,64,1024]{2,1,0:T(8,128)(2,1)}, u32[]{:S(2)}, u32[]{:S(2)}) collective-permute-start(bf16[2,64,1024]{2,1,0:T(8,128)(2,1)} %collective-permute-done.8.refs_2_), channel_id=1, source_target_pairs={{12,13},{13,14},{14,15},{7,0},{0,1},{1,2},{2,3},{4,5},{5,6},{6,7},... | collective-permute-start | bytes 786440 | tf_op jit(solution)/shard_map/ppermute | solution.py:25
  102.1 1.0 copy-done.5
  103.2 1.0 copy-done.9
  104.2 1.0 copy-done.11
  106.2 2.1 attend.3.refs_7_
  108.4 3.3 %attend.2.refs_6_ = bf16[64,1536]{1,0:T(8,128)(2,1)S(1)} custom-call(s32[6]{0:T(128)S(1)} %convert_element_type.72.flags_ref, bf16[64,4096]{1,0:T(8,128)(2,1)S(1)} %copy-done.5, bf16[64,4096]{1,0:T(8,128)(2,1)S(1)} %copy-done.3, bf16[64,4096]{1,0:T(8,128)(2,1)S(1)} %copy-done.4, bf16[2,64,4096]{2,1,0:T(8,128)(2,1)S(1)} %collective-permute-done.refs_0_, ...), custom_call_target="tpu_custom_call" | custom-call | flops 150994944 | bytes 2752512 | tf_op jit(solution)/shard_map/attend/pallas_call | solution.py:128
  111.7 3.1 %attend_last.1 = (bf16[64,1024]{1,0:T(8,128)(2,1)S(1)}, bf16[64,4096]{1,0:T(8,128)(2,1)S(1)}) custom-call(s32[6]{0:T(128)S(1)} %convert_element_type.72.flags_ref, bf16[64,4096]{1,0:T(8,128)(2,1)S(1)} %copy-done.5, bf16[64,4096]{1,0:T(8,128)(2,1)S(1)} %copy-done.3, bf16[64,4096]{1,0:T(8,128)(2,1)S(1)} %copy-done.4, ...), custom_call_target="tpu_custom_call" | custom-call | flops 100663296 | bytes 1835008 | tf_op jit(solution)/shard_map/attend_last/pallas_call | solution.py:128
  115.5 3.5 %collective-permute-start.14 = (bf16[64,4096]{1,0:T(8,128)(2,1)S(1)}, bf16[64,4096]{1,0:T(8,128)(2,1)S(1)}, u32[]{:S(2)}, u32[]{:S(2)}) collective-permute-start(bf16[64,4096]{1,0:T(8,128)(2,1)S(1)} %get-tuple-element.15.refs_0_), channel_id=1, source_target_pairs={{4,0},{5,1},{8,4},{9,5},{12,8},{13,9},{14,12},{15,13},{10,14},{11,... | collective-permute-start | bytes 1572872 | tf_op jit(solution)/shard_map/ppermute | solution.py:25
  119.8 9.9 %collective-permute-done.14.refs_1_ = bf16[64,4096]{1,0:T(8,128)(2,1)S(1)} collective-permute-done((bf16[64,4096]{1,0:T(8,128)(2,1)S(1)}, bf16[64,4096]{1,0:T(8,128)(2,1)S(1)}, u32[]{:S(2)}, u32[]{:S(2)}) %collective-permute-start.14) | collective-permute-done | bytes 524320 | tf_op jit(solution)/shard_map/ppermute | solution.py:25
  129.8 2.5 collective-permute-start.18
  132.3 1.2 collective-permute-start.19
  133.4 10.8 %collective-permute-done.18.refs_0_ = bf16[64,4096]{1,0:T(8,128)(2,1)S(1)} collective-permute-done((bf16[64,4096]{1,0:T(8,128)(2,1)S(1)}, bf16[64,4096]{1,0:T(8,128)(2,1)S(1)}, u32[]{:S(2)}, u32[]{:S(2)}) %collective-permute-start.18) | collective-permute-done | bytes 524320 | tf_op jit(solution)/shard_map/ppermute | solution.py:25
  144.6 2.4 collective-permute-start.21
  148.9 9.7 %collective-permute-done.11 = s32[1,64,4]{2,1,0:T(8,128)} collective-permute-done((s32[1,64,4]{2,1,0:T(8,128)}, s32[1,64,4]{2,1,0:T(8,128)}, u32[]{:S(2)}, u32[]{:S(2)}) %collective-permute-start.11) | collective-permute-done | bytes 1056 | tf_op jit(solution)/shard_map/ppermute | solution.py:25
  158.7 1.4 pad_add_fusion.2
  160.7 3.9 %collective-permute-done.12 = s32[2,64,4]{2,1,0:T(8,128)} collective-permute-done((s32[2,64,4]{2,1,0:T(8,128)}, s32[2,64,4]{2,1,0:T(8,128)}, u32[]{:S(2)}, u32[]{:S(2)}) %collective-permute-start.12) | collective-permute-done | bytes 2080 | tf_op jit(solution)/shard_map/ppermute | solution.py:25
  164.7 1.5 pad_add_fusion.1
  166.9 1.9 collective-permute-start.22
  170.0 4.9 %collective-permute-done.13 = s32[4,64,4]{2,1,0:T(8,128)} collective-permute-done((s32[4,64,4]{2,1,0:T(8,128)}, s32[4,64,4]{2,1,0:T(8,128)}, u32[]{:S(2)}, u32[]{:S(2)}) %collective-permute-start.13) | collective-permute-done | bytes 4128 | tf_op jit(solution)/shard_map/ppermute | solution.py:25
  175.8 1.1 collective-permute-done.23.refs_1_
  177.0 2.2 copy-done
  179.1 2.2 copy-done.2
  181.3 7.8 %experts.7 = bf16[64,4096]{1,0:T(8,128)(2,1)S(1)} custom-call(s32[1]{0:T(128)} %bitcast.11.mine_ref, s32[8]{0:T(128)S(1)} %broadcast_xor_fusion.index_ref, s32[8,64,4]{2,1,0:T(8,128)S(1)} %pad_add_fusion.meta_ref, bf16[32,4096]{1,0:T(8,128)(2,1)} %collective-permute-done.22.refs_0_, bf16[32,4096]{1,0:T(8,128)(2,1)} %collective-permute-done.23.refs_1_, ...), custom_call_target="tpu_custom_call" | custom-call | flops 1073741824 | bytes 16777216 | tf_op jit(solution)/shard_map/experts/pallas_call | solution.py:196
  189.2 2.3 collective-permute-start.24
  191.5 7.5 %experts.6 = (bf16[64,4096]{1,0:T(8,128)(2,1)S(1)}, bf16[64,4096]{1,0:T(8,128)(2,1)S(1)}) custom-call(s32[1]{0:T(128)} %bitcast.11.mine_ref, s32[8]{0:T(128)S(1)} %broadcast_xor_fusion.index_ref, s32[8,64,4]{2,1,0:T(8,128)S(1)} %pad_add_fusion.meta_ref, bf16[64,4096]{1,0:T(8,128)(2,1)S(1)} %collective-permute-done.20.refs_0_, ...), custom_call_target="tpu_custom_call" | custom-call | flops 2147483648 | bytes 16777216 | tf_op jit(solution)/shard_map/experts/pallas_call | solution.py:196
  199.4 7.9 %experts.5 = (bf16[64,4096]{1,0:T(8,128)(2,1)S(1)}, bf16[64,4096]{1,0:T(8,128)(2,1)S(1)}) custom-call(s32[1]{0:T(128)} %bitcast.11.mine_ref, s32[8]{0:T(128)S(1)} %broadcast_xor_fusion.index_ref, s32[8,64,4]{2,1,0:T(8,128)S(1)} %pad_add_fusion.meta_ref, bf16[64,4096]{1,0:T(8,128)(2,1)S(1)} %collective-permute-done.18.refs_0_, ...), custom_call_target="tpu_custom_call" | custom-call | flops 2147483648 | bytes 16777216 | tf_op jit(solution)/shard_map/experts/pallas_call | solution.py:196
  207.3 9.5 %experts.4 = (bf16[64,4096]{1,0:T(8,128)(2,1)S(1)}, bf16[64,4096]{1,0:T(8,128)(2,1)S(1)}, bf16[64,4096]{1,0:T(8,128)(2,1)S(1)}) custom-call(s32[1]{0:T(128)} %bitcast.11.mine_ref, s32[8]{0:T(128)S(1)} %broadcast_xor_fusion.index_ref, s32[8,64,4]{2,1,0:T(8,128)S(1)} %pad_add_fusion.meta_ref, bf16[64,4096]{1,0:T(8,128)(2,1)S(1)} %copy-done.7, ...), custom_call_target="tpu_custom_call" | custom-call | flops 3221225472 | bytes 16777216 | tf_op jit(solution)/shard_map/experts/pallas_call | solution.py:196
  216.9 2.1 collective-permute-start.25
  219.1 9.6 %collective-permute-done.25 = bf16[64,4096]{1,0:T(8,128)(2,1)S(1)} collective-permute-done((bf16[64,4096]{1,0:T(8,128)(2,1)S(1)}, bf16[64,4096]{1,0:T(8,128)(2,1)S(1)}, u32[]{:S(2)}, u32[]{:S(2)}) %collective-permute-start.25) | collective-permute-done | bytes 524320 | tf_op jit(solution)/shard_map/ppermute | solution.py:25
  228.9 2.2 collective-permute-start.26
  231.2 9.6 %collective-permute-done.26 = bf16[64,4096]{1,0:T(8,128)(2,1)S(1)} collective-permute-done((bf16[64,4096]{1,0:T(8,128)(2,1)S(1)}, bf16[64,4096]{1,0:T(8,128)(2,1)S(1)}, u32[]{:S(2)}, u32[]{:S(2)}) %collective-permute-start.26) | collective-permute-done | bytes 524320 | tf_op jit(solution)/shard_map/ppermute | solution.py:25
  241.0 1.8 collective-permute-start.27
  244.1 7.8 %collective-permute-done.27 = bf16[64,4096]{1,0:T(8,128)(2,1)S(1)} collective-permute-done((bf16[64,4096]{1,0:T(8,128)(2,1)S(1)}, bf16[64,4096]{1,0:T(8,128)(2,1)S(1)}, u32[]{:S(2)}, u32[]{:S(2)}) %collective-permute-start.27) | collective-permute-done | bytes 524320 | tf_op jit(solution)/shard_map/ppermute | solution.py:25
  252.8 1.1 add_convert_fusion
  (102 shorter events, 15.8 us)
Async XLA Ops:
  0.0 39.9 %copy-start.3 = (bf16[64,4096]{1,0:T(8,128)(2,1)S(1)}, bf16[64,4096]{1,0:T(8,128)(2,1)}, u32[]{:S(2)}) copy-start(bf16[64,4096]{1,0:T(8,128)(2,1)} %k_ref.5) | copy-start | bytes 1572868
  0.0 39.9 %copy-start.4 = (bf16[64,4096]{1,0:T(8,128)(2,1)S(1)}, bf16[64,4096]{1,0:T(8,128)(2,1)}, u32[]{:S(2)}) copy-start(bf16[64,4096]{1,0:T(8,128)(2,1)} %v_ref.5) | copy-start | bytes 1572868
  1.4 36.6 %collective-permute-start.5 = (bf16[2,64,1536]{2,1,0:T(8,128)(2,1)S(1)}, bf16[2,64,1536]{2,1,0:T(8,128)(2,1)S(1)}, u32[]{:S(2)}, u32[]{:S(2)}) collective-permute-start(bf16[2,64,1536]{2,1,0:T(8,128)(2,1)S(1)} %pad_maximum_fusion.4), channel_id=1, source_target_pairs={{12,4},{13,5},{14,6},{15,7},{0,8},{1,9},{2,10},{3,11},{4,12},{5,13... | collective-permute-start | bytes 1179656 | tf_op jit(solution)/shard_map/ppermute | solution.py:25
  5.5 171.4 %collective-permute-start.16 = (bf16[4096,512]{1,0:T(8,128)(2,1)}, bf16[4096,512]{1,0:T(8,128)(2,1)}, u32[]{:S(2)}, u32[]{:S(2)}) collective-permute-start(bf16[4096,512]{1,0:T(8,128)(2,1)} %refs_2_.5), channel_id=1, source_target_pairs={{0,1},{1,0},{2,3},{3,2},{4,5},{5,4},{6,7},{7,6},{8,9},{9,8},{10,11... | collective-permute-start | bytes 12582920 | tf_op jit(solution)/shard_map/ppermute | solution.py:25
  5.5 171.4 %collective-permute-start.17 = (bf16[512,4096]{1,0:T(8,128)(2,1)}, bf16[512,4096]{1,0:T(8,128)(2,1)}, u32[]{:S(2)}, u32[]{:S(2)}) collective-permute-start(bf16[512,4096]{1,0:T(8,128)(2,1)} %refs_4_.5), channel_id=1, source_target_pairs={{0,1},{1,0},{2,3},{3,2},{4,5},{5,4},{6,7},{7,6},{8,9},{9,8},{10,11... | collective-permute-start | bytes 12582920 | tf_op jit(solution)/shard_map/ppermute | solution.py:25
  6.1 47.1 %collective-permute-start.2 = (bf16[2,64,1536]{2,1,0:T(8,128)(2,1)S(1)}, bf16[2,64,1536]{2,1,0:T(8,128)(2,1)}, u32[]{:S(2)}, u32[]{:S(2)}) collective-permute-start(bf16[2,64,1536]{2,1,0:T(8,128)(2,1)S(1)} %pad_maximum_fusion.3), channel_id=1, source_target_pairs={{12,4},{13,5},{14,6},{15,7},{0,8},{1,9},{2,10},{3,11},{4,12},{5,13... | collective-permute-start | bytes 1179656 | tf_op jit(solution)/shard_map/ppermute | solution.py:25
  7.3 44.0 %collective-permute-start.8 = (bf16[2,64,1024]{2,1,0:T(8,128)(2,1)S(1)}, bf16[2,64,1024]{2,1,0:T(8,128)(2,1)}, u32[]{:S(2)}, u32[]{:S(2)}) collective-permute-start(bf16[2,64,1024]{2,1,0:T(8,128)(2,1)S(1)} %pad_maximum_fusion.5), channel_id=1, source_target_pairs={{12,4},{13,5},{14,6},{15,7},{0,8},{1,9},{2,10},{3,11},{4,12},{5,13... | collective-permute-start | bytes 786440 | tf_op jit(solution)/shard_map/ppermute | solution.py:25
  38.0 58.6 %copy-start.8 = (bf16[2,64,1536]{2,1,0:T(8,128)(2,1)}, bf16[2,64,1536]{2,1,0:T(8,128)(2,1)S(1)}, u32[]{:S(2)}) copy-start(bf16[2,64,1536]{2,1,0:T(8,128)(2,1)S(1)} %collective-permute-done.5.refs_2_) | copy-start | bytes 1179652
  38.0 19.8 %collective-permute-start.6 = (bf16[2,64,1536]{2,1,0:T(8,128)(2,1)S(1)}, bf16[2,64,1536]{2,1,0:T(8,128)(2,1)S(1)}, u32[]{:S(2)}, u32[]{:S(2)}) collective-permute-start(bf16[2,64,1536]{2,1,0:T(8,128)(2,1)S(1)} %collective-permute-done.5.refs_2_), channel_id=1, source_target_pairs={{12,13},{13,14},{14,15},{7,0},{0,1},{1,2},{2,3},{4,5},{5,6},{6,7},... | collective-permute-start | bytes 1179656 | tf_op jit(solution)/shard_map/ppermute | solution.py:25
  51.3 43.4 %collective-permute-start = (bf16[2,64,4096]{2,1,0:T(8,128)(2,1)S(1)}, bf16[2,64,4096]{2,1,0:T(8,128)(2,1)S(1)}, u32[]{:S(2)}, u32[]{:S(2)}) collective-permute-start(bf16[2,64,4096]{2,1,0:T(8,128)(2,1)S(1)} %pad_maximum_fusion), channel_id=1, source_target_pairs={{12,13},{13,14},{14,15},{7,0},{0,1},{1,2},{2,3},{4,5},{5,6},{6,7},... | collective-permute-start | bytes 3145736 | tf_op jit(solution)/shard_map/ppermute | solution.py:25
  53.2 43.4 %collective-permute-start.1 = (bf16[2,64,4096]{2,1,0:T(8,128)(2,1)S(1)}, bf16[2,64,4096]{2,1,0:T(8,128)(2,1)S(1)}, u32[]{:S(2)}, u32[]{:S(2)}) collective-permute-start(bf16[2,64,4096]{2,1,0:T(8,128)(2,1)S(1)} %pad_maximum_fusion), channel_id=1, source_target_pairs={{13,12},{14,13},{15,14},{8,15},{1,0},{2,1},{3,2},{5,4},{6,5},{7,6}... | collective-permute-start | bytes 3145736 | tf_op jit(solution)/shard_map/ppermute | solution.py:25
  58.5 15.8 %collective-permute-start.7 = (bf16[2,64,1536]{2,1,0:T(8,128)(2,1)S(1)}, bf16[2,64,1536]{2,1,0:T(8,128)(2,1)S(1)}, u32[]{:S(2)}, u32[]{:S(2)}) collective-permute-start(bf16[2,64,1536]{2,1,0:T(8,128)(2,1)S(1)} %collective-permute-done.5.refs_2_), channel_id=1, source_target_pairs={{13,12},{14,13},{15,14},{8,15},{1,0},{2,1},{3,2},{5,4},{6,5},{7,6}... | collective-permute-start | bytes 1179656 | tf_op jit(solution)/shard_map/ppermute | solution.py:25
  75.1 16.9 %collective-permute-start.3 = (bf16[2,64,1536]{2,1,0:T(8,128)(2,1)}, bf16[2,64,1536]{2,1,0:T(8,128)(2,1)S(1)}, u32[]{:S(2)}, u32[]{:S(2)}) collective-permute-start(bf16[2,64,1536]{2,1,0:T(8,128)(2,1)} %collective-permute-done.2.refs_2_), channel_id=1, source_target_pairs={{12,13},{13,14},{14,15},{7,0},{0,1},{1,2},{2,3},{4,5},{5,6},{6,7},... | collective-permute-start | bytes 1179656 | tf_op jit(solution)/shard_map/ppermute | solution.py:25
  92.7 15.6 %collective-permute-start.4 = (bf16[2,64,1536]{2,1,0:T(8,128)(2,1)}, bf16[2,64,1536]{2,1,0:T(8,128)(2,1)}, u32[]{:S(2)}, u32[]{:S(2)}) collective-permute-start(bf16[2,64,1536]{2,1,0:T(8,128)(2,1)} %collective-permute-done.2.refs_2_), channel_id=1, source_target_pairs={{13,12},{14,13},{15,14},{8,15},{1,0},{2,1},{3,2},{5,4},{6,5},{7,6}... | collective-permute-start | bytes 1179656 | tf_op jit(solution)/shard_map/ppermute | solution.py:25
  94.6 17.0 %collective-permute-start.10 = (bf16[2,64,1024]{2,1,0:T(8,128)(2,1)}, bf16[2,64,1024]{2,1,0:T(8,128)(2,1)}, u32[]{:S(2)}, u32[]{:S(2)}) collective-permute-start(bf16[2,64,1024]{2,1,0:T(8,128)(2,1)} %collective-permute-done.8.refs_2_), channel_id=1, source_target_pairs={{13,12},{14,13},{15,14},{8,15},{1,0},{2,1},{3,2},{5,4},{6,5},{7,6}... | collective-permute-start | bytes 786440 | tf_op jit(solution)/shard_map/ppermute | solution.py:25
  96.6 15.1 %collective-permute-start.9 = (bf16[2,64,1024]{2,1,0:T(8,128)(2,1)}, bf16[2,64,1024]{2,1,0:T(8,128)(2,1)}, u32[]{:S(2)}, u32[]{:S(2)}) collective-permute-start(bf16[2,64,1024]{2,1,0:T(8,128)(2,1)} %collective-permute-done.8.refs_2_), channel_id=1, source_target_pairs={{12,13},{13,14},{14,15},{7,0},{0,1},{1,2},{2,3},{4,5},{5,6},{6,7},... | collective-permute-start | bytes 786440 | tf_op jit(solution)/shard_map/ppermute | solution.py:25
  102.1 1.0 copy-start.5
  103.2 1.0 copy-start.9
  106.2 2.2 copy-start.15
  106.2 5.5 %copy-start.18 = (f32[3,4096]{1,0:T(4,128)S(1)}, f32[3,4096]{1,0:T(4,128)}, u32[]{:S(2)}) copy-start(f32[3,4096]{1,0:T(4,128)} %refs_5_.2) | copy-start | bytes 147460
  108.3 38.7 %copy-start.20 = (s32[64,2]{0,1:T(2,128)S(1)}, s32[64,2]{0,1:T(2,128)}, u32[]{:S(2)}) copy-start(s32[64,2]{0,1:T(2,128)} %param.17) | copy-start | bytes 1540
  108.3 38.7 %copy-start.21 = (s32[64,2]{0,1:T(2,128)S(1)}, s32[64,2]{0,1:T(2,128)}, u32[]{:S(2)}) copy-start(s32[64,2]{0,1:T(2,128)} %param.16) | copy-start | bytes 1540
  108.3 39.4 %copy-start.22 = (s32[8]{0:T(128)S(1)}, s32[8]{0:T(128)}, u32[]{:S(2)}) copy-start(s32[8]{0:T(128)} %constant.70.clone) | copy-start | bytes 100
  108.3 51.8 %copy-start.19 = (s32[8]{0:T(128)S(1)}, s32[8]{0:T(128)}, u32[]{:S(2)}) copy-start(s32[8]{0:T(128)} %constant.71.clone) | copy-start | bytes 100
  115.5 14.3 %collective-permute-start.14 = (bf16[64,4096]{1,0:T(8,128)(2,1)S(1)}, bf16[64,4096]{1,0:T(8,128)(2,1)S(1)}, u32[]{:S(2)}, u32[]{:S(2)}) collective-permute-start(bf16[64,4096]{1,0:T(8,128)(2,1)S(1)} %get-tuple-element.15.refs_0_), channel_id=1, source_target_pairs={{4,0},{5,1},{8,4},{9,5},{12,8},{13,9},{14,12},{15,13},{10,14},{11,... | collective-permute-start | bytes 1572872 | tf_op jit(solution)/shard_map/ppermute | solution.py:25
  119.0 13.2 %collective-permute-start.15 = (bf16[64,4096]{1,0:T(8,128)(2,1)S(1)}, bf16[64,4096]{1,0:T(8,128)(2,1)S(1)}, u32[]{:S(2)}, u32[]{:S(2)}) collective-permute-start(bf16[64,4096]{1,0:T(8,128)(2,1)S(1)} %get-tuple-element.15.refs_0_), channel_id=1, source_target_pairs={{0,4},{1,5},{4,8},{5,9},{8,12},{9,13},{12,14},{13,15},{14,10},{15,... | collective-permute-start | bytes 1572872 | tf_op jit(solution)/shard_map/ppermute | solution.py:25
  129.8 14.5 %collective-permute-start.18 = (bf16[64,4096]{1,0:T(8,128)(2,1)S(1)}, bf16[64,4096]{1,0:T(8,128)(2,1)S(1)}, u32[]{:S(2)}, u32[]{:S(2)}) collective-permute-start(bf16[64,4096]{1,0:T(8,128)(2,1)S(1)} %collective-permute-done.14.refs_1_), channel_id=1, source_target_pairs={{4,0},{5,1},{8,4},{9,5},{12,8},{13,9},{14,12},{15,13},{10,14},{11,... | collective-permute-start | bytes 1572872 | tf_op jit(solution)/shard_map/ppermute | solution.py:25
  132.3 12.4 %collective-permute-start.19 = (bf16[64,4096]{1,0:T(8,128)(2,1)S(1)}, bf16[64,4096]{1,0:T(8,128)(2,1)S(1)}, u32[]{:S(2)}, u32[]{:S(2)}) collective-permute-start(bf16[64,4096]{1,0:T(8,128)(2,1)S(1)} %collective-permute-done.15.refs_2_), channel_id=1, source_target_pairs={{0,4},{1,5},{4,8},{5,9},{8,12},{9,13},{12,14},{13,15},{14,10},{15,... | collective-permute-start | bytes 1572872 | tf_op jit(solution)/shard_map/ppermute | solution.py:25
  144.2 24.5 %collective-permute-start.20 = (bf16[64,4096]{1,0:T(8,128)(2,1)S(1)}, bf16[64,4096]{1,0:T(8,128)(2,1)S(1)}, u32[]{:S(2)}, u32[]{:S(2)}) collective-permute-start(bf16[64,4096]{1,0:T(8,128)(2,1)S(1)} %collective-permute-done.18.refs_0_), channel_id=1, source_target_pairs={{4,0},{5,1},{8,4},{9,5},{12,8},{13,9},{14,12},{15,13},{10,14},{11,... | collective-permute-start | bytes 1572872 | tf_op jit(solution)/shard_map/ppermute | solution.py:25
  144.6 21.6 %collective-permute-start.21 = (bf16[64,4096]{1,0:T(8,128)(2,1)S(1)}, bf16[64,4096]{1,0:T(8,128)(2,1)S(1)}, u32[]{:S(2)}, u32[]{:S(2)}) collective-permute-start(bf16[64,4096]{1,0:T(8,128)(2,1)S(1)} %collective-permute-done.19.refs_1_), channel_id=1, source_target_pairs={{0,4},{1,5},{4,8},{5,9},{8,12},{9,13},{12,14},{13,15},{14,10},{15,... | collective-permute-start | bytes 1572872 | tf_op jit(solution)/shard_map/ppermute | solution.py:25
  147.7 11.0 %collective-permute-start.11 = (s32[1,64,4]{2,1,0:T(8,128)}, s32[1,64,4]{2,1,0:T(8,128)}, u32[]{:S(2)}, u32[]{:S(2)}) collective-permute-start(s32[1,64,4]{2,1,0:T(8,128)} %bitcast.24), channel_id=1, source_target_pairs={{0,2},{1,3},{2,0},{3,1},{4,6},{5,7},{6,4},{7,5},{8,10},{9,11},{10,... | collective-permute-start | bytes 3080 | tf_op jit(solution)/shard_map/ppermute | solution.py:25
  160.1 4.6 %collective-permute-start.12 = (s32[2,64,4]{2,1,0:T(8,128)}, s32[2,64,4]{2,1,0:T(8,128)}, u32[]{:S(2)}, u32[]{:S(2)}) collective-permute-start(s32[2,64,4]{2,1,0:T(8,128)} %pad_add_fusion.2), channel_id=1, source_target_pairs={{0,4},{1,5},{2,6},{3,7},{4,0},{5,1},{6,2},{7,3},{8,12},{9,13},{10,... | collective-permute-start | bytes 6152 | tf_op jit(solution)/shard_map/ppermute | solution.py:25
  166.2 8.7 %collective-permute-start.13 = (s32[4,64,4]{2,1,0:T(8,128)}, s32[4,64,4]{2,1,0:T(8,128)}, u32[]{:S(2)}, u32[]{:S(2)}) collective-permute-start(s32[4,64,4]{2,1,0:T(8,128)} %pad_add_fusion.1), channel_id=1, source_target_pairs={{0,8},{1,9},{2,10},{3,11},{4,12},{5,13},{6,14},{7,15},{8,0},{9,1},... | collective-permute-start | bytes 12296 | tf_op jit(solution)/shard_map/ppermute | solution.py:25
  166.9 8.9 %collective-permute-start.22 = (bf16[32,4096]{1,0:T(8,128)(2,1)}, bf16[32,4096]{1,0:T(8,128)(2,1)}, u32[]{:S(2)}, u32[]{:S(2)}) collective-permute-start(bf16[32,4096]{1,0:T(8,128)(2,1)} %slice.62), channel_id=1, source_target_pairs={{0,4},{1,5},{4,8},{5,9},{8,12},{9,13},{12,14},{13,15},{14,10},{15,... | collective-permute-start | bytes 786440 | tf_op jit(solution)/shard_map/ppermute | solution.py:25
  169.5 7.4 %collective-permute-start.23 = (bf16[32,4096]{1,0:T(8,128)(2,1)}, bf16[32,4096]{1,0:T(8,128)(2,1)}, u32[]{:S(2)}, u32[]{:S(2)}) collective-permute-start(bf16[32,4096]{1,0:T(8,128)(2,1)} %slice.63), channel_id=1, source_target_pairs={{4,0},{5,1},{8,4},{9,5},{12,8},{13,9},{14,12},{15,13},{10,14},{11,... | collective-permute-start | bytes 786440 | tf_op jit(solution)/shard_map/ppermute | solution.py:25
  177.0 2.2 copy-start
  179.1 2.2 copy-start.2
  189.2 27.6 %collective-permute-start.24 = (bf16[32,4096]{1,0:T(8,128)(2,1)S(1)}, bf16[32,4096]{1,0:T(8,128)(2,1)S(1)}, u32[]{:S(2)}, u32[]{:S(2)}) collective-permute-start(bf16[32,4096]{1,0:T(8,128)(2,1)S(1)} %get-tuple-element.23), channel_id=1, source_target_pairs={{0,4},{1,5},{4,8},{5,9},{8,12},{9,13},{12,14},{13,15},{14,10},{15,... | collective-permute-start | bytes 786440 | tf_op jit(solution)/shard_map/ppermute | solution.py:25
  199.1 19.9 %collective-permute-start.28 = (bf16[32,4096]{1,0:T(8,128)(2,1)S(1)}, bf16[32,4096]{1,0:T(8,128)(2,1)S(1)}, u32[]{:S(2)}, u32[]{:S(2)}) collective-permute-start(bf16[32,4096]{1,0:T(8,128)(2,1)S(1)} %get-tuple-element.24), channel_id=1, source_target_pairs={{4,0},{5,1},{8,4},{9,5},{12,8},{13,9},{14,12},{15,13},{10,14},{11,... | collective-permute-start | bytes 786440 | tf_op jit(solution)/shard_map/ppermute | solution.py:25
  199.3 7.9 %copy-start.1 = (bf16[4096,512]{1,0:T(8,128)(2,1)S(1)}, bf16[4096,512]{1,0:T(8,128)(2,1)}, u32[]{:S(2)}) copy-start(bf16[4096,512]{1,0:T(8,128)(2,1)} %refs_2_.5) | copy-start | bytes 12582916
  199.3 7.9 %copy-start.7 = (bf16[64,4096]{1,0:T(8,128)(2,1)S(1)}, bf16[64,4096]{1,0:T(8,128)(2,1)}, u32[]{:S(2)}) copy-start(bf16[64,4096]{1,0:T(8,128)(2,1)} %copy-done.6) | copy-start | bytes 1572868
  216.9 36.0 %copy-start.17 = (bf16[64,1024]{1,0:T(8,128)(2,1)S(1)}, bf16[64,1024]{1,0:T(8,128)(2,1)}, u32[]{:S(2)}) copy-start(bf16[64,1024]{1,0:T(8,128)(2,1)} %copy-done.16) | copy-start | bytes 393220
  216.9 11.9 %collective-permute-start.25 = (bf16[64,4096]{1,0:T(8,128)(2,1)S(1)}, bf16[64,4096]{1,0:T(8,128)(2,1)S(1)}, u32[]{:S(2)}, u32[]{:S(2)}) collective-permute-start(bf16[64,4096]{1,0:T(8,128)(2,1)S(1)} %pad_maximum_fusion.1), channel_id=1, source_target_pairs={{0,4},{1,5},{4,8},{5,9},{8,12},{9,13},{12,14},{13,15},{14,10},{15,... | collective-permute-start | bytes 1572872 | tf_op jit(solution)/shard_map/ppermute | solution.py:25
  219.1 12.0 %collective-permute-start.29 = (bf16[64,4096]{1,0:T(8,128)(2,1)S(1)}, bf16[64,4096]{1,0:T(8,128)(2,1)S(1)}, u32[]{:S(2)}, u32[]{:S(2)}) collective-permute-start(bf16[64,4096]{1,0:T(8,128)(2,1)S(1)} %pad_maximum_fusion.2), channel_id=1, source_target_pairs={{4,0},{5,1},{8,4},{9,5},{12,8},{13,9},{14,12},{15,13},{10,14},{11,... | collective-permute-start | bytes 1572872 | tf_op jit(solution)/shard_map/ppermute | solution.py:25
  228.9 12.0 %collective-permute-start.26 = (bf16[64,4096]{1,0:T(8,128)(2,1)S(1)}, bf16[64,4096]{1,0:T(8,128)(2,1)S(1)}, u32[]{:S(2)}, u32[]{:S(2)}) collective-permute-start(bf16[64,4096]{1,0:T(8,128)(2,1)S(1)} %add_convert_fusion.4), channel_id=1, source_target_pairs={{0,4},{1,5},{4,8},{5,9},{8,12},{9,13},{12,14},{13,15},{14,10},{15,... | collective-permute-start | bytes 1572872 | tf_op jit(solution)/shard_map/ppermute | solution.py:25
  231.2 11.6 %collective-permute-start.30 = (bf16[64,4096]{1,0:T(8,128)(2,1)S(1)}, bf16[64,4096]{1,0:T(8,128)(2,1)S(1)}, u32[]{:S(2)}, u32[]{:S(2)}) collective-permute-start(bf16[64,4096]{1,0:T(8,128)(2,1)S(1)} %add_convert_fusion.2), channel_id=1, source_target_pairs={{4,0},{5,1},{8,4},{9,5},{12,8},{13,9},{14,12},{15,13},{10,14},{11,... | collective-permute-start | bytes 1572872 | tf_op jit(solution)/shard_map/ppermute | solution.py:25
  241.0 11.0 %collective-permute-start.27 = (bf16[64,4096]{1,0:T(8,128)(2,1)S(1)}, bf16[64,4096]{1,0:T(8,128)(2,1)S(1)}, u32[]{:S(2)}, u32[]{:S(2)}) collective-permute-start(bf16[64,4096]{1,0:T(8,128)(2,1)S(1)} %add_convert_fusion.3), channel_id=1, source_target_pairs={{0,4},{1,5},{4,8},{5,9},{8,12},{9,13},{12,14},{13,15},{14,10},{15,... | collective-permute-start | bytes 1572872 | tf_op jit(solution)/shard_map/ppermute | solution.py:25
  242.9 9.9 %collective-permute-start.31 = (bf16[64,4096]{1,0:T(8,128)(2,1)S(1)}, bf16[64,4096]{1,0:T(8,128)(2,1)S(1)}, u32[]{:S(2)}, u32[]{:S(2)}) collective-permute-start(bf16[64,4096]{1,0:T(8,128)(2,1)S(1)} %add_convert_fusion.1), channel_id=1, source_target_pairs={{4,0},{5,1},{8,4},{9,5},{12,8},{13,9},{14,12},{15,13},{10,14},{11,... | collective-permute-start | bytes 1572872 | tf_op jit(solution)/shard_map/ppermute | solution.py:25
  (7 other events, 5.7 us)
where the time goes:
time: 255 us; the launch traced here: 254 us
  waiting for transfers between devices  123 us (48%)
  starting transfers between devices  63.9 us (25%)
  Pallas kernels  41.2 us (16%)
  local copies, waits for them, and re-layouts  18.9 us (7%)
  other arithmetic  6.48 us (3%)
    ppermute x32, waiting for transfers between devices, permute(): return lax.ppermute(x, 'tile', pairs)  123 us
    ppermute x32, starting transfers between devices, permute(): return lax.ppermute(x, 'tile', pairs)  63.9 us
    pallas_call x4, Pallas kernels, run_experts(): pl.pallas_call(functools.partial(experts_kernel, shifts, pieces), out_sha...  32.7 us
    unnamed x46, local copies, waits for them, and re-layouts  12.2 us
    pallas_call x3, Pallas kernels, attend_chunk(): pl.pallas_call(functools.partial(attention_kernel, part // HEAD_DIM, sour...  8.56 us
  transfers between devices with their start and end apart: 32, of which 14 were waited for; matrix products, arithmetic and copies ran while one was open for 4% of the time, Pallas kernels for 13%

commit v1 on v0

--- a/solution.py
+++ b/solution.py
@@ -17,7 +17,8 @@
 MASKED = -1e30
 HEADS = (12, 12, 8)
 HEAD_GROUP = 4
-HIDDEN_STEP = 256
+HIDDEN_STEP = 512
+LANES = 128
 KERNEL_VMEM = 40 * 2**20
 
 
@@ -41,18 +42,18 @@
                     if 0 <= g - step < devices
                 ]
             )
-    sides = []
-    for step in (1, -1):
-        pairs = []
-        for g in range(devices):
-            column = g % TILE_COLS
-            if not 0 <= column - step < TILE_COLS:
-                continue
-            source = g - step
-            if grid_rows == 2 and {column, column - step} == {rotation - 1, rotation}:
-                source = (source + TILE_COLS) % devices
-            pairs.append((device(source), device(g)))
-        sides.append(pairs)
+    mate = [(i, i ^ 1) for i in range(devices)]
+    outer = []
+    for g in range(devices):
+        column = g % TILE_COLS
+        step = 1 if column % 2 else -1
+        if not 0 <= column + step < TILE_COLS:
+            continue
+        source = g + step
+        if grid_rows == 2 and {column, column + step} == {rotation - 1, rotation}:
+            source = (source + TILE_COLS) % devices
+        outer.append((device(source), device(g)))
+    sides = [mate, outer]
     return vertical, sides
 
 
@@ -60,8 +61,8 @@
     around = refs[: sources - 1]
     rest = refs[sources - 1 :]
     if last:
-        modulation_ref = rest[0]
-        before = rest[1:-2]
+        modulation_ref, meta_ref = rest[:2]
+        before = rest[2:-2]
         out_ref, normed_ref = rest[-2:]
     else:
         (out_ref,) = rest
@@ -108,12 +109,13 @@
                 (w - center) * factor * (1.0 + modulation_ref[1:2, cols])
                 + modulation_ref[0:1, cols]
             ).astype(jnp.bfloat16)
-
-
-def attend_chunk(start, part, flags, queries, key_rows, values, around, before, modulation):
+        normed_ref[:, count:] = meta_ref[...]
+
+
+def attend_chunk(start, part, flags, queries, key_rows, values, around, before, extra):
     rows, width = queries.shape
     sources = 1 + len(around)
-    last = modulation is not None
+    last = len(extra) > 0
     window = start // part
     flat = pl.BlockSpec((rows, part), lambda i, f: (0, window))
     deep = pl.BlockSpec((2, rows, part), lambda i, f: (0, 0, window))
@@ -122,9 +124,9 @@
     specs = [flat] * 3 + [deep if x.shape[2] == width else whole(x) for x in around]
     out_shape = [jax.ShapeDtypeStruct((rows, part), jnp.bfloat16)]
     if last:
-        operands += [modulation] + before
-        specs += [whole(x) for x in [modulation] + before]
-        out_shape.append(jax.ShapeDtypeStruct((rows, width), jnp.bfloat16))
+        operands += extra + before
+        specs += [whole(x) for x in extra + before]
+        out_shape.append(jax.ShapeDtypeStruct((rows, width + LANES), jnp.bfloat16))
     return pl.pallas_call(
         functools.partial(attention_kernel, part // HEAD_DIM, sources, last),
         out_shape=out_shape,
@@ -144,15 +146,26 @@
     )(flags, *operands)
 
 
-def experts_kernel(shifts, pieces, mine_ref, index_ref, meta_ref, *refs):
-    blocks = len(shifts)
-    inputs = refs[: sum(pieces)]
-    in_a, in_b, out_a, out_b = refs[sum(pieces) : sum(pieces) + 4]
-    outs = refs[sum(pieces) + 4 : sum(pieces) + 4 + blocks]
-    x_ref, total_ref, first_ref, second_ref, first_sem, second_sem = refs[
-        sum(pieces) + 4 + blocks :
-    ]
-    steps, _, step = first_ref.shape
+def route_lanes(routes, gate_fixed):
+    lanes = jnp.concatenate([routes, gate_fixed // 16, gate_fixed % 16], axis=1)
+    return jnp.pad(lanes, ((0, 0), (0, LANES - lanes.shape[1]))).astype(jnp.bfloat16)
+
+
+def gates_of(lanes, mine):
+    lanes = lanes.astype(jnp.float32)
+    gate = 0.0
+    for k in range(2):
+        fixed = lanes[:, 2 + k : 3 + k] * 16.0 + lanes[:, 4 + k : 5 + k]
+        gate = gate + jnp.where(lanes[:, k : k + 1] == mine, fixed, 0.0)
+    return gate / 1024.0
+
+
+def experts_kernel(blocks, pieces, mine_ref, *refs):
+    inputs = refs[:pieces]
+    in_a, in_b, out_a, out_b = refs[pieces : pieces + 4]
+    outs = refs[pieces + 4 : pieces + 4 + blocks]
+    x_ref, total_ref, first_ref, second_ref, first_sem, second_sem = refs[pieces + 4 + blocks :]
+    steps, width, step = first_ref.shape
     for j in range(steps):
         source_in, source_out = (in_a, out_a) if j < steps // 2 else (in_b, out_b)
         span = pl.ds(j % (steps // 2) * step, step)
@@ -168,38 +181,37 @@
     def body(j, carry):
         first, second = first_ref.at[j], second_ref.at[j]
         pltpu.make_async_copy(first, first, first_sem.at[j]).wait()
-        wide = jnp.dot(x_ref[...], first[...], preferred_element_type=jnp.float32)
+        wide = jnp.dot(x_ref[:, :width], first[...], preferred_element_type=jnp.float32)
         hidden = jax.nn.gelu(wide, approximate=True).astype(jnp.bfloat16)
         pltpu.make_async_copy(second, second, second_sem.at[j]).wait()
         total_ref[...] += jnp.dot(hidden, second[...], preferred_element_type=jnp.float32)
         return carry
 
     lax.fori_loop(0, steps, body, 0)
+    mine = mine_ref[0].astype(jnp.float32)
     for i, out in enumerate(outs):
-        block = meta_ref[index_ref[shifts[i]]]
-        chosen = jnp.where(block[:, :2] == mine_ref[0], block[:, 2:], 0)
-        gate = jnp.sum(chosen, axis=1, keepdims=True).astype(jnp.float32) / 1024.0
-        out[...] = (total_ref[i * rows : (i + 1) * rows, :] * gate).astype(jnp.bfloat16)
-
-
-def run_experts(shifts, blocks, weights, mine, index, meta):
-    pieces = [len(block) for block in blocks]
+        here = slice(i * rows, (i + 1) * rows)
+        gate = gates_of(x_ref[here, width:], mine)
+        out[...] = (total_ref[here, :] * gate).astype(jnp.bfloat16)
+
+
+def run_experts(blocks, weights, mine):
     rows = sum(x.shape[0] for x in blocks[0])
     flat = [x for block in blocks for x in block]
-    width = flat[0].shape[1]
+    width = weights[0].shape[0]
     count = len(blocks)
     hidden = sum(w.shape[1] for w in weights[:2])
     step = min(HIDDEN_STEP, weights[0].shape[1])
     steps = hidden // step
     resident = pl.BlockSpec(memory_space=pltpu.VMEM)
-    scalar = pl.BlockSpec(memory_space=pltpu.SMEM)
+    remote = pl.BlockSpec(memory_space=pl.ANY)
     return pl.pallas_call(
-        functools.partial(experts_kernel, shifts, pieces),
+        functools.partial(experts_kernel, count, len(flat)),
         out_shape=[jax.ShapeDtypeStruct((rows, width), jnp.bfloat16)] * count,
-        in_specs=[scalar, scalar] + [resident] * (1 + len(flat)) + [pl.BlockSpec(memory_space=pl.ANY)] * 4,
+        in_specs=[pl.BlockSpec(memory_space=pltpu.SMEM)] + [resident] * len(flat) + [remote] * 4,
         out_specs=[resident] * count,
         scratch_shapes=[
-            pltpu.VMEM((count * rows, width), jnp.bfloat16),
+            pltpu.VMEM((count * rows, flat[0].shape[1]), jnp.bfloat16),
             pltpu.VMEM((count * rows, width), jnp.float32),
             pltpu.VMEM((steps, width, step), jnp.bfloat16),
             pltpu.VMEM((steps, step, width), jnp.bfloat16),
@@ -213,7 +225,7 @@
             transcendentals=count * rows * hidden,
         ),
         name="experts",
-    )(mine, index, meta, *flat, *weights)
+    )(mine, *flat, *weights)
 
 
 def ring_order(chips, grid_rows):
@@ -241,18 +253,11 @@
     beside = [permute(own, pairs) for pairs in sides]
     beyond = [[[permute(x, pairs) for pairs in sides] for x in above[c]] for c in range(len(parts))]
 
-    swap = [(i, i ^ 1) for i in range(devices)]
-    weights = [expert_in, permute(expert_in, swap), expert_out, permute(expert_out, swap)]
-    chips = devices // CORES
-    meta = jnp.concatenate([routes, gate_fixed], axis=1)[None]
-    reach = 1
-    while reach < chips:
-        pairs = [(i, i ^ (reach * CORES)) for i in range(devices)]
-        meta = jnp.concatenate([meta, permute(meta, pairs)])
-        reach *= 2
+    weights = [expert_in, permute(expert_in, sides[0]), expert_out, permute(expert_out, sides[0])]
+    lanes = route_lanes(routes, gate_fixed)
 
     one = jnp.ones((), jnp.bool_)
-    cols_ok = [one, grid_col > 0, grid_col < TILE_COLS - 1]
+    cols_ok = [one, one, (grid_col > 0) & (grid_col < TILE_COLS - 1)]
     if len(vertical) == 2:
         rows_ok = [one, grid_row > 0, grid_row < grid_rows - 1]
     else:
@@ -273,13 +278,13 @@
             values,
             around,
             attended,
-            modulation if last else None,
+            [modulation, lanes] if last else [],
         )
         attended = attended + [got[0]]
     normed = got[1]
 
+    chips = devices // CORES
     order = ring_order(chips, grid_rows)
-    place = {chip: i for i, chip in enumerate(order)}
     forward = [
         (order[i] * CORES + k, order[(i + 1) % chips] * CORES + k)
         for i in range(chips)
@@ -296,21 +301,13 @@
     far_upper = permute(behind[-1][upper], forward)
     far_lower = permute(ahead[-1][lower], backward)
 
-    my_chip = position // CORES
     mine = (position // SPLIT).astype(jnp.int32).reshape(1)
-    places = jnp.array([place[c] for c in range(chips)], jnp.int32)
-    orders = jnp.array(order, jnp.int32)
-    my_place = places[my_chip]
-
-    index = orders[(my_place + jnp.arange(chips, dtype=jnp.int32)) % chips] ^ my_chip
 
     def share(shifts, blocks):
-        ring = [shift % chips for shift in shifts]
-        got = run_experts(ring, blocks, weights, mine, index, meta)
-        return dict(zip(shifts, got))
-
-    partial = share([0, 1, -1], [[normed], [ahead[1]], [behind[1]]])
-    for s in range(2, far):
+        return dict(zip(shifts, run_experts(blocks, weights, mine)))
+
+    partial = share([0], [[normed]])
+    for s in range(1, far):
         partial.update(share([s, -s], [[ahead[s]], [behind[s]]]))
     partial.update(share([far], [[far_upper, far_lower]]))
 

time: 255 us -> 236 us (0.925)
  starting transfers between devices: 63.9 us -> 56.6 us
  other arithmetic: 6.48 us -> 2.11 us
  Pallas kernels: 41.2 us -> 38.2 us
    ppermute x32 -> x29, starting transfers between devices: 63.9 us -> 56.6 us  [permute(): return lax.ppermute(x, 'tile', pairs)]
    concatenate x4 -> x1, other arithmetic: 3.86 us -> 0.01 us  [route_lanes(): lanes = jnp.concatenate([routes, gate_fixed // 16, gate_fixed % 16], axis=1)]
    pallas_call x4 -> x5, Pallas kernels: 32.7 us -> 29.7 us  [run_experts(): pl.pallas_call(functools.partial(experts_kernel, count, len(flat)), out_s...]
    ppermute x32 -> x29, waiting for transfers between devices: 123 us -> 121 us  [permute(): return lax.ppermute(x, 'tile', pairs)]
    unnamed x46 -> x48, local copies, waits for them, and re-layouts: 12.2 us -> 12.1 us
  transfers between devices with their start and end apart: 32 -> 29, of which waited for: 14 -> 14; matrix products, arithmetic and copies ran while one was open for 4% -> 2% of each run, Pallas kernels for 13% -> 14%
where the time goes in v1:
time: 236 us
  waiting for transfers between devices  121 us (51%)
  starting transfers between devices  56.6 us (24%)
  Pallas kernels  38.2 us (16%)
  local copies, waits for them, and re-layouts  17 us (7%)
    ppermute x29, waiting for transfers between devices, permute(): return lax.ppermute(x, 'tile', pairs)  121 us
    ppermute x29, starting transfers between devices, permute(): return lax.ppermute(x, 'tile', pairs)  56.6 us
    pallas_call x5, Pallas kernels, run_experts(): pl.pallas_call(functools.partial(experts_kernel, count, len(flat)), out_s...  29.7 us
    unnamed x48, local copies, waits for them, and re-layouts  12.1 us
    pallas_call x3, Pallas kernels, attend_chunk(): pl.pallas_call(functools.partial(attention_kernel, part // HEAD_DIM, sour...  8.55 us
  transfers between devices with their start and end apart: 29, of which 14 were waited for; matrix products, arithmetic and copies ran while one was open for 2% of the time, Pallas kernels for 14%

profile of v1, /device:TPU:0, one launch (start us, length us, event | category | flops | bytes accessed | tf_op | source)
XLA Modules:
  0.0 235.6 jit_solution(6114191176341468788)
XLA Ops:
  0.0 1.3 slice_bitcast_fusion
  1.4 4.1 %collective-permute-start.5 = (bf16[2,64,1536]{2,1,0:T(8,128)(2,1)S(1)}, bf16[2,64,1536]{2,1,0:T(8,128)(2,1)S(1)}, u32[]{:S(2)}, u32[]{:S(2)}) collective-permute-start(bf16[2,64,1536]{2,1,0:T(8,128)(2,1)S(1)} %pad_maximum_fusion.4), channel_id=1, source_target_pairs={{12,4},{13,5},{14,6},{15,7},{0,8},{1,9},{2,10},{3,11},{4,12},{5,13... | collective-permute-start | bytes 1179656 | tf_op jit(solution)/shard_map/ppermute | solution.py:26
  6.2 1.0 slice_bitcast_fusion.4
  7.3 2.9 %collective-permute-start.8 = (bf16[2,64,1024]{2,1,0:T(8,128)(2,1)S(1)}, bf16[2,64,1024]{2,1,0:T(8,128)(2,1)}, u32[]{:S(2)}, u32[]{:S(2)}) collective-permute-start(bf16[2,64,1024]{2,1,0:T(8,128)(2,1)S(1)} %pad_maximum_fusion.5), channel_id=1, source_target_pairs={{12,4},{13,5},{14,6},{15,7},{0,8},{1,9},{2,10},{3,11},{4,12},{5,13... | collective-permute-start | bytes 786440 | tf_op jit(solution)/shard_map/ppermute | solution.py:26
  10.2 27.8 %collective-permute-done.5.refs_2_ = bf16[2,64,1536]{2,1,0:T(8,128)(2,1)S(1)} collective-permute-done((bf16[2,64,1536]{2,1,0:T(8,128)(2,1)S(1)}, bf16[2,64,1536]{2,1,0:T(8,128)(2,1)S(1)}, u32[]{:S(2)}, u32[]{:S(2)}) %collective-permute-start.5) | collective-permute-done | bytes 393248 | tf_op jit(solution)/shard_map/ppermute | solution.py:26
  38.1 13.2 %collective-permute-done.8.refs_2_ = bf16[2,64,1024]{2,1,0:T(8,128)(2,1)} collective-permute-done((bf16[2,64,1024]{2,1,0:T(8,128)(2,1)S(1)}, bf16[2,64,1024]{2,1,0:T(8,128)(2,1)}, u32[]{:S(2)}, u32[]{:S(2)}) %collective-permute-start.8) | collective-permute-done | bytes 262176 | tf_op jit(solution)/shard_map/ppermute | solution.py:26
  51.3 3.6 %collective-permute-start.1 = (bf16[2,64,4096]{2,1,0:T(8,128)(2,1)S(1)}, bf16[2,64,4096]{2,1,0:T(8,128)(2,1)S(1)}, u32[]{:S(2)}, u32[]{:S(2)}) collective-permute-start(bf16[2,64,4096]{2,1,0:T(8,128)(2,1)S(1)} %pad_maximum_fusion), channel_id=1, source_target_pairs={{14,13},{13,14},{8,15},{7,0},{2,1},{1,2},{6,5},{5,6},{0,7},{15,8},... | collective-permute-start | bytes 3145736 | tf_op jit(solution)/shard_map/ppermute | solution.py:26
  55.6 2.9 %collective-permute-start.7 = (bf16[2,64,1536]{2,1,0:T(8,128)(2,1)S(1)}, bf16[2,64,1536]{2,1,0:T(8,128)(2,1)S(1)}, u32[]{:S(2)}, u32[]{:S(2)}) collective-permute-start(bf16[2,64,1536]{2,1,0:T(8,128)(2,1)S(1)} %collective-permute-done.5.refs_2_), channel_id=1, source_target_pairs={{14,13},{13,14},{8,15},{7,0},{2,1},{1,2},{6,5},{5,6},{0,7},{15,8},... | collective-permute-start | bytes 1179656 | tf_op jit(solution)/shard_map/ppermute | solution.py:26
  58.5 14.1 %collective-permute-done.7.refs_4_ = bf16[2,64,1536]{2,1,0:T(8,128)(2,1)S(1)} collective-permute-done((bf16[2,64,1536]{2,1,0:T(8,128)(2,1)S(1)}, bf16[2,64,1536]{2,1,0:T(8,128)(2,1)S(1)}, u32[]{:S(2)}, u32[]{:S(2)}) %collective-permute-start.7) | collective-permute-done | bytes 393248 | tf_op jit(solution)/shard_map/ppermute | solution.py:26
  73.4 15.0 %collective-permute-start.3 = (bf16[2,64,1536]{2,1,0:T(8,128)(2,1)}, bf16[2,64,1536]{2,1,0:T(8,128)(2,1)S(1)}, u32[]{:S(2)}, u32[]{:S(2)}) collective-permute-start(bf16[2,64,1536]{2,1,0:T(8,128)(2,1)} %collective-permute-done.2.refs_2_), channel_id=1, source_target_pairs={{0,1},{1,0},{2,3},{3,2},{4,5},{5,4},{6,7},{7,6},{8,9},{9,8},{10,11... | collective-permute-start | bytes 1179656 | tf_op jit(solution)/shard_map/ppermute | solution.py:26
  88.3 1.6 collective-permute-done.3.refs_3_
  90.6 3.1 %collective-permute-start.10 = (bf16[2,64,1024]{2,1,0:T(8,128)(2,1)}, bf16[2,64,1024]{2,1,0:T(8,128)(2,1)}, u32[]{:S(2)}, u32[]{:S(2)}) collective-permute-start(bf16[2,64,1024]{2,1,0:T(8,128)(2,1)} %collective-permute-done.8.refs_2_), channel_id=1, source_target_pairs={{14,13},{13,14},{8,15},{7,0},{2,1},{1,2},{6,5},{5,6},{0,7},{15,8},... | collective-permute-start | bytes 786440 | tf_op jit(solution)/shard_map/ppermute | solution.py:26
  93.9 3.4 %collective-permute-start.4 = (bf16[2,64,1536]{2,1,0:T(8,128)(2,1)}, bf16[2,64,1536]{2,1,0:T(8,128)(2,1)}, u32[]{:S(2)}, u32[]{:S(2)}) collective-permute-start(bf16[2,64,1536]{2,1,0:T(8,128)(2,1)} %collective-permute-done.2.refs_2_), channel_id=1, source_target_pairs={{14,13},{13,14},{8,15},{7,0},{2,1},{1,2},{6,5},{5,6},{0,7},{15,8},... | collective-permute-start | bytes 1179656 | tf_op jit(solution)/shard_map/ppermute | solution.py:26
  97.5 1.0 copy-done.6
  98.6 1.0 copy-done.12
  99.6 1.0 copy-done.14
  100.6 1.0 copy-done.16
  101.6 2.1 attend.3.refs_8_
  104.2 3.3 %attend.2.refs_7_ = bf16[64,1536]{1,0:T(8,128)(2,1)S(1)} custom-call(s32[6]{0:T(128)S(1)} %add_convert_fusion.7.flags_ref, bf16[64,4096]{1,0:T(8,128)(2,1)S(1)} %copy-done.6, bf16[64,4096]{1,0:T(8,128)(2,1)S(1)} %copy-done.4, bf16[64,4096]{1,0:T(8,128)(2,1)S(1)} %copy-done.5, bf16[2,64,4096]{2,1,0:T(8,128)(2,1)S(1)} %collective-permute-done.refs_0_, ...), custom_call_target="tpu_custom_call" | custom-call | flops 150994944 | bytes 2752512 | tf_op jit(solution)/shard_map/attend/pallas_call | solution.py:130
  107.5 3.1 %attend_last.1 = (bf16[64,1024]{1,0:T(8,128)(2,1)S(1)}, bf16[64,4224]{1,0:T(8,128)(2,1)S(1)}) custom-call(s32[6]{0:T(128)S(1)} %add_convert_fusion.7.flags_ref, bf16[64,4096]{1,0:T(8,128)(2,1)S(1)} %copy-done.6, bf16[64,4096]{1,0:T(8,128)(2,1)S(1)} %copy-done.4, bf16[64,4096]{1,0:T(8,128)(2,1)S(1)} %copy-done.5, ...), custom_call_target="tpu_custom_call" | custom-call | flops 100663296 | bytes 1835008 | tf_op jit(solution)/shard_map/attend_last/pallas_call | solution.py:130
  111.3 5.8 %collective-permute-start.11 = (bf16[64,4224]{1,0:T(8,128)(2,1)S(1)}, bf16[64,4224]{1,0:T(8,128)(2,1)S(1)}, u32[]{:S(2)}, u32[]{:S(2)}) collective-permute-start(bf16[64,4224]{1,0:T(8,128)(2,1)S(1)} %get-tuple-element.14.refs_0_), channel_id=1, source_target_pairs={{4,0},{5,1},{8,4},{9,5},{12,8},{13,9},{14,12},{15,13},{10,14},{11,... | collective-permute-start | bytes 1622024 | tf_op jit(solution)/shard_map/ppermute | solution.py:26
  117.9 11.0 %collective-permute-done.12.refs_1_ = bf16[64,4224]{1,0:T(8,128)(2,1)S(1)} collective-permute-done((bf16[64,4224]{1,0:T(8,128)(2,1)S(1)}, bf16[64,4224]{1,0:T(8,128)(2,1)S(1)}, u32[]{:S(2)}, u32[]{:S(2)}) %collective-permute-start.12) | collective-permute-done | bytes 540704 | tf_op jit(solution)/shard_map/ppermute | solution.py:26
  128.9 2.3 collective-permute-start.15
  131.2 12.7 %collective-permute-done.16.refs_1_ = bf16[64,4224]{1,0:T(8,128)(2,1)S(1)} collective-permute-done((bf16[64,4224]{1,0:T(8,128)(2,1)S(1)}, bf16[64,4224]{1,0:T(8,128)(2,1)S(1)}, u32[]{:S(2)}, u32[]{:S(2)}) %collective-permute-start.16) | collective-permute-done | bytes 540704 | tf_op jit(solution)/shard_map/ppermute | solution.py:26
  143.9 2.4 %collective-permute-start.17 = (bf16[64,4224]{1,0:T(8,128)(2,1)S(1)}, bf16[64,4224]{1,0:T(8,128)(2,1)S(1)}, u32[]{:S(2)}, u32[]{:S(2)}) collective-permute-start(bf16[64,4224]{1,0:T(8,128)(2,1)S(1)} %collective-permute-done.15.refs_0_), channel_id=1, source_target_pairs={{4,0},{5,1},{8,4},{9,5},{12,8},{13,9},{14,12},{15,13},{10,14},{11,... | collective-permute-start | bytes 1622024 | tf_op jit(solution)/shard_map/ppermute | solution.py:26
  146.3 11.9 %collective-permute-done.18.refs_1_ = bf16[64,4224]{1,0:T(8,128)(2,1)S(1)} collective-permute-done((bf16[64,4224]{1,0:T(8,128)(2,1)S(1)}, bf16[64,4224]{1,0:T(8,128)(2,1)S(1)}, u32[]{:S(2)}, u32[]{:S(2)}) %collective-permute-start.18) | collective-permute-done | bytes 540704 | tf_op jit(solution)/shard_map/ppermute | solution.py:26
  159.9 1.7 collective-permute-start.20
  161.7 5.1 %collective-permute-done.19.refs_0_ = bf16[32,4224]{1,0:T(8,128)(2,1)S(1)} collective-permute-done((bf16[32,4224]{1,0:T(8,128)(2,1)}, bf16[32,4224]{1,0:T(8,128)(2,1)S(1)}, u32[]{:S(2)}, u32[]{:S(2)}) %collective-permute-start.19) | collective-permute-done | bytes 270368 | tf_op jit(solution)/shard_map/ppermute | solution.py:26
  166.8 1.1 collective-permute-done.20.refs_1_
  167.9 2.2 copy-done
  170.1 2.2 copy-done.2
  172.3 6.2 %experts.8 = bf16[64,4096]{1,0:T(8,128)(2,1)S(1)} custom-call(s32[1]{0:T(128)} %bitcast.10.mine_ref, bf16[32,4224]{1,0:T(8,128)(2,1)S(1)} %collective-permute-done.19.refs_0_, bf16[32,4224]{1,0:T(8,128)(2,1)} %collective-permute-done.20.refs_1_, bf16[4096,512]{1,0:T(8,128)(2,1)S(1)} %copy-done, bf16[4096,512]{1,0:T(8,128)(2,1)} %collective-permute-done.13.refs_3_.refs_2_, ...), custom_call_target="tpu_custom_call" | custom-call | flops 1073741824 | bytes 16777216 | tf_op jit(solution)/shard_map/experts/pallas_call | solution.py:208
  179.2 1.4 collective-permute-start.25
  180.6 6.1 %experts.7 = (bf16[64,4096]{1,0:T(8,128)(2,1)S(1)}, bf16[64,4096]{1,0:T(8,128)(2,1)S(1)}) custom-call(s32[1]{0:T(128)} %bitcast.10.mine_ref, bf16[64,4224]{1,0:T(8,128)(2,1)S(1)} %collective-permute-done.17.refs_0_, bf16[64,4224]{1,0:T(8,128)(2,1)S(1)} %collective-permute-done.18.refs_1_, bf16[4096,512]{1,0:T(8,128)(2,1)S(1)} %copy-done, ...), custom_call_target="tpu_custom_call" | custom-call | flops 2147483648 | bytes 16777216 | tf_op jit(solution)/shard_map/experts/pallas_call | solution.py:208
  186.7 6.1 %experts.6 = (bf16[64,4096]{1,0:T(8,128)(2,1)S(1)}, bf16[64,4096]{1,0:T(8,128)(2,1)S(1)}) custom-call(s32[1]{0:T(128)} %bitcast.10.mine_ref, bf16[64,4224]{1,0:T(8,128)(2,1)S(1)} %copy-done.8, bf16[64,4224]{1,0:T(8,128)(2,1)S(1)} %collective-permute-done.16.refs_1_, bf16[4096,512]{1,0:T(8,128)(2,1)S(1)} %copy-done, ...), custom_call_target="tpu_custom_call" | custom-call | flops 2147483648 | bytes 16777216 | tf_op jit(solution)/shard_map/experts/pallas_call | solution.py:208
  192.8 6.1 %experts.5 = (bf16[64,4096]{1,0:T(8,128)(2,1)S(1)}, bf16[64,4096]{1,0:T(8,128)(2,1)S(1)}) custom-call(s32[1]{0:T(128)} %bitcast.10.mine_ref, bf16[64,4224]{1,0:T(8,128)(2,1)S(1)} %collective-permute-done.11.refs_0_, bf16[64,4224]{1,0:T(8,128)(2,1)S(1)} %collective-permute-done.12.refs_1_, bf16[4096,512]{1,0:T(8,128)(2,1)S(1)} %copy-done, ...), custom_call_target="tpu_custom_call" | custom-call | flops 2147483648 | bytes 16777216 | tf_op jit(solution)/shard_map/experts/pallas_call | solution.py:208
  199.9 1.4 collective-permute-start.26
  201.3 9.7 %collective-permute-done.22 = bf16[64,4096]{1,0:T(8,128)(2,1)S(1)} collective-permute-done((bf16[64,4096]{1,0:T(8,128)(2,1)S(1)}, bf16[64,4096]{1,0:T(8,128)(2,1)S(1)}, u32[]{:S(2)}, u32[]{:S(2)}) %collective-permute-start.22) | collective-permute-done | bytes 524320 | tf_op jit(solution)/shard_map/ppermute | solution.py:26
  211.2 0.9 collective-permute-start.23
  212.2 1.2 collective-permute-start.27
  213.4 9.7 %collective-permute-done.23 = bf16[64,4096]{1,0:T(8,128)(2,1)S(1)} collective-permute-done((bf16[64,4096]{1,0:T(8,128)(2,1)S(1)}, bf16[64,4096]{1,0:T(8,128)(2,1)S(1)}, u32[]{:S(2)}, u32[]{:S(2)}) %collective-permute-start.23) | collective-permute-done | bytes 524320 | tf_op jit(solution)/shard_map/ppermute | solution.py:26
  223.3 0.9 collective-permute-start.24
  224.3 1.2 collective-permute-start.28
  225.5 0.9 slice.51
  226.4 5.2 %experts.9 = bf16[64,4096]{1,0:T(8,128)(2,1)S(1)} custom-call(s32[1]{0:T(128)} %bitcast.10.mine_ref, bf16[64,4224]{1,0:T(8,128)(2,1)S(1)} %copy-done.10, bf16[4096,512]{1,0:T(8,128)(2,1)S(1)} %copy-done.1, bf16[4096,512]{1,0:T(8,128)(2,1)} %collective-permute-done.13.refs_3_.refs_2_, bf16[512,4096]{1,0:T(8,128)(2,1)S(1)} %copy-done.3, ...), custom_call_target="tpu_custom_call" | custom-call | flops 1073741824 | bytes 16777216 | tf_op jit(solution)/shard_map/experts/pallas_call | solution.py:208
  231.7 1.6 collective-permute-done.24
  233.3 1.2 collective-permute-done.28
  234.5 1.1 add_convert_fusion
  (94 shorter events, 9.3 us)
Async XLA Ops:
  0.0 38.0 %copy-start.5 = (bf16[64,4096]{1,0:T(8,128)(2,1)S(1)}, bf16[64,4096]{1,0:T(8,128)(2,1)}, u32[]{:S(2)}) copy-start(bf16[64,4096]{1,0:T(8,128)(2,1)} %v_ref.5) | copy-start | bytes 1572868
  0.0 38.0 %copy-start.4 = (bf16[64,4096]{1,0:T(8,128)(2,1)S(1)}, bf16[64,4096]{1,0:T(8,128)(2,1)}, u32[]{:S(2)}) copy-start(bf16[64,4096]{1,0:T(8,128)(2,1)} %k_ref.5) | copy-start | bytes 1572868
  0.0 97.2 %copy-start.22 = (s32[64,2]{0,1:T(2,128)S(1)}, s32[64,2]{0,1:T(2,128)}, u32[]{:S(2)}) copy-start(s32[64,2]{0,1:T(2,128)} %param.15) | copy-start | bytes 1540
  0.0 97.3 %copy-start.23 = (s32[64,2]{0,1:T(2,128)S(1)}, s32[64,2]{0,1:T(2,128)}, u32[]{:S(2)}) copy-start(s32[64,2]{0,1:T(2,128)} %param.14) | copy-start | bytes 1540
  1.4 36.6 %collective-permute-start.5 = (bf16[2,64,1536]{2,1,0:T(8,128)(2,1)S(1)}, bf16[2,64,1536]{2,1,0:T(8,128)(2,1)S(1)}, u32[]{:S(2)}, u32[]{:S(2)}) collective-permute-start(bf16[2,64,1536]{2,1,0:T(8,128)(2,1)S(1)} %pad_maximum_fusion.4), channel_id=1, source_target_pairs={{12,4},{13,5},{14,6},{15,7},{0,8},{1,9},{2,10},{3,11},{4,12},{5,13... | collective-permute-start | bytes 1179656 | tf_op jit(solution)/shard_map/ppermute | solution.py:26
  5.6 45.7 %collective-permute-start.2 = (bf16[2,64,1536]{2,1,0:T(8,128)(2,1)S(1)}, bf16[2,64,1536]{2,1,0:T(8,128)(2,1)}, u32[]{:S(2)}, u32[]{:S(2)}) collective-permute-start(bf16[2,64,1536]{2,1,0:T(8,128)(2,1)S(1)} %pad_maximum_fusion.3), channel_id=1, source_target_pairs={{12,4},{13,5},{14,6},{15,7},{0,8},{1,9},{2,10},{3,11},{4,12},{5,13... | collective-permute-start | bytes 1179656 | tf_op jit(solution)/shard_map/ppermute | solution.py:26
  5.7 162.2 %collective-permute-start.13 = (bf16[4096,512]{1,0:T(8,128)(2,1)}, bf16[4096,512]{1,0:T(8,128)(2,1)}, u32[]{:S(2)}, u32[]{:S(2)}) collective-permute-start(bf16[4096,512]{1,0:T(8,128)(2,1)} %refs_1_.1), channel_id=1, source_target_pairs={{0,1},{1,0},{2,3},{3,2},{4,5},{5,4},{6,7},{7,6},{8,9},{9,8},{10,11... | collective-permute-start | bytes 12582920 | tf_op jit(solution)/shard_map/ppermute | solution.py:26
  5.8 162.1 %collective-permute-start.14 = (bf16[512,4096]{1,0:T(8,128)(2,1)}, bf16[512,4096]{1,0:T(8,128)(2,1)}, u32[]{:S(2)}, u32[]{:S(2)}) collective-permute-start(bf16[512,4096]{1,0:T(8,128)(2,1)} %refs_3_.1), channel_id=1, source_target_pairs={{0,1},{1,0},{2,3},{3,2},{4,5},{5,4},{6,7},{7,6},{8,9},{9,8},{10,11... | collective-permute-start | bytes 12582920 | tf_op jit(solution)/shard_map/ppermute | solution.py:26
  7.3 44.0 %collective-permute-start.8 = (bf16[2,64,1024]{2,1,0:T(8,128)(2,1)S(1)}, bf16[2,64,1024]{2,1,0:T(8,128)(2,1)}, u32[]{:S(2)}, u32[]{:S(2)}) collective-permute-start(bf16[2,64,1024]{2,1,0:T(8,128)(2,1)S(1)} %pad_maximum_fusion.5), channel_id=1, source_target_pairs={{12,4},{13,5},{14,6},{15,7},{0,8},{1,9},{2,10},{3,11},{4,12},{5,13... | collective-permute-start | bytes 786440 | tf_op jit(solution)/shard_map/ppermute | solution.py:26
  38.0 55.9 %copy-start.11 = (bf16[2,64,1536]{2,1,0:T(8,128)(2,1)}, bf16[2,64,1536]{2,1,0:T(8,128)(2,1)S(1)}, u32[]{:S(2)}) copy-start(bf16[2,64,1536]{2,1,0:T(8,128)(2,1)S(1)} %collective-permute-done.5.refs_2_) | copy-start | bytes 1179652
  38.0 16.9 %collective-permute-start.6 = (bf16[2,64,1536]{2,1,0:T(8,128)(2,1)S(1)}, bf16[2,64,1536]{2,1,0:T(8,128)(2,1)S(1)}, u32[]{:S(2)}, u32[]{:S(2)}) collective-permute-start(bf16[2,64,1536]{2,1,0:T(8,128)(2,1)S(1)} %collective-permute-done.5.refs_2_), channel_id=1, source_target_pairs={{0,1},{1,0},{2,3},{3,2},{4,5},{5,4},{6,7},{7,6},{8,9},{9,8},{10,11... | collective-permute-start | bytes 1179656 | tf_op jit(solution)/shard_map/ppermute | solution.py:26
  51.3 42.5 %collective-permute-start = (bf16[2,64,4096]{2,1,0:T(8,128)(2,1)S(1)}, bf16[2,64,4096]{2,1,0:T(8,128)(2,1)S(1)}, u32[]{:S(2)}, u32[]{:S(2)}) collective-permute-start(bf16[2,64,4096]{2,1,0:T(8,128)(2,1)S(1)} %pad_maximum_fusion), channel_id=1, source_target_pairs={{0,1},{1,0},{2,3},{3,2},{4,5},{5,4},{6,7},{7,6},{8,9},{9,8},{10,11... | collective-permute-start | bytes 3145736 | tf_op jit(solution)/shard_map/ppermute | solution.py:26
  51.3 42.5 %collective-permute-start.1 = (bf16[2,64,4096]{2,1,0:T(8,128)(2,1)S(1)}, bf16[2,64,4096]{2,1,0:T(8,128)(2,1)S(1)}, u32[]{:S(2)}, u32[]{:S(2)}) collective-permute-start(bf16[2,64,4096]{2,1,0:T(8,128)(2,1)S(1)} %pad_maximum_fusion), channel_id=1, source_target_pairs={{14,13},{13,14},{8,15},{7,0},{2,1},{1,2},{6,5},{5,6},{0,7},{15,8},... | collective-permute-start | bytes 3145736 | tf_op jit(solution)/shard_map/ppermute | solution.py:26
  55.6 17.0 %collective-permute-start.7 = (bf16[2,64,1536]{2,1,0:T(8,128)(2,1)S(1)}, bf16[2,64,1536]{2,1,0:T(8,128)(2,1)S(1)}, u32[]{:S(2)}, u32[]{:S(2)}) collective-permute-start(bf16[2,64,1536]{2,1,0:T(8,128)(2,1)S(1)} %collective-permute-done.5.refs_2_), channel_id=1, source_target_pairs={{14,13},{13,14},{8,15},{7,0},{2,1},{1,2},{6,5},{5,6},{0,7},{15,8},... | collective-permute-start | bytes 1179656 | tf_op jit(solution)/shard_map/ppermute | solution.py:26
  73.4 16.5 %collective-permute-start.3 = (bf16[2,64,1536]{2,1,0:T(8,128)(2,1)}, bf16[2,64,1536]{2,1,0:T(8,128)(2,1)S(1)}, u32[]{:S(2)}, u32[]{:S(2)}) collective-permute-start(bf16[2,64,1536]{2,1,0:T(8,128)(2,1)} %collective-permute-done.2.refs_2_), channel_id=1, source_target_pairs={{0,1},{1,0},{2,3},{3,2},{4,5},{5,4},{6,7},{7,6},{8,9},{9,8},{10,11... | collective-permute-start | bytes 1179656 | tf_op jit(solution)/shard_map/ppermute | solution.py:26
  90.6 16.8 %collective-permute-start.10 = (bf16[2,64,1024]{2,1,0:T(8,128)(2,1)}, bf16[2,64,1024]{2,1,0:T(8,128)(2,1)}, u32[]{:S(2)}, u32[]{:S(2)}) collective-permute-start(bf16[2,64,1024]{2,1,0:T(8,128)(2,1)} %collective-permute-done.8.refs_2_), channel_id=1, source_target_pairs={{14,13},{13,14},{8,15},{7,0},{2,1},{1,2},{6,5},{5,6},{0,7},{15,8},... | collective-permute-start | bytes 786440 | tf_op jit(solution)/shard_map/ppermute | solution.py:26
  93.8 13.7 %collective-permute-start.9 = (bf16[2,64,1024]{2,1,0:T(8,128)(2,1)}, bf16[2,64,1024]{2,1,0:T(8,128)(2,1)}, u32[]{:S(2)}, u32[]{:S(2)}) collective-permute-start(bf16[2,64,1024]{2,1,0:T(8,128)(2,1)} %collective-permute-done.8.refs_2_), channel_id=1, source_target_pairs={{0,1},{1,0},{2,3},{3,2},{4,5},{5,4},{6,7},{7,6},{8,9},{9,8},{10,11... | collective-permute-start | bytes 786440 | tf_op jit(solution)/shard_map/ppermute | solution.py:26
  93.9 10.3 %collective-permute-start.4 = (bf16[2,64,1536]{2,1,0:T(8,128)(2,1)}, bf16[2,64,1536]{2,1,0:T(8,128)(2,1)}, u32[]{:S(2)}, u32[]{:S(2)}) collective-permute-start(bf16[2,64,1536]{2,1,0:T(8,128)(2,1)} %collective-permute-done.2.refs_2_), channel_id=1, source_target_pairs={{14,13},{13,14},{8,15},{7,0},{2,1},{1,2},{6,5},{5,6},{0,7},{15,8},... | collective-permute-start | bytes 1179656 | tf_op jit(solution)/shard_map/ppermute | solution.py:26
  97.5 1.0 copy-start.6
  98.6 1.0 copy-start.12
  99.6 1.0 copy-start.14
  100.6 1.0 copy-start.16
  101.6 2.6 %copy-start.18 = (bf16[2,64,1536]{2,1,0:T(8,128)(2,1)S(1)}, bf16[2,64,1536]{2,1,0:T(8,128)(2,1)}, u32[]{:S(2)}) copy-start(bf16[2,64,1536]{2,1,0:T(8,128)(2,1)} %copy-done.17) | copy-start | bytes 1179652
  101.6 5.9 %copy-start.21 = (f32[3,4096]{1,0:T(4,128)S(1)}, f32[3,4096]{1,0:T(4,128)}, u32[]{:S(2)}) copy-start(f32[3,4096]{1,0:T(4,128)} %refs_5_.1) | copy-start | bytes 147460
  111.3 17.6 %collective-permute-start.12 = (bf16[64,4224]{1,0:T(8,128)(2,1)S(1)}, bf16[64,4224]{1,0:T(8,128)(2,1)S(1)}, u32[]{:S(2)}, u32[]{:S(2)}) collective-permute-start(bf16[64,4224]{1,0:T(8,128)(2,1)S(1)} %get-tuple-element.14.refs_0_), channel_id=1, source_target_pairs={{0,4},{1,5},{4,8},{5,9},{8,12},{9,13},{12,14},{13,15},{14,10},{15,... | collective-permute-start | bytes 1622024 | tf_op jit(solution)/shard_map/ppermute | solution.py:26
  111.3 17.6 %collective-permute-start.11 = (bf16[64,4224]{1,0:T(8,128)(2,1)S(1)}, bf16[64,4224]{1,0:T(8,128)(2,1)S(1)}, u32[]{:S(2)}, u32[]{:S(2)}) collective-permute-start(bf16[64,4224]{1,0:T(8,128)(2,1)S(1)} %get-tuple-element.14.refs_0_), channel_id=1, source_target_pairs={{4,0},{5,1},{8,4},{9,5},{12,8},{13,9},{14,12},{15,13},{10,14},{11,... | collective-permute-start | bytes 1622024 | tf_op jit(solution)/shard_map/ppermute | solution.py:26
  128.9 15.0 %collective-permute-start.16 = (bf16[64,4224]{1,0:T(8,128)(2,1)S(1)}, bf16[64,4224]{1,0:T(8,128)(2,1)S(1)}, u32[]{:S(2)}, u32[]{:S(2)}) collective-permute-start(bf16[64,4224]{1,0:T(8,128)(2,1)S(1)} %collective-permute-done.12.refs_1_), channel_id=1, source_target_pairs={{0,4},{1,5},{4,8},{5,9},{8,12},{9,13},{12,14},{13,15},{14,10},{15,... | collective-permute-start | bytes 1622024 | tf_op jit(solution)/shard_map/ppermute | solution.py:26
  128.9 15.0 %collective-permute-start.15 = (bf16[64,4224]{1,0:T(8,128)(2,1)S(1)}, bf16[64,4224]{1,0:T(8,128)(2,1)S(1)}, u32[]{:S(2)}, u32[]{:S(2)}) collective-permute-start(bf16[64,4224]{1,0:T(8,128)(2,1)S(1)} %collective-permute-done.11.refs_0_), channel_id=1, source_target_pairs={{4,0},{5,1},{8,4},{9,5},{12,8},{13,9},{14,12},{15,13},{10,14},{11,... | collective-permute-start | bytes 1622024 | tf_op jit(solution)/shard_map/ppermute | solution.py:26
  143.9 14.3 %collective-permute-start.18 = (bf16[64,4224]{1,0:T(8,128)(2,1)S(1)}, bf16[64,4224]{1,0:T(8,128)(2,1)S(1)}, u32[]{:S(2)}, u32[]{:S(2)}) collective-permute-start(bf16[64,4224]{1,0:T(8,128)(2,1)S(1)} %collective-permute-done.16.refs_1_), channel_id=1, source_target_pairs={{0,4},{1,5},{4,8},{5,9},{8,12},{9,13},{12,14},{13,15},{14,10},{15,... | collective-permute-start | bytes 1622024 | tf_op jit(solution)/shard_map/ppermute | solution.py:26
  143.9 15.3 %copy-start.7 = (bf16[64,4224]{1,0:T(8,128)(2,1)}, bf16[64,4224]{1,0:T(8,128)(2,1)S(1)}, u32[]{:S(2)}) copy-start(bf16[64,4224]{1,0:T(8,128)(2,1)S(1)} %collective-permute-done.15.refs_0_) | copy-start | bytes 1622020
  143.9 15.3 %collective-permute-start.17 = (bf16[64,4224]{1,0:T(8,128)(2,1)S(1)}, bf16[64,4224]{1,0:T(8,128)(2,1)S(1)}, u32[]{:S(2)}, u32[]{:S(2)}) collective-permute-start(bf16[64,4224]{1,0:T(8,128)(2,1)S(1)} %collective-permute-done.15.refs_0_), channel_id=1, source_target_pairs={{4,0},{5,1},{8,4},{9,5},{12,8},{13,9},{14,12},{15,13},{10,14},{11,... | collective-permute-start | bytes 1622024 | tf_op jit(solution)/shard_map/ppermute | solution.py:26
  158.9 7.9 %collective-permute-start.19 = (bf16[32,4224]{1,0:T(8,128)(2,1)}, bf16[32,4224]{1,0:T(8,128)(2,1)S(1)}, u32[]{:S(2)}, u32[]{:S(2)}) collective-permute-start(bf16[32,4224]{1,0:T(8,128)(2,1)} %slice.60), channel_id=1, source_target_pairs={{0,4},{1,5},{4,8},{5,9},{8,12},{9,13},{12,14},{13,15},{14,10},{15,... | collective-permute-start | bytes 811016 | tf_op jit(solution)/shard_map/ppermute | solution.py:26
  159.9 8.0 %collective-permute-start.20 = (bf16[32,4224]{1,0:T(8,128)(2,1)}, bf16[32,4224]{1,0:T(8,128)(2,1)}, u32[]{:S(2)}, u32[]{:S(2)}) collective-permute-start(bf16[32,4224]{1,0:T(8,128)(2,1)} %slice.61), channel_id=1, source_target_pairs={{4,0},{5,1},{8,4},{9,5},{12,8},{13,9},{14,12},{15,13},{10,14},{11,... | collective-permute-start | bytes 811016 | tf_op jit(solution)/shard_map/ppermute | solution.py:26
  167.9 2.2 copy-start
  170.1 2.2 copy-start.2
  178.5 20.4 %collective-permute-start.21 = (bf16[32,4096]{1,0:T(8,128)(2,1)S(1)}, bf16[32,4096]{1,0:T(8,128)(2,1)S(1)}, u32[]{:S(2)}, u32[]{:S(2)}) collective-permute-start(bf16[32,4096]{1,0:T(8,128)(2,1)S(1)} %get-tuple-element.21), channel_id=1, source_target_pairs={{0,4},{1,5},{4,8},{5,9},{8,12},{9,13},{12,14},{13,15},{14,10},{15,... | collective-permute-start | bytes 786440 | tf_op jit(solution)/shard_map/ppermute | solution.py:26
  179.2 7.5 %copy-start.8 = (bf16[64,4224]{1,0:T(8,128)(2,1)S(1)}, bf16[64,4224]{1,0:T(8,128)(2,1)}, u32[]{:S(2)}) copy-start(bf16[64,4224]{1,0:T(8,128)(2,1)} %copy-done.7) | copy-start | bytes 1622020
  179.2 20.6 %collective-permute-start.25 = (bf16[32,4096]{1,0:T(8,128)(2,1)S(1)}, bf16[32,4096]{1,0:T(8,128)(2,1)S(1)}, u32[]{:S(2)}, u32[]{:S(2)}) collective-permute-start(bf16[32,4096]{1,0:T(8,128)(2,1)S(1)} %get-tuple-element.22), channel_id=1, source_target_pairs={{4,0},{5,1},{8,4},{9,5},{12,8},{13,9},{14,12},{15,13},{10,14},{11,... | collective-permute-start | bytes 786440 | tf_op jit(solution)/shard_map/ppermute | solution.py:26
  199.0 27.4 %copy-start.3 = (bf16[512,4096]{1,0:T(8,128)(2,1)S(1)}, bf16[512,4096]{1,0:T(8,128)(2,1)}, u32[]{:S(2)}) copy-start(bf16[512,4096]{1,0:T(8,128)(2,1)} %refs_3_.1) | copy-start | bytes 12582916
  199.1 27.3 %copy-start.1 = (bf16[4096,512]{1,0:T(8,128)(2,1)S(1)}, bf16[4096,512]{1,0:T(8,128)(2,1)}, u32[]{:S(2)}) copy-start(bf16[4096,512]{1,0:T(8,128)(2,1)} %refs_1_.1) | copy-start | bytes 12582916
  199.1 27.3 %copy-start.10 = (bf16[64,4224]{1,0:T(8,128)(2,1)S(1)}, bf16[64,4224]{1,0:T(8,128)(2,1)}, u32[]{:S(2)}) copy-start(bf16[64,4224]{1,0:T(8,128)(2,1)} %copy-done.9) | copy-start | bytes 1622020
  199.1 12.0 %collective-permute-start.22 = (bf16[64,4096]{1,0:T(8,128)(2,1)S(1)}, bf16[64,4096]{1,0:T(8,128)(2,1)S(1)}, u32[]{:S(2)}, u32[]{:S(2)}) collective-permute-start(bf16[64,4096]{1,0:T(8,128)(2,1)S(1)} %pad_maximum_fusion.1), channel_id=1, source_target_pairs={{0,4},{1,5},{4,8},{5,9},{8,12},{9,13},{12,14},{13,15},{14,10},{15,... | collective-permute-start | bytes 1572872 | tf_op jit(solution)/shard_map/ppermute | solution.py:26
  199.9 12.2 %collective-permute-start.26 = (bf16[64,4096]{1,0:T(8,128)(2,1)S(1)}, bf16[64,4096]{1,0:T(8,128)(2,1)S(1)}, u32[]{:S(2)}, u32[]{:S(2)}) collective-permute-start(bf16[64,4096]{1,0:T(8,128)(2,1)S(1)} %pad_maximum_fusion.2), channel_id=1, source_target_pairs={{4,0},{5,1},{8,4},{9,5},{12,8},{13,9},{14,12},{15,13},{10,14},{11,... | collective-permute-start | bytes 1572872 | tf_op jit(solution)/shard_map/ppermute | solution.py:26
  211.2 12.0 %collective-permute-start.23 = (bf16[64,4096]{1,0:T(8,128)(2,1)S(1)}, bf16[64,4096]{1,0:T(8,128)(2,1)S(1)}, u32[]{:S(2)}, u32[]{:S(2)}) collective-permute-start(bf16[64,4096]{1,0:T(8,128)(2,1)S(1)} %add_convert_fusion.4), channel_id=1, source_target_pairs={{0,4},{1,5},{4,8},{5,9},{8,12},{9,13},{12,14},{13,15},{14,10},{15,... | collective-permute-start | bytes 1572872 | tf_op jit(solution)/shard_map/ppermute | solution.py:26
  212.2 12.0 %collective-permute-start.27 = (bf16[64,4096]{1,0:T(8,128)(2,1)S(1)}, bf16[64,4096]{1,0:T(8,128)(2,1)S(1)}, u32[]{:S(2)}, u32[]{:S(2)}) collective-permute-start(bf16[64,4096]{1,0:T(8,128)(2,1)S(1)} %add_convert_fusion.2), channel_id=1, source_target_pairs={{4,0},{5,1},{8,4},{9,5},{12,8},{13,9},{14,12},{15,13},{10,14},{11,... | collective-permute-start | bytes 1572872 | tf_op jit(solution)/shard_map/ppermute | solution.py:26
  223.3 10.0 %collective-permute-start.24 = (bf16[64,4096]{1,0:T(8,128)(2,1)S(1)}, bf16[64,4096]{1,0:T(8,128)(2,1)S(1)}, u32[]{:S(2)}, u32[]{:S(2)}) collective-permute-start(bf16[64,4096]{1,0:T(8,128)(2,1)S(1)} %add_convert_fusion.3), channel_id=1, source_target_pairs={{0,4},{1,5},{4,8},{5,9},{8,12},{9,13},{12,14},{13,15},{14,10},{15,... | collective-permute-start | bytes 1572872 | tf_op jit(solution)/shard_map/ppermute | solution.py:26
  224.3 10.2 %collective-permute-start.28 = (bf16[64,4096]{1,0:T(8,128)(2,1)S(1)}, bf16[64,4096]{1,0:T(8,128)(2,1)S(1)}, u32[]{:S(2)}, u32[]{:S(2)}) collective-permute-start(bf16[64,4096]{1,0:T(8,128)(2,1)S(1)} %add_convert_fusion.1), channel_id=1, source_target_pairs={{4,0},{5,1},{8,4},{9,5},{12,8},{13,9},{14,12},{15,13},{10,14},{11,... | collective-permute-start | bytes 1572872 | tf_op jit(solution)/shard_map/ppermute | solution.py:26
  226.4 8.1 %copy-start.20 = (bf16[64,1024]{1,0:T(8,128)(2,1)S(1)}, bf16[64,1024]{1,0:T(8,128)(2,1)}, u32[]{:S(2)}) copy-start(bf16[64,1024]{1,0:T(8,128)(2,1)} %copy-done.19) | copy-start | bytes 393220
  (5 other events, 3.7 us)

commit v2 on v1

--- a/solution.py
+++ b/solution.py
@@ -15,11 +15,12 @@
 CORES = 2
 EPSILON = 1e-06
 MASKED = -1e30
-HEADS = (12, 12, 8)
+HEADS = (12, 14, 6)
 HEAD_GROUP = 4
 HIDDEN_STEP = 512
 LANES = 128
-KERNEL_VMEM = 40 * 2**20
+ATTEND_VMEM = 16 * 2**20
+EXPERT_VMEM = 26 * 2**20
 
 
 def permute(x, pairs):
@@ -57,7 +58,7 @@
     return vertical, sides
 
 
-def attention_kernel(heads, sources, last, flags_ref, q_ref, k_ref, v_ref, *refs):
+def attention_kernel(start, heads, sources, last, flags_ref, q_ref, k_ref, v_ref, *refs):
     around = refs[: sources - 1]
     rest = refs[sources - 1 :]
     if last:
@@ -78,19 +79,27 @@
             slice(h * HEAD_DIM, (h + 1) * HEAD_DIM)
             for h in range(first, min(heads, first + HEAD_GROUP))
         ]
-        keys = [jnp.concatenate([k_ref[:, c]] + [r[0, :, c] for r in around], axis=0) for c in cols]
+        there = [slice(start + c.start, start + c.stop) for c in cols]
+        pick = lambda ref, i, c, t: ref[i, :, t if ref.shape[2] == q_ref.shape[1] else c]
+        keys = [
+            jnp.concatenate([k_ref[:, t]] + [pick(r, 0, c, t) for r in around], axis=0)
+            for c, t in zip(cols, there)
+        ]
         scores = [
             lax.dot_general(
-                q_ref[:, c], k, (((1,), (1,)), ((), ())), preferred_element_type=jnp.float32
+                q_ref[:, t], k, (((1,), (1,)), ((), ())), preferred_element_type=jnp.float32
             )
-            for c, k in zip(cols, keys)
+            for t, k in zip(there, keys)
         ]
         scores = [jnp.where(bias < 0.0, MASKED, x * scale) for x in scores]
         highest = [jnp.max(x, axis=-1, keepdims=True) for x in scores]
         raised = [jnp.exp(x - m) for x, m in zip(scores, highest)]
         total = [jnp.sum(x, axis=-1, keepdims=True) for x in raised]
         probs = [(x / t).astype(jnp.bfloat16) for x, t in zip(raised, total)]
-        vals = [jnp.concatenate([v_ref[:, c]] + [r[1, :, c] for r in around], axis=0) for c in cols]
+        vals = [
+            jnp.concatenate([v_ref[:, t]] + [pick(r, 1, c, t) for r in around], axis=0)
+            for c, t in zip(cols, there)
+        ]
         pieces = [jnp.dot(p, v, preferred_element_type=jnp.float32) for p, v in zip(probs, vals)]
         for c, piece in zip(cols, pieces):
             out_ref[:, c] = piece.astype(jnp.bfloat16)
@@ -101,10 +110,10 @@
         center = sum(jnp.sum(w, axis=-1, keepdims=True) for w in wide) / count
         spread = sum(jnp.sum(jnp.square(w - center), axis=-1, keepdims=True) for w in wide) / count
         factor = lax.rsqrt(spread + EPSILON)
-        start = 0
+        done = 0
         for w in wide:
-            cols = slice(start, start + w.shape[1])
-            start += w.shape[1]
+            cols = slice(done, done + w.shape[1])
+            done += w.shape[1]
             normed_ref[:, cols] = (
                 (w - center) * factor * (1.0 + modulation_ref[1:2, cols])
                 + modulation_ref[0:1, cols]
@@ -116,27 +125,18 @@
     rows, width = queries.shape
     sources = 1 + len(around)
     last = len(extra) > 0
-    window = start // part
-    flat = pl.BlockSpec((rows, part), lambda i, f: (0, window))
-    deep = pl.BlockSpec((2, rows, part), lambda i, f: (0, 0, window))
-    whole = lambda x: pl.BlockSpec(x.shape, lambda i, f: (0,) * x.ndim)
     operands = [queries, key_rows, values] + around
-    specs = [flat] * 3 + [deep if x.shape[2] == width else whole(x) for x in around]
     out_shape = [jax.ShapeDtypeStruct((rows, part), jnp.bfloat16)]
     if last:
         operands += extra + before
-        specs += [whole(x) for x in extra + before]
         out_shape.append(jax.ShapeDtypeStruct((rows, width + LANES), jnp.bfloat16))
+    resident = pl.BlockSpec(memory_space=pltpu.VMEM)
     return pl.pallas_call(
-        functools.partial(attention_kernel, part // HEAD_DIM, sources, last),
+        functools.partial(attention_kernel, start, part // HEAD_DIM, sources, last),
         out_shape=out_shape,
-        grid_spec=pltpu.PrefetchScalarGridSpec(
-            num_scalar_prefetch=1,
-            grid=(1,),
-            in_specs=specs,
-            out_specs=[whole(x) for x in out_shape],
-        ),
-        compiler_params=pltpu.CompilerParams(vmem_limit_bytes=KERNEL_VMEM),
+        in_specs=[pl.BlockSpec(memory_space=pltpu.SMEM)] + [resident] * len(operands),
+        out_specs=[resident] * len(out_shape),
+        compiler_params=pltpu.CompilerParams(vmem_limit_bytes=ATTEND_VMEM),
         cost_estimate=pl.CostEstimate(
             flops=4 * rows * sources * rows * part,
             bytes_accessed=(2 * sources + 2) * rows * part * 2,
@@ -218,7 +218,7 @@
             pltpu.SemaphoreType.DMA((steps,)),
             pltpu.SemaphoreType.DMA((steps,)),
         ],
-        compiler_params=pltpu.CompilerParams(vmem_limit_bytes=KERNEL_VMEM),
+        compiler_params=pltpu.CompilerParams(vmem_limit_bytes=EXPERT_VMEM),
         cost_estimate=pl.CostEstimate(
             flops=4 * count * rows * width * hidden,
             bytes_accessed=4 * width * hidden,

time: 236 us -> 214 us (0.907)
  waiting for transfers between devices: 121 us -> 104 us
  Pallas kernels: 38.2 us -> 34.6 us
    ppermute x29, waiting for transfers between devices: 121 us -> 104 us  [permute(): return lax.ppermute(x, 'tile', pairs)]
    pallas_call x5, Pallas kernels: 29.7 us -> 26.9 us  [run_experts(): pl.pallas_call(functools.partial(experts_kernel, count, len(flat)), out_s...]
    unnamed x48 -> x44, local copies, waits for them, and re-layouts: 12.1 us -> 10.5 us
  transfers between devices with their start and end apart: 29 -> 29, of which waited for: 14 -> 16; matrix products, arithmetic and copies ran while one was open for 2% -> 3% of each run, Pallas kernels for 14% -> 13%
where the time goes in v2:
time: 214 us
  waiting for transfers between devices  104 us (49%)
  starting transfers between devices  54.8 us (26%)
  Pallas kernels  34.6 us (16%)
  local copies, waits for them, and re-layouts  16.9 us (8%)
  other arithmetic  2.68 us (1%)
    ppermute x29, waiting for transfers between devices, permute(): return lax.ppermute(x, 'tile', pairs)  104 us
    ppermute x29, starting transfers between devices, permute(): return lax.ppermute(x, 'tile', pairs)  54.8 us
    pallas_call x5, Pallas kernels, run_experts(): pl.pallas_call(functools.partial(experts_kernel, count, len(flat)), out_s...  26.9 us
    unnamed x44, local copies, waits for them, and re-layouts  10.5 us
    pallas_call x3, Pallas kernels, attend_chunk(): pl.pallas_call(functools.partial(attention_kernel, start, part // HEAD_DI...  7.71 us
  transfers between devices with their start and end apart: 29, of which 16 were waited for; matrix products, arithmetic and copies ran while one was open for 3% of the time, Pallas kernels for 13%

profile of v2, /device:TPU:0, one launch (start us, length us, event | category | flops | bytes accessed | tf_op | source)
XLA Modules:
  0.0 213.6 jit_solution(12221281378731510970)
XLA Ops:
  0.0 1.1 slice_bitcast_fusion.2
  1.2 4.1 %collective-permute-start.2 = (bf16[2,64,1536]{2,1,0:T(8,128)(2,1)S(1)}, bf16[2,64,1536]{2,1,0:T(8,128)(2,1)S(1)}, u32[]{:S(2)}, u32[]{:S(2)}) collective-permute-start(bf16[2,64,1536]{2,1,0:T(8,128)(2,1)S(1)} %pad_maximum_fusion.4), channel_id=1, source_target_pairs={{12,4},{13,5},{14,6},{15,7},{0,8},{1,9},{2,10},{3,11},{4,12},{5,13... | collective-permute-start | bytes 1179656 | tf_op jit(solution)/shard_map/ppermute | solution.py:27
  5.3 1.0 slice_bitcast_fusion.4
  7.0 1.1 slice_bitcast_fusion
  8.1 2.9 %collective-permute-start.5 = (bf16[2,64,1792]{2,1,0:T(8,128)(2,1)S(1)}, bf16[2,64,1792]{2,1,0:T(8,128)(2,1)}, u32[]{:S(2)}, u32[]{:S(2)}) collective-permute-start(bf16[2,64,1792]{2,1,0:T(8,128)(2,1)S(1)} %pad_maximum_fusion.3), channel_id=1, source_target_pairs={{12,4},{13,5},{14,6},{15,7},{0,8},{1,9},{2,10},{3,11},{4,12},{5,13... | collective-permute-start | bytes 1376264 | tf_op jit(solution)/shard_map/ppermute | solution.py:27
  11.0 26.7 %collective-permute-done.2.refs_2_ = bf16[2,64,1536]{2,1,0:T(8,128)(2,1)S(1)} collective-permute-done((bf16[2,64,1536]{2,1,0:T(8,128)(2,1)S(1)}, bf16[2,64,1536]{2,1,0:T(8,128)(2,1)S(1)}, u32[]{:S(2)}, u32[]{:S(2)}) %collective-permute-start.2) | collective-permute-done | bytes 393248 | tf_op jit(solution)/shard_map/ppermute | solution.py:27
  37.8 4.3 %collective-permute-done.8.refs_2_ = bf16[2,64,768]{2,1,0:T(8,128)(2,1)} collective-permute-done((bf16[2,64,768]{2,1,0:T(8,128)(2,1)S(1)}, bf16[2,64,768]{2,1,0:T(8,128)(2,1)}, u32[]{:S(2)}, u32[]{:S(2)}) %collective-permute-start.8) | collective-permute-done | bytes 196640 | tf_op jit(solution)/shard_map/ppermute | solution.py:27
  42.1 2.2 %collective-permute-start.4 = (bf16[2,64,1536]{2,1,0:T(8,128)(2,1)S(1)}, bf16[2,64,1536]{2,1,0:T(8,128)(2,1)S(1)}, u32[]{:S(2)}, u32[]{:S(2)}) collective-permute-start(bf16[2,64,1536]{2,1,0:T(8,128)(2,1)S(1)} %collective-permute-done.2.refs_2_), channel_id=1, source_target_pairs={{14,13},{13,14},{8,15},{7,0},{2,1},{1,2},{6,5},{5,6},{0,7},{15,8},... | collective-permute-start | bytes 1179656 | tf_op jit(solution)/shard_map/ppermute | solution.py:27
  44.5 6.6 %collective-permute-done.5.refs_2_ = bf16[2,64,1792]{2,1,0:T(8,128)(2,1)} collective-permute-done((bf16[2,64,1792]{2,1,0:T(8,128)(2,1)S(1)}, bf16[2,64,1792]{2,1,0:T(8,128)(2,1)}, u32[]{:S(2)}, u32[]{:S(2)}) %collective-permute-start.5) | collective-permute-done | bytes 458784 | tf_op jit(solution)/shard_map/ppermute | solution.py:27
  51.8 3.6 %collective-permute-start.1 = (bf16[2,64,4096]{2,1,0:T(8,128)(2,1)S(1)}, bf16[2,64,4096]{2,1,0:T(8,128)(2,1)S(1)}, u32[]{:S(2)}, u32[]{:S(2)}) collective-permute-start(bf16[2,64,4096]{2,1,0:T(8,128)(2,1)S(1)} %pad_maximum_fusion), channel_id=1, source_target_pairs={{14,13},{13,14},{8,15},{7,0},{2,1},{1,2},{6,5},{5,6},{0,7},{15,8},... | collective-permute-start | bytes 3145736 | tf_op jit(solution)/shard_map/ppermute | solution.py:27
  57.0 2.0 collective-permute-done.6.refs_3_
  59.7 2.1 collective-permute-start.7
  61.9 4.3 %collective-permute-start.10 = (bf16[2,64,768]{2,1,0:T(8,128)(2,1)}, bf16[2,64,768]{2,1,0:T(8,128)(2,1)}, u32[]{:S(2)}, u32[]{:S(2)}) collective-permute-start(bf16[2,64,768]{2,1,0:T(8,128)(2,1)} %collective-permute-done.8.refs_2_), channel_id=1, source_target_pairs={{14,13},{13,14},{8,15},{7,0},{2,1},{1,2},{6,5},{5,6},{0,7},{15,8},... | collective-permute-start | bytes 589832 | tf_op jit(solution)/shard_map/ppermute | solution.py:27
  66.3 2.7 %collective-permute-done.1.refs_1_ = bf16[2,64,4096]{2,1,0:T(8,128)(2,1)S(1)} collective-permute-done((bf16[2,64,4096]{2,1,0:T(8,128)(2,1)S(1)}, bf16[2,64,4096]{2,1,0:T(8,128)(2,1)S(1)}, u32[]{:S(2)}, u32[]{:S(2)}) %collective-permute-start.1) | collective-permute-done | bytes 1048608 | tf_op jit(solution)/shard_map/ppermute | solution.py:27
  68.9 17.8 %collective-permute-start.9 = (bf16[2,64,768]{2,1,0:T(8,128)(2,1)}, bf16[2,64,768]{2,1,0:T(8,128)(2,1)}, u32[]{:S(2)}, u32[]{:S(2)}) collective-permute-start(bf16[2,64,768]{2,1,0:T(8,128)(2,1)} %collective-permute-done.8.refs_2_), channel_id=1, source_target_pairs={{0,1},{1,0},{2,3},{3,2},{4,5},{5,4},{6,7},{7,6},{8,9},{9,8},{10,11... | collective-permute-start | bytes 589832 | tf_op jit(solution)/shard_map/ppermute | solution.py:27
  88.2 1.0 copy-done.6
  89.2 1.0 copy-done.16
  90.2 1.0 copy-done.18
  91.2 2.1 attend.2.refs_7_
  93.4 3.1 %attend.3.refs_8_ = bf16[64,1792]{1,0:T(8,128)(2,1)S(1)} custom-call(s32[6]{0:T(128)S(1)} %add_convert_fusion.7.flags_ref, bf16[64,4096]{1,0:T(8,128)(2,1)S(1)} %copy-done.6, bf16[64,4096]{1,0:T(8,128)(2,1)S(1)} %copy-done.4, bf16[64,4096]{1,0:T(8,128)(2,1)S(1)} %copy-done.5, bf16[2,64,4096]{2,1,0:T(8,128)(2,1)S(1)} %collective-permute-done.refs_0_, ...), custom_call_target="tpu_custom_call" | custom-call | flops 176160768 | bytes 3211264 | tf_op jit(solution)/shard_map/attend/pallas_call | solution.py:134
  96.5 2.5 %attend_last.1 = (bf16[64,768]{1,0:T(8,128)(2,1)S(1)}, bf16[64,4224]{1,0:T(8,128)(2,1)S(1)}) custom-call(s32[6]{0:T(128)S(1)} %add_convert_fusion.7.flags_ref, bf16[64,4096]{1,0:T(8,128)(2,1)S(1)} %copy-done.6, bf16[64,4096]{1,0:T(8,128)(2,1)S(1)} %copy-done.4, bf16[64,4096]{1,0:T(8,128)(2,1)S(1)} %copy-done.5, ...), custom_call_target="tpu_custom_call" | custom-call | flops 75497472 | bytes 1376256 | tf_op jit(solution)/shard_map/attend_last/pallas_call | solution.py:134
  99.1 2.0 collective-permute-start.11
  101.9 11.4 %collective-permute-done.12.refs_1_ = bf16[64,4224]{1,0:T(8,128)(2,1)S(1)} collective-permute-done((bf16[64,4224]{1,0:T(8,128)(2,1)S(1)}, bf16[64,4224]{1,0:T(8,128)(2,1)S(1)}, u32[]{:S(2)}, u32[]{:S(2)}) %collective-permute-start.12) | collective-permute-done | bytes 540704 | tf_op jit(solution)/shard_map/ppermute | solution.py:27
  113.6 1.7 collective-permute-start.15
  115.3 11.3 %collective-permute-done.16.refs_1_ = bf16[64,4224]{1,0:T(8,128)(2,1)S(1)} collective-permute-done((bf16[64,4224]{1,0:T(8,128)(2,1)S(1)}, bf16[64,4224]{1,0:T(8,128)(2,1)S(1)}, u32[]{:S(2)}, u32[]{:S(2)}) %collective-permute-start.16) | collective-permute-done | bytes 540704 | tf_op jit(solution)/shard_map/ppermute | solution.py:27
  127.2 1.5 collective-permute-start.17
  128.6 10.5 %collective-permute-done.18.refs_1_ = bf16[64,4224]{1,0:T(8,128)(2,1)S(1)} collective-permute-done((bf16[64,4224]{1,0:T(8,128)(2,1)S(1)}, bf16[64,4224]{1,0:T(8,128)(2,1)S(1)}, u32[]{:S(2)}, u32[]{:S(2)}) %collective-permute-start.18) | collective-permute-done | bytes 540704 | tf_op jit(solution)/shard_map/ppermute | solution.py:27
  141.8 1.6 collective-permute-start.20
  143.4 4.9 %collective-permute-done.19.refs_0_ = bf16[32,4224]{1,0:T(8,128)(2,1)S(1)} collective-permute-done((bf16[32,4224]{1,0:T(8,128)(2,1)}, bf16[32,4224]{1,0:T(8,128)(2,1)S(1)}, u32[]{:S(2)}, u32[]{:S(2)}) %collective-permute-start.19) | collective-permute-done | bytes 270368 | tf_op jit(solution)/shard_map/ppermute | solution.py:27
  149.0 2.2 %copy-done = bf16[4096,512]{1,0:T(8,128)(2,1)S(1)} copy-done((bf16[4096,512]{1,0:T(8,128)(2,1)S(1)}, bf16[4096,512]{1,0:T(8,128)(2,1)}, u32[]{:S(2)}) %copy-start) | copy-done | bytes 4194328
  151.2 2.2 %copy-done.2 = bf16[512,4096]{1,0:T(8,128)(2,1)S(1)} copy-done((bf16[512,4096]{1,0:T(8,128)(2,1)S(1)}, bf16[512,4096]{1,0:T(8,128)(2,1)}, u32[]{:S(2)}) %copy-start.2) | copy-done | bytes 4194328
  153.4 6.2 %experts.8 = bf16[64,4096]{1,0:T(8,128)(2,1)S(1)} custom-call(s32[1]{0:T(128)} %bitcast.10.mine_ref, bf16[32,4224]{1,0:T(8,128)(2,1)S(1)} %collective-permute-done.19.refs_0_, bf16[32,4224]{1,0:T(8,128)(2,1)} %collective-permute-done.20.refs_1_, bf16[4096,512]{1,0:T(8,128)(2,1)S(1)} %copy-done, bf16[4096,512]{1,0:T(8,128)(2,1)} %collective-permute-done.13.refs_3_.refs_2_, ...), custom_call_target="tpu_custom_call" | custom-call | flops 1073741824 | bytes 16777216 | tf_op jit(solution)/shard_map/experts/pallas_call | solution.py:208
  159.6 1.5 collective-permute-start.21
  161.8 5.2 %experts.7 = (bf16[64,4096]{1,0:T(8,128)(2,1)S(1)}, bf16[64,4096]{1,0:T(8,128)(2,1)S(1)}) custom-call(s32[1]{0:T(128)} %bitcast.10.mine_ref, bf16[64,4224]{1,0:T(8,128)(2,1)S(1)} %collective-permute-done.17.refs_0_, bf16[64,4224]{1,0:T(8,128)(2,1)S(1)} %collective-permute-done.18.refs_1_, bf16[4096,512]{1,0:T(8,128)(2,1)S(1)} %copy-done, ...), custom_call_target="tpu_custom_call" | custom-call | flops 2147483648 | bytes 16777216 | tf_op jit(solution)/shard_map/experts/pallas_call | solution.py:208
  166.9 5.2 %experts.6 = (bf16[64,4096]{1,0:T(8,128)(2,1)S(1)}, bf16[64,4096]{1,0:T(8,128)(2,1)S(1)}) custom-call(s32[1]{0:T(128)} %bitcast.10.mine_ref, bf16[64,4224]{1,0:T(8,128)(2,1)S(1)} %copy-done.10, bf16[64,4224]{1,0:T(8,128)(2,1)S(1)} %collective-permute-done.16.refs_1_, bf16[4096,512]{1,0:T(8,128)(2,1)S(1)} %copy-done, ...), custom_call_target="tpu_custom_call" | custom-call | flops 2147483648 | bytes 16777216 | tf_op jit(solution)/shard_map/experts/pallas_call | solution.py:208
  172.2 5.2 %experts.5 = (bf16[64,4096]{1,0:T(8,128)(2,1)S(1)}, bf16[64,4096]{1,0:T(8,128)(2,1)S(1)}) custom-call(s32[1]{0:T(128)} %bitcast.10.mine_ref, bf16[64,4224]{1,0:T(8,128)(2,1)S(1)} %collective-permute-done.11.refs_0_, bf16[64,4224]{1,0:T(8,128)(2,1)S(1)} %collective-permute-done.12.refs_1_, bf16[4096,512]{1,0:T(8,128)(2,1)S(1)} %copy-done, ...), custom_call_target="tpu_custom_call" | custom-call | flops 2147483648 | bytes 16777216 | tf_op jit(solution)/shard_map/experts/pallas_call | solution.py:208
  177.5 1.5 collective-permute-start.22
  179.7 9.7 %collective-permute-done.22 = bf16[64,4096]{1,0:T(8,128)(2,1)S(1)} collective-permute-done((bf16[64,4096]{1,0:T(8,128)(2,1)S(1)}, bf16[64,4096]{1,0:T(8,128)(2,1)S(1)}, u32[]{:S(2)}, u32[]{:S(2)}) %collective-permute-start.22) | collective-permute-done | bytes 524320 | tf_op jit(solution)/shard_map/ppermute | solution.py:27
  189.6 1.0 collective-permute-start.23
  190.7 1.1 collective-permute-start.27
  191.8 9.7 %collective-permute-done.23 = bf16[64,4096]{1,0:T(8,128)(2,1)S(1)} collective-permute-done((bf16[64,4096]{1,0:T(8,128)(2,1)S(1)}, bf16[64,4096]{1,0:T(8,128)(2,1)S(1)}, u32[]{:S(2)}, u32[]{:S(2)}) %collective-permute-start.23) | collective-permute-done | bytes 524320 | tf_op jit(solution)/shard_map/ppermute | solution.py:27
  201.7 1.0 collective-permute-start.24
  202.8 1.1 collective-permute-start.28
  203.9 0.9 slice.51
  204.8 5.2 %experts.9 = bf16[64,4096]{1,0:T(8,128)(2,1)S(1)} custom-call(s32[1]{0:T(128)} %bitcast.10.mine_ref, bf16[64,4224]{1,0:T(8,128)(2,1)S(1)} %copy-done.12, bf16[4096,512]{1,0:T(8,128)(2,1)S(1)} %copy-done.1, bf16[4096,512]{1,0:T(8,128)(2,1)} %collective-permute-done.13.refs_3_.refs_2_, bf16[512,4096]{1,0:T(8,128)(2,1)S(1)} %copy-done.3, ...), custom_call_target="tpu_custom_call" | custom-call | flops 1073741824 | bytes 16777216 | tf_op jit(solution)/shard_map/experts/pallas_call | solution.py:208
  210.1 1.4 collective-permute-done.24
  211.5 1.0 collective-permute-done.28
  212.5 1.1 add_convert_fusion
  (91 shorter events, 12.7 us)
Async XLA Ops:
  0.0 44.3 %copy-start.5 = (bf16[64,4096]{1,0:T(8,128)(2,1)S(1)}, bf16[64,4096]{1,0:T(8,128)(2,1)}, u32[]{:S(2)}) copy-start(bf16[64,4096]{1,0:T(8,128)(2,1)} %v_ref.5) | copy-start | bytes 1572868
  0.0 44.3 %copy-start.4 = (bf16[64,4096]{1,0:T(8,128)(2,1)S(1)}, bf16[64,4096]{1,0:T(8,128)(2,1)}, u32[]{:S(2)}) copy-start(bf16[64,4096]{1,0:T(8,128)(2,1)} %k_ref.5) | copy-start | bytes 1572868
  0.0 57.0 %copy-start.21 = (s32[64,2]{0,1:T(2,128)S(1)}, s32[64,2]{0,1:T(2,128)}, u32[]{:S(2)}) copy-start(s32[64,2]{0,1:T(2,128)} %param.14) | copy-start | bytes 1540
  0.0 61.9 %copy-start.20 = (s32[64,2]{0,1:T(2,128)S(1)}, s32[64,2]{0,1:T(2,128)}, u32[]{:S(2)}) copy-start(s32[64,2]{0,1:T(2,128)} %param.15) | copy-start | bytes 1540
  1.2 36.6 %collective-permute-start.2 = (bf16[2,64,1536]{2,1,0:T(8,128)(2,1)S(1)}, bf16[2,64,1536]{2,1,0:T(8,128)(2,1)S(1)}, u32[]{:S(2)}, u32[]{:S(2)}) collective-permute-start(bf16[2,64,1536]{2,1,0:T(8,128)(2,1)S(1)} %pad_maximum_fusion.4), channel_id=1, source_target_pairs={{12,4},{13,5},{14,6},{15,7},{0,8},{1,9},{2,10},{3,11},{4,12},{5,13... | collective-permute-start | bytes 1179656 | tf_op jit(solution)/shard_map/ppermute | solution.py:27
  6.3 35.8 %collective-permute-start.8 = (bf16[2,64,768]{2,1,0:T(8,128)(2,1)S(1)}, bf16[2,64,768]{2,1,0:T(8,128)(2,1)}, u32[]{:S(2)}, u32[]{:S(2)}) collective-permute-start(bf16[2,64,768]{2,1,0:T(8,128)(2,1)S(1)} %pad_maximum_fusion.5), channel_id=1, source_target_pairs={{12,4},{13,5},{14,6},{15,7},{0,8},{1,9},{2,10},{3,11},{4,12},{5,13... | collective-permute-start | bytes 589832 | tf_op jit(solution)/shard_map/ppermute | solution.py:27
  6.4 142.6 %collective-permute-start.13 = (bf16[4096,512]{1,0:T(8,128)(2,1)}, bf16[4096,512]{1,0:T(8,128)(2,1)}, u32[]{:S(2)}, u32[]{:S(2)}) collective-permute-start(bf16[4096,512]{1,0:T(8,128)(2,1)} %refs_1_.1), channel_id=1, source_target_pairs={{0,1},{1,0},{2,3},{3,2},{4,5},{5,4},{6,7},{7,6},{8,9},{9,8},{10,11... | collective-permute-start | bytes 12582920 | tf_op jit(solution)/shard_map/ppermute | solution.py:27
  6.5 142.5 %collective-permute-start.14 = (bf16[512,4096]{1,0:T(8,128)(2,1)}, bf16[512,4096]{1,0:T(8,128)(2,1)}, u32[]{:S(2)}, u32[]{:S(2)}) collective-permute-start(bf16[512,4096]{1,0:T(8,128)(2,1)} %refs_3_.1), channel_id=1, source_target_pairs={{0,1},{1,0},{2,3},{3,2},{4,5},{5,4},{6,7},{7,6},{8,9},{9,8},{10,11... | collective-permute-start | bytes 12582920 | tf_op jit(solution)/shard_map/ppermute | solution.py:27
  8.1 43.0 %collective-permute-start.5 = (bf16[2,64,1792]{2,1,0:T(8,128)(2,1)S(1)}, bf16[2,64,1792]{2,1,0:T(8,128)(2,1)}, u32[]{:S(2)}, u32[]{:S(2)}) collective-permute-start(bf16[2,64,1792]{2,1,0:T(8,128)(2,1)S(1)} %pad_maximum_fusion.3), channel_id=1, source_target_pairs={{12,4},{13,5},{14,6},{15,7},{0,8},{1,9},{2,10},{3,11},{4,12},{5,13... | collective-permute-start | bytes 1376264 | tf_op jit(solution)/shard_map/ppermute | solution.py:27
  37.8 13.3 %collective-permute-start.3 = (bf16[2,64,1536]{2,1,0:T(8,128)(2,1)S(1)}, bf16[2,64,1536]{2,1,0:T(8,128)(2,1)S(1)}, u32[]{:S(2)}, u32[]{:S(2)}) collective-permute-start(bf16[2,64,1536]{2,1,0:T(8,128)(2,1)S(1)} %collective-permute-done.2.refs_2_), channel_id=1, source_target_pairs={{0,1},{1,0},{2,3},{3,2},{4,5},{5,4},{6,7},{7,6},{8,9},{9,8},{10,11... | collective-permute-start | bytes 1179656 | tf_op jit(solution)/shard_map/ppermute | solution.py:27
  42.1 14.1 %collective-permute-start.4 = (bf16[2,64,1536]{2,1,0:T(8,128)(2,1)S(1)}, bf16[2,64,1536]{2,1,0:T(8,128)(2,1)S(1)}, u32[]{:S(2)}, u32[]{:S(2)}) collective-permute-start(bf16[2,64,1536]{2,1,0:T(8,128)(2,1)S(1)} %collective-permute-done.2.refs_2_), channel_id=1, source_target_pairs={{14,13},{13,14},{8,15},{7,0},{2,1},{1,2},{6,5},{5,6},{0,7},{15,8},... | collective-permute-start | bytes 1179656 | tf_op jit(solution)/shard_map/ppermute | solution.py:27
  51.1 10.8 %collective-permute-start = (bf16[2,64,4096]{2,1,0:T(8,128)(2,1)S(1)}, bf16[2,64,4096]{2,1,0:T(8,128)(2,1)S(1)}, u32[]{:S(2)}, u32[]{:S(2)}) collective-permute-start(bf16[2,64,4096]{2,1,0:T(8,128)(2,1)S(1)} %pad_maximum_fusion), channel_id=1, source_target_pairs={{0,1},{1,0},{2,3},{3,2},{4,5},{5,4},{6,7},{7,6},{8,9},{9,8},{10,11... | collective-permute-start | bytes 3145736 | tf_op jit(solution)/shard_map/ppermute | solution.py:27
  51.8 17.1 %collective-permute-start.1 = (bf16[2,64,4096]{2,1,0:T(8,128)(2,1)S(1)}, bf16[2,64,4096]{2,1,0:T(8,128)(2,1)S(1)}, u32[]{:S(2)}, u32[]{:S(2)}) collective-permute-start(bf16[2,64,4096]{2,1,0:T(8,128)(2,1)S(1)} %pad_maximum_fusion), channel_id=1, source_target_pairs={{14,13},{13,14},{8,15},{7,0},{2,1},{1,2},{6,5},{5,6},{0,7},{15,8},... | collective-permute-start | bytes 3145736 | tf_op jit(solution)/shard_map/ppermute | solution.py:27
  57.0 2.0 collective-permute-start.6
  59.7 33.6 %collective-permute-start.7 = (bf16[2,64,1792]{2,1,0:T(8,128)(2,1)}, bf16[2,64,1792]{2,1,0:T(8,128)(2,1)}, u32[]{:S(2)}, u32[]{:S(2)}) collective-permute-start(bf16[2,64,1792]{2,1,0:T(8,128)(2,1)} %collective-permute-done.5.refs_2_), channel_id=1, source_target_pairs={{14,13},{13,14},{8,15},{7,0},{2,1},{1,2},{6,5},{5,6},{0,7},{15,8},... | collective-permute-start | bytes 1376264 | tf_op jit(solution)/shard_map/ppermute | solution.py:27
  61.9 34.6 %collective-permute-start.10 = (bf16[2,64,768]{2,1,0:T(8,128)(2,1)}, bf16[2,64,768]{2,1,0:T(8,128)(2,1)}, u32[]{:S(2)}, u32[]{:S(2)}) collective-permute-start(bf16[2,64,768]{2,1,0:T(8,128)(2,1)} %collective-permute-done.8.refs_2_), channel_id=1, source_target_pairs={{14,13},{13,14},{8,15},{7,0},{2,1},{1,2},{6,5},{5,6},{0,7},{15,8},... | collective-permute-start | bytes 589832 | tf_op jit(solution)/shard_map/ppermute | solution.py:27
  68.9 27.6 %collective-permute-start.9 = (bf16[2,64,768]{2,1,0:T(8,128)(2,1)}, bf16[2,64,768]{2,1,0:T(8,128)(2,1)}, u32[]{:S(2)}, u32[]{:S(2)}) collective-permute-start(bf16[2,64,768]{2,1,0:T(8,128)(2,1)} %collective-permute-done.8.refs_2_), channel_id=1, source_target_pairs={{0,1},{1,0},{2,3},{3,2},{4,5},{5,4},{6,7},{7,6},{8,9},{9,8},{10,11... | collective-permute-start | bytes 589832 | tf_op jit(solution)/shard_map/ppermute | solution.py:27
  88.2 1.0 copy-start.6
  89.2 1.0 copy-start.16
  90.2 1.0 copy-start.18
  91.2 2.1 copy-start.14
  91.2 5.3 %copy-start.19 = (f32[3,4096]{1,0:T(4,128)S(1)}, f32[3,4096]{1,0:T(4,128)}, u32[]{:S(2)}) copy-start(f32[3,4096]{1,0:T(4,128)} %refs_5_.1) | copy-start | bytes 147460
  93.3 5.7 %copy-start.7 = (bf16[64,1536]{1,0:T(8,128)(2,1)}, bf16[64,1536]{1,0:T(8,128)(2,1)S(1)}, u32[]{:S(2)}) copy-start(bf16[64,1536]{1,0:T(8,128)(2,1)S(1)} %attend.2.refs_7_) | copy-start | bytes 589828
  99.0 14.2 %collective-permute-start.12 = (bf16[64,4224]{1,0:T(8,128)(2,1)S(1)}, bf16[64,4224]{1,0:T(8,128)(2,1)S(1)}, u32[]{:S(2)}, u32[]{:S(2)}) collective-permute-start(bf16[64,4224]{1,0:T(8,128)(2,1)S(1)} %get-tuple-element.14.refs_0_), channel_id=1, source_target_pairs={{0,4},{1,5},{4,8},{5,9},{8,12},{9,13},{12,14},{13,15},{14,10},{15,... | collective-permute-start | bytes 1622024 | tf_op jit(solution)/shard_map/ppermute | solution.py:27
  99.1 14.5 %collective-permute-start.11 = (bf16[64,4224]{1,0:T(8,128)(2,1)S(1)}, bf16[64,4224]{1,0:T(8,128)(2,1)S(1)}, u32[]{:S(2)}, u32[]{:S(2)}) collective-permute-start(bf16[64,4224]{1,0:T(8,128)(2,1)S(1)} %get-tuple-element.14.refs_0_), channel_id=1, source_target_pairs={{4,0},{5,1},{8,4},{9,5},{12,8},{13,9},{14,12},{15,13},{10,14},{11,... | collective-permute-start | bytes 1622024 | tf_op jit(solution)/shard_map/ppermute | solution.py:27
  101.1 0.8 copy-start.11
  113.3 13.3 %collective-permute-start.16 = (bf16[64,4224]{1,0:T(8,128)(2,1)S(1)}, bf16[64,4224]{1,0:T(8,128)(2,1)S(1)}, u32[]{:S(2)}, u32[]{:S(2)}) collective-permute-start(bf16[64,4224]{1,0:T(8,128)(2,1)S(1)} %collective-permute-done.12.refs_1_), channel_id=1, source_target_pairs={{0,4},{1,5},{4,8},{5,9},{8,12},{9,13},{12,14},{13,15},{14,10},{15,... | collective-permute-start | bytes 1622024 | tf_op jit(solution)/shard_map/ppermute | solution.py:27
  113.6 13.6 %collective-permute-start.15 = (bf16[64,4224]{1,0:T(8,128)(2,1)S(1)}, bf16[64,4224]{1,0:T(8,128)(2,1)S(1)}, u32[]{:S(2)}, u32[]{:S(2)}) collective-permute-start(bf16[64,4224]{1,0:T(8,128)(2,1)S(1)} %collective-permute-done.11.refs_0_), channel_id=1, source_target_pairs={{4,0},{5,1},{8,4},{9,5},{12,8},{13,9},{14,12},{15,13},{10,14},{11,... | collective-permute-start | bytes 1622024 | tf_op jit(solution)/shard_map/ppermute | solution.py:27
  126.6 12.5 %collective-permute-start.18 = (bf16[64,4224]{1,0:T(8,128)(2,1)S(1)}, bf16[64,4224]{1,0:T(8,128)(2,1)S(1)}, u32[]{:S(2)}, u32[]{:S(2)}) collective-permute-start(bf16[64,4224]{1,0:T(8,128)(2,1)S(1)} %collective-permute-done.16.refs_1_), channel_id=1, source_target_pairs={{0,4},{1,5},{4,8},{5,9},{8,12},{9,13},{12,14},{13,15},{14,10},{15,... | collective-permute-start | bytes 1622024 | tf_op jit(solution)/shard_map/ppermute | solution.py:27
  127.2 13.9 %copy-start.9 = (bf16[64,4224]{1,0:T(8,128)(2,1)}, bf16[64,4224]{1,0:T(8,128)(2,1)S(1)}, u32[]{:S(2)}) copy-start(bf16[64,4224]{1,0:T(8,128)(2,1)S(1)} %collective-permute-done.15.refs_0_) | copy-start | bytes 1622020
  127.2 13.9 %collective-permute-start.17 = (bf16[64,4224]{1,0:T(8,128)(2,1)S(1)}, bf16[64,4224]{1,0:T(8,128)(2,1)S(1)}, u32[]{:S(2)}, u32[]{:S(2)}) collective-permute-start(bf16[64,4224]{1,0:T(8,128)(2,1)S(1)} %collective-permute-done.15.refs_0_), channel_id=1, source_target_pairs={{4,0},{5,1},{8,4},{9,5},{12,8},{13,9},{14,12},{15,13},{10,14},{11,... | collective-permute-start | bytes 1622024 | tf_op jit(solution)/shard_map/ppermute | solution.py:27
  139.8 8.4 %collective-permute-start.19 = (bf16[32,4224]{1,0:T(8,128)(2,1)}, bf16[32,4224]{1,0:T(8,128)(2,1)S(1)}, u32[]{:S(2)}, u32[]{:S(2)}) collective-permute-start(bf16[32,4224]{1,0:T(8,128)(2,1)} %slice.60), channel_id=1, source_target_pairs={{0,4},{1,5},{4,8},{5,9},{8,12},{9,13},{12,14},{13,15},{14,10},{15,... | collective-permute-start | bytes 811016 | tf_op jit(solution)/shard_map/ppermute | solution.py:27
  141.8 7.2 %collective-permute-start.20 = (bf16[32,4224]{1,0:T(8,128)(2,1)}, bf16[32,4224]{1,0:T(8,128)(2,1)}, u32[]{:S(2)}, u32[]{:S(2)}) collective-permute-start(bf16[32,4224]{1,0:T(8,128)(2,1)} %slice.61), channel_id=1, source_target_pairs={{4,0},{5,1},{8,4},{9,5},{12,8},{13,9},{14,12},{15,13},{10,14},{11,... | collective-permute-start | bytes 811016 | tf_op jit(solution)/shard_map/ppermute | solution.py:27
  149.0 2.2 %copy-start = (bf16[4096,512]{1,0:T(8,128)(2,1)S(1)}, bf16[4096,512]{1,0:T(8,128)(2,1)}, u32[]{:S(2)}) copy-start(bf16[4096,512]{1,0:T(8,128)(2,1)} %refs_1_.1) | copy-start | bytes 12582916
  151.2 2.2 %copy-start.2 = (bf16[512,4096]{1,0:T(8,128)(2,1)S(1)}, bf16[512,4096]{1,0:T(8,128)(2,1)}, u32[]{:S(2)}) copy-start(bf16[512,4096]{1,0:T(8,128)(2,1)} %refs_3_.1) | copy-start | bytes 12582916
  159.6 17.7 %collective-permute-start.21 = (bf16[32,4096]{1,0:T(8,128)(2,1)S(1)}, bf16[32,4096]{1,0:T(8,128)(2,1)S(1)}, u32[]{:S(2)}, u32[]{:S(2)}) collective-permute-start(bf16[32,4096]{1,0:T(8,128)(2,1)S(1)} %get-tuple-element.21), channel_id=1, source_target_pairs={{0,4},{1,5},{4,8},{5,9},{8,12},{9,13},{12,14},{13,15},{14,10},{15,... | collective-permute-start | bytes 786440 | tf_op jit(solution)/shard_map/ppermute | solution.py:27
  161.1 5.8 %copy-start.10 = (bf16[64,4224]{1,0:T(8,128)(2,1)S(1)}, bf16[64,4224]{1,0:T(8,128)(2,1)}, u32[]{:S(2)}) copy-start(bf16[64,4224]{1,0:T(8,128)(2,1)} %copy-done.9) | copy-start | bytes 1622020
  161.1 17.9 %collective-permute-start.25 = (bf16[32,4096]{1,0:T(8,128)(2,1)S(1)}, bf16[32,4096]{1,0:T(8,128)(2,1)S(1)}, u32[]{:S(2)}, u32[]{:S(2)}) collective-permute-start(bf16[32,4096]{1,0:T(8,128)(2,1)S(1)} %get-tuple-element.22), channel_id=1, source_target_pairs={{4,0},{5,1},{8,4},{9,5},{12,8},{13,9},{14,12},{15,13},{10,14},{11,... | collective-permute-start | bytes 786440 | tf_op jit(solution)/shard_map/ppermute | solution.py:27
  177.4 27.4 %copy-start.3 = (bf16[512,4096]{1,0:T(8,128)(2,1)S(1)}, bf16[512,4096]{1,0:T(8,128)(2,1)}, u32[]{:S(2)}) copy-start(bf16[512,4096]{1,0:T(8,128)(2,1)} %refs_3_.1) | copy-start | bytes 12582916
  177.5 27.3 %copy-start.1 = (bf16[4096,512]{1,0:T(8,128)(2,1)S(1)}, bf16[4096,512]{1,0:T(8,128)(2,1)}, u32[]{:S(2)}) copy-start(bf16[4096,512]{1,0:T(8,128)(2,1)} %refs_1_.1) | copy-start | bytes 12582916
  177.5 27.3 %copy-start.12 = (bf16[64,4224]{1,0:T(8,128)(2,1)S(1)}, bf16[64,4224]{1,0:T(8,128)(2,1)}, u32[]{:S(2)}) copy-start(bf16[64,4224]{1,0:T(8,128)(2,1)} %copy-done.11) | copy-start | bytes 1622020
  177.5 12.0 %collective-permute-start.22 = (bf16[64,4096]{1,0:T(8,128)(2,1)S(1)}, bf16[64,4096]{1,0:T(8,128)(2,1)S(1)}, u32[]{:S(2)}, u32[]{:S(2)}) collective-permute-start(bf16[64,4096]{1,0:T(8,128)(2,1)S(1)} %pad_maximum_fusion.1), channel_id=1, source_target_pairs={{0,4},{1,5},{4,8},{5,9},{8,12},{9,13},{12,14},{13,15},{14,10},{15,... | collective-permute-start | bytes 1572872 | tf_op jit(solution)/shard_map/ppermute | solution.py:27
  179.1 11.5 %collective-permute-start.26 = (bf16[64,4096]{1,0:T(8,128)(2,1)S(1)}, bf16[64,4096]{1,0:T(8,128)(2,1)S(1)}, u32[]{:S(2)}, u32[]{:S(2)}) collective-permute-start(bf16[64,4096]{1,0:T(8,128)(2,1)S(1)} %pad_maximum_fusion.2), channel_id=1, source_target_pairs={{4,0},{5,1},{8,4},{9,5},{12,8},{13,9},{14,12},{15,13},{10,14},{11,... | collective-permute-start | bytes 1572872 | tf_op jit(solution)/shard_map/ppermute | solution.py:27
  189.6 12.0 %collective-permute-start.23 = (bf16[64,4096]{1,0:T(8,128)(2,1)S(1)}, bf16[64,4096]{1,0:T(8,128)(2,1)S(1)}, u32[]{:S(2)}, u32[]{:S(2)}) collective-permute-start(bf16[64,4096]{1,0:T(8,128)(2,1)S(1)} %add_convert_fusion.4), channel_id=1, source_target_pairs={{0,4},{1,5},{4,8},{5,9},{8,12},{9,13},{12,14},{13,15},{14,10},{15,... | collective-permute-start | bytes 1572872 | tf_op jit(solution)/shard_map/ppermute | solution.py:27
  190.7 12.0 %collective-permute-start.27 = (bf16[64,4096]{1,0:T(8,128)(2,1)S(1)}, bf16[64,4096]{1,0:T(8,128)(2,1)S(1)}, u32[]{:S(2)}, u32[]{:S(2)}) collective-permute-start(bf16[64,4096]{1,0:T(8,128)(2,1)S(1)} %add_convert_fusion.2), channel_id=1, source_target_pairs={{4,0},{5,1},{8,4},{9,5},{12,8},{13,9},{14,12},{15,13},{10,14},{11,... | collective-permute-start | bytes 1572872 | tf_op jit(solution)/shard_map/ppermute | solution.py:27
  201.7 9.8 %collective-permute-start.24 = (bf16[64,4096]{1,0:T(8,128)(2,1)S(1)}, bf16[64,4096]{1,0:T(8,128)(2,1)S(1)}, u32[]{:S(2)}, u32[]{:S(2)}) collective-permute-start(bf16[64,4096]{1,0:T(8,128)(2,1)S(1)} %add_convert_fusion.3), channel_id=1, source_target_pairs={{0,4},{1,5},{4,8},{5,9},{8,12},{9,13},{12,14},{13,15},{14,10},{15,... | collective-permute-start | bytes 1572872 | tf_op jit(solution)/shard_map/ppermute | solution.py:27
  202.8 9.7 %collective-permute-start.28 = (bf16[64,4096]{1,0:T(8,128)(2,1)S(1)}, bf16[64,4096]{1,0:T(8,128)(2,1)S(1)}, u32[]{:S(2)}, u32[]{:S(2)}) collective-permute-start(bf16[64,4096]{1,0:T(8,128)(2,1)S(1)} %add_convert_fusion.1), channel_id=1, source_target_pairs={{4,0},{5,1},{8,4},{9,5},{12,8},{13,9},{14,12},{15,13},{10,14},{11,... | collective-permute-start | bytes 1572872 | tf_op jit(solution)/shard_map/ppermute | solution.py:27
  204.8 7.7 %copy-start.8 = (bf16[64,1536]{1,0:T(8,128)(2,1)S(1)}, bf16[64,1536]{1,0:T(8,128)(2,1)}, u32[]{:S(2)}) copy-start(bf16[64,1536]{1,0:T(8,128)(2,1)} %copy-done.7) | copy-start | bytes 589828
  (3 other events, 2.3 us)

commit v3 on v2

--- a/solution.py
+++ b/solution.py
@@ -15,7 +15,7 @@
 CORES = 2
 EPSILON = 1e-06
 MASKED = -1e30
-HEADS = (12, 14, 6)
+HEADS = (12, 12, 8)
 HEAD_GROUP = 4
 HIDDEN_STEP = 512
 LANES = 128
@@ -63,8 +63,8 @@
     rest = refs[sources - 1 :]
     if last:
         modulation_ref, meta_ref = rest[:2]
-        before = rest[2:-2]
-        out_ref, normed_ref = rest[-2:]
+        before = rest[2:-3]
+        out_ref, upper_ref, lower_ref = rest[-3:]
     else:
         (out_ref,) = rest
     rows = q_ref.shape[0]
@@ -110,15 +110,18 @@
         center = sum(jnp.sum(w, axis=-1, keepdims=True) for w in wide) / count
         spread = sum(jnp.sum(jnp.square(w - center), axis=-1, keepdims=True) for w in wide) / count
         factor = lax.rsqrt(spread + EPSILON)
-        done = 0
+        done, half = 0, rows // 2
         for w in wide:
             cols = slice(done, done + w.shape[1])
             done += w.shape[1]
-            normed_ref[:, cols] = (
+            normed = (
                 (w - center) * factor * (1.0 + modulation_ref[1:2, cols])
                 + modulation_ref[0:1, cols]
             ).astype(jnp.bfloat16)
-        normed_ref[:, count:] = meta_ref[...]
+            upper_ref[:, cols] = normed[:half]
+            lower_ref[:, cols] = normed[half:]
+        upper_ref[:, count:] = meta_ref[:half]
+        lower_ref[:, count:] = meta_ref[half:]
 
 
 def attend_chunk(start, part, flags, queries, key_rows, values, around, before, extra):
@@ -129,7 +132,7 @@
     out_shape = [jax.ShapeDtypeStruct((rows, part), jnp.bfloat16)]
     if last:
         operands += extra + before
-        out_shape.append(jax.ShapeDtypeStruct((rows, width + LANES), jnp.bfloat16))
+        out_shape += [jax.ShapeDtypeStruct((rows // 2, width + LANES), jnp.bfloat16)] * 2
     resident = pl.BlockSpec(memory_space=pltpu.VMEM)
     return pl.pallas_call(
         functools.partial(attention_kernel, start, part // HEAD_DIM, sources, last),
@@ -160,22 +163,20 @@
     return gate / 1024.0
 
 
-def experts_kernel(blocks, pieces, mine_ref, *refs):
+def experts_kernel(pieces, mine_ref, *refs):
     inputs = refs[:pieces]
     in_a, in_b, out_a, out_b = refs[pieces : pieces + 4]
-    outs = refs[pieces + 4 : pieces + 4 + blocks]
-    x_ref, total_ref, first_ref, second_ref, first_sem, second_sem = refs[pieces + 4 + blocks :]
+    outs = refs[pieces + 4 : 2 * pieces + 4]
+    x_ref, total_ref, first_ref, second_ref, first_sem, second_sem = refs[2 * pieces + 4 :]
     steps, width, step = first_ref.shape
     for j in range(steps):
         source_in, source_out = (in_a, out_a) if j < steps // 2 else (in_b, out_b)
         span = pl.ds(j % (steps // 2) * step, step)
         pltpu.make_async_copy(source_in.at[:, span], first_ref.at[j], first_sem.at[j]).start()
         pltpu.make_async_copy(source_out.at[span], second_ref.at[j], second_sem.at[j]).start()
-    start = 0
-    for ref in inputs:
-        x_ref[start : start + ref.shape[0], :] = ref[...]
-        start += ref.shape[0]
-    rows = start // blocks
+    rows = inputs[0].shape[0]
+    for i, ref in enumerate(inputs):
+        x_ref[i * rows : (i + 1) * rows, :] = ref[...]
     total_ref[...] = jnp.zeros_like(total_ref)
 
     def body(j, carry):
@@ -195,18 +196,17 @@
         out[...] = (total_ref[here, :] * gate).astype(jnp.bfloat16)
 
 
-def run_experts(blocks, weights, mine):
-    rows = sum(x.shape[0] for x in blocks[0])
-    flat = [x for block in blocks for x in block]
+def run_experts(flat, weights, mine):
+    rows = flat[0].shape[0]
     width = weights[0].shape[0]
-    count = len(blocks)
+    count = len(flat)
     hidden = sum(w.shape[1] for w in weights[:2])
     step = min(HIDDEN_STEP, weights[0].shape[1])
     steps = hidden // step
     resident = pl.BlockSpec(memory_space=pltpu.VMEM)
     remote = pl.BlockSpec(memory_space=pl.ANY)
     return pl.pallas_call(
-        functools.partial(experts_kernel, count, len(flat)),
+        functools.partial(experts_kernel, count),
         out_shape=[jax.ShapeDtypeStruct((rows, width), jnp.bfloat16)] * count,
         in_specs=[pl.BlockSpec(memory_space=pltpu.SMEM)] + [resident] * len(flat) + [remote] * 4,
         out_specs=[resident] * count,
@@ -228,6 +228,35 @@
     )(mine, *flat, *weights)
 
 
+def combine_kernel(parts, modulation_ref, *refs):
+    attended = refs[:parts]
+    upper = refs[parts : parts + 3]
+    lower = refs[parts + 3 : parts + 6]
+    out_ref = refs[-1]
+    half = upper[0].shape[0]
+    start = 0
+    for ref in attended:
+        cols = slice(start, start + ref.shape[1])
+        start += ref.shape[1]
+        for here, shares in ((slice(0, half), upper), (slice(half, 2 * half), lower)):
+            mixture = sum(share[:, cols].astype(jnp.float32) for share in shares)
+            own = ref[here, :].astype(jnp.float32)
+            out_ref[here, cols] = (own + modulation_ref[2:3, cols] * mixture).astype(jnp.bfloat16)
+
+
+def combine(attended, modulation, upper, lower):
+    shape = (2 * upper[0].shape[0], upper[0].shape[1])
+    resident = pl.BlockSpec(memory_space=pltpu.VMEM)
+    return pl.pallas_call(
+        functools.partial(combine_kernel, len(attended)),
+        out_shape=jax.ShapeDtypeStruct(shape, jnp.bfloat16),
+        in_specs=[resident] * (1 + len(attended) + 6),
+        out_specs=resident,
+        compiler_params=pltpu.CompilerParams(vmem_limit_bytes=ATTEND_VMEM),
+        name="combine",
+    )(modulation, *attended, *upper, *lower)
+
+
 def ring_order(chips, grid_rows):
     if grid_rows == 2:
         return list(range(0, chips, 2)) + list(range(chips - 1, 0, -2))
@@ -235,7 +264,7 @@
 
 
 def block(queries, key_rows, values, modulation, expert_in, expert_out, routes, gate_fixed):
-    rows, width = queries.shape
+    _, width = queries.shape
     devices = lax.axis_size("tile")
     position = lax.axis_index("tile")
     grid_rows = devices // TILE_COLS
@@ -281,7 +310,7 @@
             [modulation, lanes] if last else [],
         )
         attended = attended + [got[0]]
-    normed = got[1]
+    upper, lower = got[1:]
 
     chips = devices // CORES
     order = ring_order(chips, grid_rows)
@@ -291,42 +320,54 @@
         for k in range(CORES)
     ]
     backward = [(b, a) for a, b in forward]
-    half = rows // 2
     far = chips // 2
-    upper, lower = slice(0, half), slice(half, rows)
-    ahead, behind = [normed], [normed]
-    for _ in range(1, far):
-        behind.append(permute(behind[-1], forward))
-        ahead.append(permute(ahead[-1], backward))
-    far_upper = permute(behind[-1][upper], forward)
-    far_lower = permute(ahead[-1][lower], backward)
-
     mine = (position // SPLIT).astype(jnp.int32).reshape(1)
-
-    def share(shifts, blocks):
-        return dict(zip(shifts, run_experts(blocks, weights, mine)))
-
-    partial = share([0], [[normed]])
-    for s in range(1, far):
-        partial.update(share([s, -s], [[ahead[s]], [behind[s]]]))
-    partial.update(share([far], [[far_upper, far_lower]]))
-
-    wide = lambda a: a.astype(jnp.float32)
-    add = lambda a, b: (wide(a) + wide(b)).astype(jnp.bfloat16)
-    up = permute(partial[far][upper], forward)
-    down = permute(partial[far][lower], backward)
-    for s in range(far - 1, 0, -1):
-        up_sum, down_sum = partial[s], partial[-s]
-        if s == far - 1:
-            up_sum = jnp.concatenate([add(up_sum[upper], up), up_sum[lower]], axis=0)
-            down_sum = jnp.concatenate([down_sum[upper], add(down_sum[lower], down)], axis=0)
-        else:
-            up_sum, down_sum = add(up_sum, up), add(down_sum, down)
-        up = permute(up_sum, forward)
-        down = permute(down_sum, backward)
-    mixture = wide(up) + wide(down) + wide(partial[0])
-    attended = wide(jnp.concatenate(attended, axis=1))
-    return (attended + modulation[2] * mixture).astype(jnp.bfloat16)
+    add = lambda a, b: (a.astype(jnp.float32) + b.astype(jnp.float32)).astype(jnp.bfloat16)
+
+    rows_of = {("upper", 0): upper, ("lower", 0): lower}
+    for s in range(1, far + 1):
+        for kind, half, sign, pairs in (
+            ("long", "upper", -1, forward),
+            ("long", "lower", 1, backward),
+            ("short", "lower", -1, forward),
+            ("short", "upper", 1, backward),
+        ):
+            if kind == "long" or s < far:
+                rows_of[half, sign * s] = permute(rows_of[half, sign * (s - 1)], pairs)
+
+    partial = {}
+
+    def share(keys):
+        partial.update(zip(keys, run_experts([rows_of[k] for k in keys], weights, mine)))
+
+    for s in range(1, far + 1):
+        keys = [("upper", -s), ("lower", s)]
+        if s == 1:
+            keys += [("upper", 0), ("lower", 0)]
+        elif s < far:
+            keys += [("lower", -(s - 1)), ("upper", s - 1)]
+        share(keys)
+    share([("lower", 1 - far), ("upper", far - 1)])
+
+    def reduce_chain(kind, half, sign, pairs):
+        hops = far if kind == "long" else far - 1
+        x = partial[half, -sign * hops if kind == "long" else sign * hops]
+        for s in range(hops, 0, -1):
+            x = permute(x, pairs)
+            if s > 1:
+                x = add(x, partial[half, sign * (s - 1)])
+        return x
+
+    long_f = reduce_chain("long", "upper", 1, forward)
+    long_b = reduce_chain("long", "lower", -1, backward)
+    short_f = reduce_chain("short", "lower", 1, forward)
+    short_b = reduce_chain("short", "upper", -1, backward)
+    return combine(
+        attended,
+        modulation,
+        [long_f, short_b, partial["upper", 0]],
+        [long_b, short_f, partial["lower", 0]],
+    )
 
 
 def solution(mesh):

time: 214 us -> 227 us (1.061)
  starting transfers between devices: 54.8 us -> 68.9 us
    ppermute x29 -> x41, starting transfers between devices: 54.8 us -> 68.9 us  [permute(): return lax.ppermute(x, 'tile', pairs)]
    slice x6 -> x0, local copies, waits for them, and re-layouts: 2.39 us -> none  [the longest x1 0.86 us: block(): return (attended + modulation[2] * mixture).astype(jnp.bfloat16)]
    unnamed x44 -> x50, local copies, waits for them, and re-layouts: 10.5 us -> 12.8 us
    pallas_call x5 -> x6, Pallas kernels: 26.9 us -> 28.3 us  [the longest x5 27.2 us: run_experts(): pl.pallas_call(functools.partial(experts_kernel, count), out_shape=[jax.S...]
    ppermute x29 -> x41, waiting for transfers between devices: 104 us -> 105 us  [permute(): return lax.ppermute(x, 'tile', pairs)]
  transfers between devices with their start and end apart: 29 -> 41, of which waited for: 16 -> 22; matrix products, arithmetic and copies ran while one was open for 3% -> 1% of each run, Pallas kernels for 13% -> 15%
where the time goes in v3:
time: 227 us; the launch traced here: 226 us
  waiting for transfers between devices  105 us (46%)
  starting transfers between devices  68.9 us (30%)
  Pallas kernels  35.6 us (16%)
  local copies, waits for them, and re-layouts  15.2 us (7%)
    ppermute x41, waiting for transfers between devices, permute(): return lax.ppermute(x, 'tile', pairs)  105 us
    ppermute x41, starting transfers between devices, permute(): return lax.ppermute(x, 'tile', pairs)  68.9 us
    pallas_call x5, Pallas kernels, run_experts(): pl.pallas_call(functools.partial(experts_kernel, count), out_shape=[jax.S...  27.2 us
    unnamed x50, local copies, waits for them, and re-layouts  12.8 us
    pallas_call x3, Pallas kernels, attend_chunk(): pl.pallas_call(functools.partial(attention_kernel, start, part // HEAD_DI...  7.36 us
  transfers between devices with their start and end apart: 41, of which 22 were waited for; matrix products, arithmetic and copies ran while one was open for 1% of the time, Pallas kernels for 15%

profile of v3, /device:TPU:0, one launch (start us, length us, event | category | flops | bytes accessed | tf_op | source)
XLA Modules:
  0.0 226.3 jit_solution(16270656615490747728)
XLA Ops:
  2.0 4.1 %collective-permute-start.2 = (bf16[2,64,1536]{2,1,0:T(8,128)(2,1)S(1)}, bf16[2,64,1536]{2,1,0:T(8,128)(2,1)S(1)}, u32[]{:S(2)}, u32[]{:S(2)}) collective-permute-start(bf16[2,64,1536]{2,1,0:T(8,128)(2,1)S(1)} %pad_maximum_fusion.1), channel_id=1, source_target_pairs={{12,4},{13,5},{14,6},{15,7},{0,8},{1,9},{2,10},{3,11},{4,12},{5,13... | collective-permute-start | bytes 1179656 | tf_op jit(solution)/shard_map/ppermute | solution.py:27
  7.2 3.0 %collective-permute-start.8 = (bf16[2,64,1024]{2,1,0:T(8,128)(2,1)S(1)}, bf16[2,64,1024]{2,1,0:T(8,128)(2,1)}, u32[]{:S(2)}, u32[]{:S(2)}) collective-permute-start(bf16[2,64,1024]{2,1,0:T(8,128)(2,1)S(1)} %pad_maximum_fusion.3), channel_id=1, source_target_pairs={{12,4},{13,5},{14,6},{15,7},{0,8},{1,9},{2,10},{3,11},{4,12},{5,13... | collective-permute-start | bytes 786440 | tf_op jit(solution)/shard_map/ppermute | solution.py:27
  10.2 28.3 %collective-permute-done.2.refs_2_ = bf16[2,64,1536]{2,1,0:T(8,128)(2,1)S(1)} collective-permute-done((bf16[2,64,1536]{2,1,0:T(8,128)(2,1)S(1)}, bf16[2,64,1536]{2,1,0:T(8,128)(2,1)S(1)}, u32[]{:S(2)}, u32[]{:S(2)}) %collective-permute-start.2) | collective-permute-done | bytes 393248 | tf_op jit(solution)/shard_map/ppermute | solution.py:27
  38.6 13.4 %collective-permute-done.8.refs_2_ = bf16[2,64,1024]{2,1,0:T(8,128)(2,1)} collective-permute-done((bf16[2,64,1024]{2,1,0:T(8,128)(2,1)S(1)}, bf16[2,64,1024]{2,1,0:T(8,128)(2,1)}, u32[]{:S(2)}, u32[]{:S(2)}) %collective-permute-start.8) | collective-permute-done | bytes 262176 | tf_op jit(solution)/shard_map/ppermute | solution.py:27
  52.0 3.6 %collective-permute-start.1 = (bf16[2,64,4096]{2,1,0:T(8,128)(2,1)S(1)}, bf16[2,64,4096]{2,1,0:T(8,128)(2,1)S(1)}, u32[]{:S(2)}, u32[]{:S(2)}) collective-permute-start(bf16[2,64,4096]{2,1,0:T(8,128)(2,1)S(1)} %pad_maximum_fusion), channel_id=1, source_target_pairs={{14,13},{13,14},{8,15},{7,0},{2,1},{1,2},{6,5},{5,6},{0,7},{15,8},... | collective-permute-start | bytes 3145736 | tf_op jit(solution)/shard_map/ppermute | solution.py:27
  56.4 2.9 %collective-permute-start.4 = (bf16[2,64,1536]{2,1,0:T(8,128)(2,1)S(1)}, bf16[2,64,1536]{2,1,0:T(8,128)(2,1)S(1)}, u32[]{:S(2)}, u32[]{:S(2)}) collective-permute-start(bf16[2,64,1536]{2,1,0:T(8,128)(2,1)S(1)} %collective-permute-done.2.refs_2_), channel_id=1, source_target_pairs={{14,13},{13,14},{8,15},{7,0},{2,1},{1,2},{6,5},{5,6},{0,7},{15,8},... | collective-permute-start | bytes 1179656 | tf_op jit(solution)/shard_map/ppermute | solution.py:27
  59.3 14.1 %collective-permute-done.4.refs_4_ = bf16[2,64,1536]{2,1,0:T(8,128)(2,1)S(1)} collective-permute-done((bf16[2,64,1536]{2,1,0:T(8,128)(2,1)S(1)}, bf16[2,64,1536]{2,1,0:T(8,128)(2,1)S(1)}, u32[]{:S(2)}, u32[]{:S(2)}) %collective-permute-start.4) | collective-permute-done | bytes 393248 | tf_op jit(solution)/shard_map/ppermute | solution.py:27
  74.1 15.0 %collective-permute-start.6 = (bf16[2,64,1536]{2,1,0:T(8,128)(2,1)}, bf16[2,64,1536]{2,1,0:T(8,128)(2,1)S(1)}, u32[]{:S(2)}, u32[]{:S(2)}) collective-permute-start(bf16[2,64,1536]{2,1,0:T(8,128)(2,1)} %collective-permute-done.5.refs_2_), channel_id=1, source_target_pairs={{0,1},{1,0},{2,3},{3,2},{4,5},{5,4},{6,7},{7,6},{8,9},{9,8},{10,11... | collective-permute-start | bytes 1179656 | tf_op jit(solution)/shard_map/ppermute | solution.py:27
  91.8 3.1 %collective-permute-start.10 = (bf16[2,64,1024]{2,1,0:T(8,128)(2,1)}, bf16[2,64,1024]{2,1,0:T(8,128)(2,1)}, u32[]{:S(2)}, u32[]{:S(2)}) collective-permute-start(bf16[2,64,1024]{2,1,0:T(8,128)(2,1)} %collective-permute-done.8.refs_2_), channel_id=1, source_target_pairs={{14,13},{13,14},{8,15},{7,0},{2,1},{1,2},{6,5},{5,6},{0,7},{15,8},... | collective-permute-start | bytes 786440 | tf_op jit(solution)/shard_map/ppermute | solution.py:27
  94.9 3.3 %collective-permute-start.7 = (bf16[2,64,1536]{2,1,0:T(8,128)(2,1)}, bf16[2,64,1536]{2,1,0:T(8,128)(2,1)}, u32[]{:S(2)}, u32[]{:S(2)}) collective-permute-start(bf16[2,64,1536]{2,1,0:T(8,128)(2,1)} %collective-permute-done.5.refs_2_), channel_id=1, source_target_pairs={{14,13},{13,14},{8,15},{7,0},{2,1},{1,2},{6,5},{5,6},{0,7},{15,8},... | collective-permute-start | bytes 1179656 | tf_op jit(solution)/shard_map/ppermute | solution.py:27
  102.6 2.1 attend.2.refs_7_.refs_0_
  105.2 2.7 %attend.3.refs_8_.refs_1_ = bf16[64,1536]{1,0:T(8,128)(2,1)S(1)} custom-call(s32[6]{0:T(128)S(1)} %add_convert_fusion.10.flags_ref, bf16[64,4096]{1,0:T(8,128)(2,1)S(1)} %copy-done.6, bf16[64,4096]{1,0:T(8,128)(2,1)S(1)} %copy-done.4, bf16[64,4096]{1,0:T(8,128)(2,1)S(1)} %copy-done.5, bf16[2,64,4096]{2,1,0:T(8,128)(2,1)S(1)} %collective-permute-done.refs_0_, ...), custom_call_target="tpu_custom_call" | custom-call | flops 150994944 | bytes 2752512 | tf_op jit(solution)/shard_map/attend/pallas_call | solution.py:137
  107.9 2.6 %attend_last.1 = (bf16[64,1024]{1,0:T(8,128)(2,1)S(1)}, bf16[32,4224]{1,0:T(8,128)(2,1)S(1)}, bf16[32,4224]{1,0:T(8,128)(2,1)S(1)}) custom-call(s32[6]{0:T(128)S(1)} %add_convert_fusion.10.flags_ref, bf16[64,4096]{1,0:T(8,128)(2,1)S(1)} %copy-done.6, bf16[64,4096]{1,0:T(8,128)(2,1)S(1)} %copy-done.4, bf16[64,4096]{1,0:T(8,128)(2,1)S(1)} %copy-done.5, ...), custom_call_target="tpu_custom_call" | custom-call | flops 100663296 | bytes 1835008 | tf_op jit(solution)/shard_map/attend_last/pallas_call | solution.py:137
  111.2 5.6 %collective-permute-start.15 = (bf16[32,4224]{1,0:T(8,128)(2,1)S(1)}, bf16[32,4224]{1,0:T(8,128)(2,1)S(1)}, u32[]{:S(2)}, u32[]{:S(2)}) collective-permute-start(bf16[32,4224]{1,0:T(8,128)(2,1)S(1)} %get-tuple-element.26.refs_3_), channel_id=1, source_target_pairs={{4,0},{5,1},{8,4},{9,5},{12,8},{13,9},{14,12},{15,13},{10,14},{11,... | collective-permute-start | bytes 811016 | tf_op jit(solution)/shard_map/ppermute | solution.py:27
  117.6 5.3 %collective-permute-done.11.refs_0_ = bf16[32,4224]{1,0:T(8,128)(2,1)S(1)} collective-permute-done((bf16[32,4224]{1,0:T(8,128)(2,1)S(1)}, bf16[32,4224]{1,0:T(8,128)(2,1)S(1)}, u32[]{:S(2)}, u32[]{:S(2)}) %collective-permute-start.11) | collective-permute-done | bytes 270368 | tf_op jit(solution)/shard_map/ppermute | solution.py:27
  122.8 2.3 %collective-permute-start.25 = (bf16[32,4224]{1,0:T(8,128)(2,1)S(1)}, bf16[32,4224]{1,0:T(8,128)(2,1)S(1)}, u32[]{:S(2)}, u32[]{:S(2)}) collective-permute-start(bf16[32,4224]{1,0:T(8,128)(2,1)S(1)} %get-tuple-element.25.refs_2_), channel_id=1, source_target_pairs={{4,0},{5,1},{8,4},{9,5},{12,8},{13,9},{14,12},{15,13},{10,14},{11,... | collective-permute-start | bytes 811016 | tf_op jit(solution)/shard_map/ppermute | solution.py:27
  125.8 2.8 %collective-permute-done.22.refs_2_ = bf16[32,4224]{1,0:T(8,128)(2,1)S(1)} collective-permute-done((bf16[32,4224]{1,0:T(8,128)(2,1)S(1)}, bf16[32,4224]{1,0:T(8,128)(2,1)S(1)}, u32[]{:S(2)}, u32[]{:S(2)}) %collective-permute-start.22) | collective-permute-done | bytes 270368 | tf_op jit(solution)/shard_map/ppermute | solution.py:27
  129.3 2.7 %collective-permute-done.25.refs_3_ = bf16[32,4224]{1,0:T(8,128)(2,1)S(1)} collective-permute-done((bf16[32,4224]{1,0:T(8,128)(2,1)S(1)}, bf16[32,4224]{1,0:T(8,128)(2,1)S(1)}, u32[]{:S(2)}, u32[]{:S(2)}) %collective-permute-start.25) | collective-permute-done | bytes 270368 | tf_op jit(solution)/shard_map/ppermute | solution.py:27
  132.0 3.2 %collective-permute-done.12.refs_0_ = bf16[32,4224]{1,0:T(8,128)(2,1)S(1)} collective-permute-done((bf16[32,4224]{1,0:T(8,128)(2,1)S(1)}, bf16[32,4224]{1,0:T(8,128)(2,1)S(1)}, u32[]{:S(2)}, u32[]{:S(2)}) %collective-permute-start.12) | collective-permute-done | bytes 270368 | tf_op jit(solution)/shard_map/ppermute | solution.py:27
  135.8 1.8 collective-permute-done.16.refs_1_
  137.6 2.5 %collective-permute-start.17 = (bf16[32,4224]{1,0:T(8,128)(2,1)S(1)}, bf16[32,4224]{1,0:T(8,128)(2,1)S(1)}, u32[]{:S(2)}, u32[]{:S(2)}) collective-permute-start(bf16[32,4224]{1,0:T(8,128)(2,1)S(1)} %collective-permute-done.16.refs_1_), channel_id=1, source_target_pairs={{4,0},{5,1},{8,4},{9,5},{12,8},{13,9},{14,12},{15,13},{10,14},{11,... | collective-permute-start | bytes 811016 | tf_op jit(solution)/shard_map/ppermute | solution.py:27
  140.1 1.7 collective-permute-done.23.refs_2_
  141.8 2.0 collective-permute-start.26
  143.8 3.5 %collective-permute-done.13.refs_0_ = bf16[32,4224]{1,0:T(8,128)(2,1)S(1)} collective-permute-done((bf16[32,4224]{1,0:T(8,128)(2,1)S(1)}, bf16[32,4224]{1,0:T(8,128)(2,1)S(1)}, u32[]{:S(2)}, u32[]{:S(2)}) %collective-permute-start.13) | collective-permute-done | bytes 270368 | tf_op jit(solution)/shard_map/ppermute | solution.py:27
  147.4 2.1 collective-permute-start.18
  149.4 3.3 %collective-permute-done.26.refs_3_ = bf16[32,4224]{1,0:T(8,128)(2,1)S(1)} collective-permute-done((bf16[32,4224]{1,0:T(8,128)(2,1)S(1)}, bf16[32,4224]{1,0:T(8,128)(2,1)S(1)}, u32[]{:S(2)}, u32[]{:S(2)}) %collective-permute-start.26) | collective-permute-done | bytes 270368 | tf_op jit(solution)/shard_map/ppermute | solution.py:27
  152.8 1.7 collective-permute-start.24
  154.4 2.2 collective-permute-done.14.refs_0_
  156.6 2.0 collective-permute-done.18.refs_1_
  158.7 2.2 copy-done
  160.9 2.2 copy-done.2
  163.0 6.2 %experts.5 = (bf16[32,4096]{1,0:T(8,128)(2,1)S(1)}, bf16[32,4096]{1,0:T(8,128)(2,1)S(1)}) custom-call(s32[1]{0:T(128)} %bitcast.9.mine_ref, bf16[32,4224]{1,0:T(8,128)(2,1)S(1)} %collective-permute-done.14.refs_0_, bf16[32,4224]{1,0:T(8,128)(2,1)} %collective-permute-done.18.refs_1_, bf16[4096,512]{1,0:T(8,128)(2,1)S(1)} %copy-done, ...), custom_call_target="tpu_custom_call" | custom-call | flops 1073741824 | bytes 16777216 | tf_op jit(solution)/shard_map/experts/pallas_call | solution.py:208
  169.3 5.5 %experts.7 = (bf16[32,4096]{1,0:T(8,128)(2,1)S(1)}, bf16[32,4096]{1,0:T(8,128)(2,1)S(1)}, bf16[32,4096]{1,0:T(8,128)(2,1)S(1)}, bf16[32,4096]{1,0:T(8,128)(2,1)S(1)}) custom-call(s32[1]{0:T(128)} %bitcast.9.mine_ref, bf16[32,4224]{1,0:T(8,128)(2,1)S(1)} %collective-permute-done.13.refs_0_, bf16[32,4224]{1,0:T(8,128)(2,1)S(1)} %collective-permute-done.17.refs_1_, ...), custom_call_target="tpu_custom_call" | custom-call | flops 2147483648 | bytes 16777216 | tf_op jit(solution)/shard_map/experts/pallas_call | solution.py:208
  174.8 2.5 %collective-permute-start.31 = (bf16[32,4096]{1,0:T(8,128)(2,1)S(1)}, bf16[32,4096]{1,0:T(8,128)(2,1)S(1)}, u32[]{:S(2)}, u32[]{:S(2)}) collective-permute-start(bf16[32,4096]{1,0:T(8,128)(2,1)S(1)} %get-tuple-element.31), channel_id=1, source_target_pairs={{4,0},{5,1},{8,4},{9,5},{12,8},{13,9},{14,12},{15,13},{10,14},{11,... | collective-permute-start | bytes 786440 | tf_op jit(solution)/shard_map/ppermute | solution.py:27
  177.3 1.7 collective-permute-start.34
  179.0 5.2 %experts.8 = (bf16[32,4096]{1,0:T(8,128)(2,1)S(1)}, bf16[32,4096]{1,0:T(8,128)(2,1)S(1)}, bf16[32,4096]{1,0:T(8,128)(2,1)S(1)}, bf16[32,4096]{1,0:T(8,128)(2,1)S(1)}) custom-call(s32[1]{0:T(128)} %bitcast.9.mine_ref, bf16[32,4224]{1,0:T(8,128)(2,1)S(1)} %collective-permute-done.12.refs_0_, bf16[32,4224]{1,0:T(8,128)(2,1)S(1)} %collective-permute-done.16.refs_1_, ...), custom_call_target="tpu_custom_call" | custom-call | flops 2147483648 | bytes 16777216 | tf_op jit(solution)/shard_map/experts/pallas_call | solution.py:208
  184.8 5.2 %experts.6 = (bf16[32,4096]{1,0:T(8,128)(2,1)S(1)}, bf16[32,4096]{1,0:T(8,128)(2,1)S(1)}) custom-call(s32[1]{0:T(128)} %bitcast.9.mine_ref, bf16[32,4224]{1,0:T(8,128)(2,1)S(1)} %collective-permute-done.24.refs_0_, bf16[32,4224]{1,0:T(8,128)(2,1)S(1)} %collective-permute-done.27.refs_1_, bf16[4096,512]{1,0:T(8,128)(2,1)S(1)} %copy-done.1, ...), custom_call_target="tpu_custom_call" | custom-call | flops 1073741824 | bytes 16777216 | tf_op jit(solution)/shard_map/experts/pallas_call | solution.py:208
  190.0 5.2 %experts.9 = (bf16[32,4096]{1,0:T(8,128)(2,1)S(1)}, bf16[32,4096]{1,0:T(8,128)(2,1)S(1)}, bf16[32,4096]{1,0:T(8,128)(2,1)S(1)}, bf16[32,4096]{1,0:T(8,128)(2,1)S(1)}) custom-call(s32[1]{0:T(128)} %bitcast.9.mine_ref, bf16[32,4224]{1,0:T(8,128)(2,1)S(1)} %collective-permute-done.11.refs_0_, bf16[32,4224]{1,0:T(8,128)(2,1)S(1)} %collective-permute-done.15.refs_1_, ...), custom_call_target="tpu_custom_call" | custom-call | flops 2147483648 | bytes 16777216 | tf_op jit(solution)/shard_map/experts/pallas_call | solution.py:208
  195.5 2.1 collective-permute-start.32
  197.6 1.8 collective-permute-start.35
  199.8 4.8 %collective-permute-done.28 = bf16[32,4096]{1,0:T(8,128)(2,1)S(1)} collective-permute-done((bf16[32,4096]{1,0:T(8,128)(2,1)S(1)}, bf16[32,4096]{1,0:T(8,128)(2,1)S(1)}, u32[]{:S(2)}, u32[]{:S(2)}) %collective-permute-start.28) | collective-permute-done | bytes 262176 | tf_op jit(solution)/shard_map/ppermute | solution.py:27
  204.8 2.1 collective-permute-start.33
  206.8 3.5 %collective-permute-done.35 = bf16[32,4096]{1,0:T(8,128)(2,1)S(1)} collective-permute-done((bf16[32,4096]{1,0:T(8,128)(2,1)S(1)}, bf16[32,4096]{1,0:T(8,128)(2,1)S(1)}, u32[]{:S(2)}, u32[]{:S(2)}) %collective-permute-start.35) | collective-permute-done | bytes 262176 | tf_op jit(solution)/shard_map/ppermute | solution.py:27
  210.4 2.0 collective-permute-start.36
  212.6 3.2 %collective-permute-done.29 = bf16[32,4096]{1,0:T(8,128)(2,1)S(1)} collective-permute-done((bf16[32,4096]{1,0:T(8,128)(2,1)S(1)}, bf16[32,4096]{1,0:T(8,128)(2,1)S(1)}, u32[]{:S(2)}, u32[]{:S(2)}) %collective-permute-start.29) | collective-permute-done | bytes 262176 | tf_op jit(solution)/shard_map/ppermute | solution.py:27
  215.9 2.8 %collective-permute-done.36 = bf16[32,4096]{1,0:T(8,128)(2,1)S(1)} collective-permute-done((bf16[32,4096]{1,0:T(8,128)(2,1)S(1)}, bf16[32,4096]{1,0:T(8,128)(2,1)S(1)}, u32[]{:S(2)}, u32[]{:S(2)}) %collective-permute-start.36) | collective-permute-done | bytes 262176 | tf_op jit(solution)/shard_map/ppermute | solution.py:27
  218.8 2.0 collective-permute-start.37
  221.2 2.8 %collective-permute-done.30.refs_3_ = bf16[32,4096]{1,0:T(8,128)(2,1)S(1)} collective-permute-done((bf16[32,4096]{1,0:T(8,128)(2,1)S(1)}, bf16[32,4096]{1,0:T(8,128)(2,1)S(1)}, u32[]{:S(2)}, u32[]{:S(2)}) %collective-permute-start.30) | collective-permute-done | bytes 262176 | tf_op jit(solution)/shard_map/ppermute | solution.py:27
  (116 shorter events, 20.2 us)
Async XLA Ops:
  0.0 38.5 %copy-start.4 = (bf16[64,4096]{1,0:T(8,128)(2,1)S(1)}, bf16[64,4096]{1,0:T(8,128)(2,1)}, u32[]{:S(2)}) copy-start(bf16[64,4096]{1,0:T(8,128)(2,1)} %k_ref.5) | copy-start | bytes 1572868
  0.0 38.5 %copy-start.5 = (bf16[64,4096]{1,0:T(8,128)(2,1)S(1)}, bf16[64,4096]{1,0:T(8,128)(2,1)}, u32[]{:S(2)}) copy-start(bf16[64,4096]{1,0:T(8,128)(2,1)} %v_ref.5) | copy-start | bytes 1572868
  0.0 98.3 %copy-start.23 = (s32[64,2]{0,1:T(2,128)S(1)}, s32[64,2]{0,1:T(2,128)}, u32[]{:S(2)}) copy-start(s32[64,2]{0,1:T(2,128)} %param.15) | copy-start | bytes 1540
  0.0 98.3 %copy-start.24 = (s32[64,2]{0,1:T(2,128)S(1)}, s32[64,2]{0,1:T(2,128)}, u32[]{:S(2)}) copy-start(s32[64,2]{0,1:T(2,128)} %param.14) | copy-start | bytes 1540
  0.0 158.6 %collective-permute-start.19 = (bf16[4096,512]{1,0:T(8,128)(2,1)}, bf16[4096,512]{1,0:T(8,128)(2,1)}, u32[]{:S(2)}, u32[]{:S(2)}) collective-permute-start(bf16[4096,512]{1,0:T(8,128)(2,1)} %refs_4_.9), channel_id=1, source_target_pairs={{0,1},{1,0},{2,3},{3,2},{4,5},{5,4},{6,7},{7,6},{8,9},{9,8},{10,11... | collective-permute-start | bytes 12582920 | tf_op jit(solution)/shard_map/ppermute | solution.py:27
  0.6 158.1 %collective-permute-start.20 = (bf16[512,4096]{1,0:T(8,128)(2,1)}, bf16[512,4096]{1,0:T(8,128)(2,1)}, u32[]{:S(2)}, u32[]{:S(2)}) collective-permute-start(bf16[512,4096]{1,0:T(8,128)(2,1)} %refs_6_.5), channel_id=1, source_target_pairs={{0,1},{1,0},{2,3},{3,2},{4,5},{5,4},{6,7},{7,6},{8,9},{9,8},{10,11... | collective-permute-start | bytes 12582920 | tf_op jit(solution)/shard_map/ppermute | solution.py:27
  2.0 36.5 %collective-permute-start.2 = (bf16[2,64,1536]{2,1,0:T(8,128)(2,1)S(1)}, bf16[2,64,1536]{2,1,0:T(8,128)(2,1)S(1)}, u32[]{:S(2)}, u32[]{:S(2)}) collective-permute-start(bf16[2,64,1536]{2,1,0:T(8,128)(2,1)S(1)} %pad_maximum_fusion.1), channel_id=1, source_target_pairs={{12,4},{13,5},{14,6},{15,7},{0,8},{1,9},{2,10},{3,11},{4,12},{5,13... | collective-permute-start | bytes 1179656 | tf_op jit(solution)/shard_map/ppermute | solution.py:27
  6.1 45.9 %collective-permute-start.5 = (bf16[2,64,1536]{2,1,0:T(8,128)(2,1)S(1)}, bf16[2,64,1536]{2,1,0:T(8,128)(2,1)}, u32[]{:S(2)}, u32[]{:S(2)}) collective-permute-start(bf16[2,64,1536]{2,1,0:T(8,128)(2,1)S(1)} %pad_maximum_fusion.2), channel_id=1, source_target_pairs={{12,4},{13,5},{14,6},{15,7},{0,8},{1,9},{2,10},{3,11},{4,12},{5,13... | collective-permute-start | bytes 1179656 | tf_op jit(solution)/shard_map/ppermute | solution.py:27
  7.2 44.8 %collective-permute-start.8 = (bf16[2,64,1024]{2,1,0:T(8,128)(2,1)S(1)}, bf16[2,64,1024]{2,1,0:T(8,128)(2,1)}, u32[]{:S(2)}, u32[]{:S(2)}) collective-permute-start(bf16[2,64,1024]{2,1,0:T(8,128)(2,1)S(1)} %pad_maximum_fusion.3), channel_id=1, source_target_pairs={{12,4},{13,5},{14,6},{15,7},{0,8},{1,9},{2,10},{3,11},{4,12},{5,13... | collective-permute-start | bytes 786440 | tf_op jit(solution)/shard_map/ppermute | solution.py:27
  38.5 56.4 %copy-start.7 = (bf16[2,64,1536]{2,1,0:T(8,128)(2,1)}, bf16[2,64,1536]{2,1,0:T(8,128)(2,1)S(1)}, u32[]{:S(2)}) copy-start(bf16[2,64,1536]{2,1,0:T(8,128)(2,1)S(1)} %collective-permute-done.2.refs_2_) | copy-start | bytes 1179652
  38.5 17.1 %collective-permute-start.3 = (bf16[2,64,1536]{2,1,0:T(8,128)(2,1)S(1)}, bf16[2,64,1536]{2,1,0:T(8,128)(2,1)S(1)}, u32[]{:S(2)}, u32[]{:S(2)}) collective-permute-start(bf16[2,64,1536]{2,1,0:T(8,128)(2,1)S(1)} %collective-permute-done.2.refs_2_), channel_id=1, source_target_pairs={{0,1},{1,0},{2,3},{3,2},{4,5},{5,4},{6,7},{7,6},{8,9},{9,8},{10,11... | collective-permute-start | bytes 1179656 | tf_op jit(solution)/shard_map/ppermute | solution.py:27
  52.0 39.7 %collective-permute-start = (bf16[2,64,4096]{2,1,0:T(8,128)(2,1)S(1)}, bf16[2,64,4096]{2,1,0:T(8,128)(2,1)S(1)}, u32[]{:S(2)}, u32[]{:S(2)}) collective-permute-start(bf16[2,64,4096]{2,1,0:T(8,128)(2,1)S(1)} %pad_maximum_fusion), channel_id=1, source_target_pairs={{0,1},{1,0},{2,3},{3,2},{4,5},{5,4},{6,7},{7,6},{8,9},{9,8},{10,11... | collective-permute-start | bytes 3145736 | tf_op jit(solution)/shard_map/ppermute | solution.py:27
  52.0 42.9 %collective-permute-start.1 = (bf16[2,64,4096]{2,1,0:T(8,128)(2,1)S(1)}, bf16[2,64,4096]{2,1,0:T(8,128)(2,1)S(1)}, u32[]{:S(2)}, u32[]{:S(2)}) collective-permute-start(bf16[2,64,4096]{2,1,0:T(8,128)(2,1)S(1)} %pad_maximum_fusion), channel_id=1, source_target_pairs={{14,13},{13,14},{8,15},{7,0},{2,1},{1,2},{6,5},{5,6},{0,7},{15,8},... | collective-permute-start | bytes 3145736 | tf_op jit(solution)/shard_map/ppermute | solution.py:27
  56.4 17.0 %collective-permute-start.4 = (bf16[2,64,1536]{2,1,0:T(8,128)(2,1)S(1)}, bf16[2,64,1536]{2,1,0:T(8,128)(2,1)S(1)}, u32[]{:S(2)}, u32[]{:S(2)}) collective-permute-start(bf16[2,64,1536]{2,1,0:T(8,128)(2,1)S(1)} %collective-permute-done.2.refs_2_), channel_id=1, source_target_pairs={{14,13},{13,14},{8,15},{7,0},{2,1},{1,2},{6,5},{5,6},{0,7},{15,8},... | collective-permute-start | bytes 1179656 | tf_op jit(solution)/shard_map/ppermute | solution.py:27
  74.1 16.5 %collective-permute-start.6 = (bf16[2,64,1536]{2,1,0:T(8,128)(2,1)}, bf16[2,64,1536]{2,1,0:T(8,128)(2,1)S(1)}, u32[]{:S(2)}, u32[]{:S(2)}) collective-permute-start(bf16[2,64,1536]{2,1,0:T(8,128)(2,1)} %collective-permute-done.5.refs_2_), channel_id=1, source_target_pairs={{0,1},{1,0},{2,3},{3,2},{4,5},{5,4},{6,7},{7,6},{8,9},{9,8},{10,11... | collective-permute-start | bytes 1179656 | tf_op jit(solution)/shard_map/ppermute | solution.py:27
  91.4 16.5 %collective-permute-start.9 = (bf16[2,64,1024]{2,1,0:T(8,128)(2,1)}, bf16[2,64,1024]{2,1,0:T(8,128)(2,1)}, u32[]{:S(2)}, u32[]{:S(2)}) collective-permute-start(bf16[2,64,1024]{2,1,0:T(8,128)(2,1)} %collective-permute-done.8.refs_2_), channel_id=1, source_target_pairs={{0,1},{1,0},{2,3},{3,2},{4,5},{5,4},{6,7},{7,6},{8,9},{9,8},{10,11... | collective-permute-start | bytes 786440 | tf_op jit(solution)/shard_map/ppermute | solution.py:27
  91.8 16.1 %collective-permute-start.10 = (bf16[2,64,1024]{2,1,0:T(8,128)(2,1)}, bf16[2,64,1024]{2,1,0:T(8,128)(2,1)}, u32[]{:S(2)}, u32[]{:S(2)}) collective-permute-start(bf16[2,64,1024]{2,1,0:T(8,128)(2,1)} %collective-permute-done.8.refs_2_), channel_id=1, source_target_pairs={{14,13},{13,14},{8,15},{7,0},{2,1},{1,2},{6,5},{5,6},{0,7},{15,8},... | collective-permute-start | bytes 786440 | tf_op jit(solution)/shard_map/ppermute | solution.py:27
  94.9 10.3 %collective-permute-start.7 = (bf16[2,64,1536]{2,1,0:T(8,128)(2,1)}, bf16[2,64,1536]{2,1,0:T(8,128)(2,1)}, u32[]{:S(2)}, u32[]{:S(2)}) collective-permute-start(bf16[2,64,1536]{2,1,0:T(8,128)(2,1)} %collective-permute-done.5.refs_2_), channel_id=1, source_target_pairs={{14,13},{13,14},{8,15},{7,0},{2,1},{1,2},{6,5},{5,6},{0,7},{15,8},... | collective-permute-start | bytes 1179656 | tf_op jit(solution)/shard_map/ppermute | solution.py:27
  111.2 11.6 %collective-permute-start.11 = (bf16[32,4224]{1,0:T(8,128)(2,1)S(1)}, bf16[32,4224]{1,0:T(8,128)(2,1)S(1)}, u32[]{:S(2)}, u32[]{:S(2)}) collective-permute-start(bf16[32,4224]{1,0:T(8,128)(2,1)S(1)} %get-tuple-element.25.refs_2_), channel_id=1, source_target_pairs={{0,4},{1,5},{4,8},{5,9},{8,12},{9,13},{12,14},{13,15},{14,10},{15,... | collective-permute-start | bytes 811016 | tf_op jit(solution)/shard_map/ppermute | solution.py:27
  111.2 14.6 %collective-permute-start.15 = (bf16[32,4224]{1,0:T(8,128)(2,1)S(1)}, bf16[32,4224]{1,0:T(8,128)(2,1)S(1)}, u32[]{:S(2)}, u32[]{:S(2)}) collective-permute-start(bf16[32,4224]{1,0:T(8,128)(2,1)S(1)} %get-tuple-element.26.refs_3_), channel_id=1, source_target_pairs={{4,0},{5,1},{8,4},{9,5},{12,8},{13,9},{14,12},{15,13},{10,14},{11,... | collective-permute-start | bytes 811016 | tf_op jit(solution)/shard_map/ppermute | solution.py:27
  116.8 11.8 %collective-permute-start.22 = (bf16[32,4224]{1,0:T(8,128)(2,1)S(1)}, bf16[32,4224]{1,0:T(8,128)(2,1)S(1)}, u32[]{:S(2)}, u32[]{:S(2)}) collective-permute-start(bf16[32,4224]{1,0:T(8,128)(2,1)S(1)} %get-tuple-element.26.refs_3_), channel_id=1, source_target_pairs={{0,4},{1,5},{4,8},{5,9},{8,12},{9,13},{12,14},{13,15},{14,10},{15,... | collective-permute-start | bytes 811016 | tf_op jit(solution)/shard_map/ppermute | solution.py:27
  122.8 9.2 %collective-permute-start.25 = (bf16[32,4224]{1,0:T(8,128)(2,1)S(1)}, bf16[32,4224]{1,0:T(8,128)(2,1)S(1)}, u32[]{:S(2)}, u32[]{:S(2)}) collective-permute-start(bf16[32,4224]{1,0:T(8,128)(2,1)S(1)} %get-tuple-element.25.refs_2_), channel_id=1, source_target_pairs={{4,0},{5,1},{8,4},{9,5},{12,8},{13,9},{14,12},{15,13},{10,14},{11,... | collective-permute-start | bytes 811016 | tf_op jit(solution)/shard_map/ppermute | solution.py:27
  125.8 9.4 %collective-permute-start.12 = (bf16[32,4224]{1,0:T(8,128)(2,1)S(1)}, bf16[32,4224]{1,0:T(8,128)(2,1)S(1)}, u32[]{:S(2)}, u32[]{:S(2)}) collective-permute-start(bf16[32,4224]{1,0:T(8,128)(2,1)S(1)} %collective-permute-done.11.refs_0_), channel_id=1, source_target_pairs={{0,4},{1,5},{4,8},{5,9},{8,12},{9,13},{12,14},{13,15},{14,10},{15,... | collective-permute-start | bytes 811016 | tf_op jit(solution)/shard_map/ppermute | solution.py:27
  128.6 9.0 %collective-permute-start.16 = (bf16[32,4224]{1,0:T(8,128)(2,1)S(1)}, bf16[32,4224]{1,0:T(8,128)(2,1)S(1)}, u32[]{:S(2)}, u32[]{:S(2)}) collective-permute-start(bf16[32,4224]{1,0:T(8,128)(2,1)S(1)} %collective-permute-done.15.refs_1_), channel_id=1, source_target_pairs={{4,0},{5,1},{8,4},{9,5},{12,8},{13,9},{14,12},{15,13},{10,14},{11,... | collective-permute-start | bytes 811016 | tf_op jit(solution)/shard_map/ppermute | solution.py:27
  132.0 9.8 %collective-permute-start.23 = (bf16[32,4224]{1,0:T(8,128)(2,1)S(1)}, bf16[32,4224]{1,0:T(8,128)(2,1)S(1)}, u32[]{:S(2)}, u32[]{:S(2)}) collective-permute-start(bf16[32,4224]{1,0:T(8,128)(2,1)S(1)} %collective-permute-done.22.refs_2_), channel_id=1, source_target_pairs={{0,4},{1,5},{4,8},{5,9},{8,12},{9,13},{12,14},{13,15},{14,10},{15,... | collective-permute-start | bytes 811016 | tf_op jit(solution)/shard_map/ppermute | solution.py:27
  135.2 12.2 %collective-permute-start.13 = (bf16[32,4224]{1,0:T(8,128)(2,1)S(1)}, bf16[32,4224]{1,0:T(8,128)(2,1)S(1)}, u32[]{:S(2)}, u32[]{:S(2)}) collective-permute-start(bf16[32,4224]{1,0:T(8,128)(2,1)S(1)} %collective-permute-done.12.refs_0_), channel_id=1, source_target_pairs={{0,4},{1,5},{4,8},{5,9},{8,12},{9,13},{12,14},{13,15},{14,10},{15,... | collective-permute-start | bytes 811016 | tf_op jit(solution)/shard_map/ppermute | solution.py:27
  137.6 9.7 %collective-permute-start.17 = (bf16[32,4224]{1,0:T(8,128)(2,1)S(1)}, bf16[32,4224]{1,0:T(8,128)(2,1)S(1)}, u32[]{:S(2)}, u32[]{:S(2)}) collective-permute-start(bf16[32,4224]{1,0:T(8,128)(2,1)S(1)} %collective-permute-done.16.refs_1_), channel_id=1, source_target_pairs={{4,0},{5,1},{8,4},{9,5},{12,8},{13,9},{14,12},{15,13},{10,14},{11,... | collective-permute-start | bytes 811016 | tf_op jit(solution)/shard_map/ppermute | solution.py:27
  141.8 10.9 %collective-permute-start.26 = (bf16[32,4224]{1,0:T(8,128)(2,1)S(1)}, bf16[32,4224]{1,0:T(8,128)(2,1)S(1)}, u32[]{:S(2)}, u32[]{:S(2)}) collective-permute-start(bf16[32,4224]{1,0:T(8,128)(2,1)S(1)} %collective-permute-done.25.refs_3_), channel_id=1, source_target_pairs={{4,0},{5,1},{8,4},{9,5},{12,8},{13,9},{14,12},{15,13},{10,14},{11,... | collective-permute-start | bytes 811016 | tf_op jit(solution)/shard_map/ppermute | solution.py:27
  147.3 9.3 %collective-permute-start.14 = (bf16[32,4224]{1,0:T(8,128)(2,1)S(1)}, bf16[32,4224]{1,0:T(8,128)(2,1)S(1)}, u32[]{:S(2)}, u32[]{:S(2)}) collective-permute-start(bf16[32,4224]{1,0:T(8,128)(2,1)S(1)} %collective-permute-done.13.refs_0_), channel_id=1, source_target_pairs={{0,4},{1,5},{4,8},{5,9},{8,12},{9,13},{12,14},{13,15},{14,10},{15,... | collective-permute-start | bytes 811016 | tf_op jit(solution)/shard_map/ppermute | solution.py:27
  147.4 11.3 %collective-permute-start.18 = (bf16[32,4224]{1,0:T(8,128)(2,1)S(1)}, bf16[32,4224]{1,0:T(8,128)(2,1)}, u32[]{:S(2)}, u32[]{:S(2)}) collective-permute-start(bf16[32,4224]{1,0:T(8,128)(2,1)S(1)} %collective-permute-done.17.refs_1_), channel_id=1, source_target_pairs={{4,0},{5,1},{8,4},{9,5},{12,8},{13,9},{14,12},{15,13},{10,14},{11,... | collective-permute-start | bytes 811016 | tf_op jit(solution)/shard_map/ppermute | solution.py:27
  152.8 31.4 %collective-permute-start.24 = (bf16[32,4224]{1,0:T(8,128)(2,1)S(1)}, bf16[32,4224]{1,0:T(8,128)(2,1)S(1)}, u32[]{:S(2)}, u32[]{:S(2)}) collective-permute-start(bf16[32,4224]{1,0:T(8,128)(2,1)S(1)} %collective-permute-done.23.refs_2_), channel_id=1, source_target_pairs={{0,4},{1,5},{4,8},{5,9},{8,12},{9,13},{12,14},{13,15},{14,10},{15,... | collective-permute-start | bytes 811016 | tf_op jit(solution)/shard_map/ppermute | solution.py:27
  156.6 28.1 %collective-permute-start.27 = (bf16[32,4224]{1,0:T(8,128)(2,1)S(1)}, bf16[32,4224]{1,0:T(8,128)(2,1)S(1)}, u32[]{:S(2)}, u32[]{:S(2)}) collective-permute-start(bf16[32,4224]{1,0:T(8,128)(2,1)S(1)} %collective-permute-done.26.refs_3_), channel_id=1, source_target_pairs={{4,0},{5,1},{8,4},{9,5},{12,8},{13,9},{14,12},{15,13},{10,14},{11,... | collective-permute-start | bytes 811016 | tf_op jit(solution)/shard_map/ppermute | solution.py:27
  169.2 26.0 %collective-permute-start.21 = (bf16[32,4096]{1,0:T(8,128)(2,1)S(1)}, bf16[32,4096]{1,0:T(8,128)(2,1)S(1)}, u32[]{:S(2)}, u32[]{:S(2)}) collective-permute-start(bf16[32,4096]{1,0:T(8,128)(2,1)S(1)} %get-tuple-element.27), channel_id=1, source_target_pairs={{0,4},{1,5},{4,8},{5,9},{8,12},{9,13},{12,14},{13,15},{14,10},{15,... | collective-permute-start | bytes 786440 | tf_op jit(solution)/shard_map/ppermute | solution.py:27
  174.8 20.6 %collective-permute-start.31 = (bf16[32,4096]{1,0:T(8,128)(2,1)S(1)}, bf16[32,4096]{1,0:T(8,128)(2,1)S(1)}, u32[]{:S(2)}, u32[]{:S(2)}) collective-permute-start(bf16[32,4096]{1,0:T(8,128)(2,1)S(1)} %get-tuple-element.31), channel_id=1, source_target_pairs={{4,0},{5,1},{8,4},{9,5},{12,8},{13,9},{14,12},{15,13},{10,14},{11,... | collective-permute-start | bytes 786440 | tf_op jit(solution)/shard_map/ppermute | solution.py:27
  177.3 20.2 %collective-permute-start.34 = (bf16[32,4096]{1,0:T(8,128)(2,1)S(1)}, bf16[32,4096]{1,0:T(8,128)(2,1)S(1)}, u32[]{:S(2)}, u32[]{:S(2)}) collective-permute-start(bf16[32,4096]{1,0:T(8,128)(2,1)S(1)} %get-tuple-element.35), channel_id=1, source_target_pairs={{4,0},{5,1},{8,4},{9,5},{12,8},{13,9},{14,12},{15,13},{10,14},{11,... | collective-permute-start | bytes 786440 | tf_op jit(solution)/shard_map/ppermute | solution.py:27
  184.2 15.1 %collective-permute-start.38 = (bf16[32,4096]{1,0:T(8,128)(2,1)S(1)}, bf16[32,4096]{1,0:T(8,128)(2,1)S(1)}, u32[]{:S(2)}, u32[]{:S(2)}) collective-permute-start(bf16[32,4096]{1,0:T(8,128)(2,1)S(1)} %get-tuple-element.39), channel_id=1, source_target_pairs={{0,4},{1,5},{4,8},{5,9},{8,12},{9,13},{12,14},{13,15},{14,10},{15,... | collective-permute-start | bytes 786440 | tf_op jit(solution)/shard_map/ppermute | solution.py:27
  195.2 30.0 %copy-start.20 = (f32[3,4096]{1,0:T(4,128)S(1)}, f32[3,4096]{1,0:T(4,128)}, u32[]{:S(2)}) copy-start(f32[3,4096]{1,0:T(4,128)} %modulation_ref.1) | copy-start | bytes 147460
  195.2 30.0 %copy-start.22 = (bf16[64,1024]{1,0:T(8,128)(2,1)S(1)}, bf16[64,1024]{1,0:T(8,128)(2,1)}, u32[]{:S(2)}) copy-start(bf16[64,1024]{1,0:T(8,128)(2,1)} %copy-done.21) | copy-start | bytes 393220
  195.3 9.2 %collective-permute-start.28 = (bf16[32,4096]{1,0:T(8,128)(2,1)S(1)}, bf16[32,4096]{1,0:T(8,128)(2,1)S(1)}, u32[]{:S(2)}, u32[]{:S(2)}) collective-permute-start(bf16[32,4096]{1,0:T(8,128)(2,1)S(1)} %add_convert_fusion.9), channel_id=1, source_target_pairs={{0,4},{1,5},{4,8},{5,9},{8,12},{9,13},{12,14},{13,15},{14,10},{15,... | collective-permute-start | bytes 786440 | tf_op jit(solution)/shard_map/ppermute | solution.py:27
  195.5 9.2 %collective-permute-start.32 = (bf16[32,4096]{1,0:T(8,128)(2,1)S(1)}, bf16[32,4096]{1,0:T(8,128)(2,1)S(1)}, u32[]{:S(2)}, u32[]{:S(2)}) collective-permute-start(bf16[32,4096]{1,0:T(8,128)(2,1)S(1)} %add_convert_fusion.6), channel_id=1, source_target_pairs={{4,0},{5,1},{8,4},{9,5},{12,8},{13,9},{14,12},{15,13},{10,14},{11,... | collective-permute-start | bytes 786440 | tf_op jit(solution)/shard_map/ppermute | solution.py:27
  197.6 12.7 %collective-permute-start.35 = (bf16[32,4096]{1,0:T(8,128)(2,1)S(1)}, bf16[32,4096]{1,0:T(8,128)(2,1)S(1)}, u32[]{:S(2)}, u32[]{:S(2)}) collective-permute-start(bf16[32,4096]{1,0:T(8,128)(2,1)S(1)} %add_convert_fusion.4), channel_id=1, source_target_pairs={{4,0},{5,1},{8,4},{9,5},{12,8},{13,9},{14,12},{15,13},{10,14},{11,... | collective-permute-start | bytes 786440 | tf_op jit(solution)/shard_map/ppermute | solution.py:27
  199.4 13.0 %collective-permute-start.39 = (bf16[32,4096]{1,0:T(8,128)(2,1)S(1)}, bf16[32,4096]{1,0:T(8,128)(2,1)S(1)}, u32[]{:S(2)}, u32[]{:S(2)}) collective-permute-start(bf16[32,4096]{1,0:T(8,128)(2,1)S(1)} %add_convert_fusion.1), channel_id=1, source_target_pairs={{0,4},{1,5},{4,8},{5,9},{8,12},{9,13},{12,14},{13,15},{14,10},{15,... | collective-permute-start | bytes 786440 | tf_op jit(solution)/shard_map/ppermute | solution.py:27
  204.6 11.2 %collective-permute-start.29 = (bf16[32,4096]{1,0:T(8,128)(2,1)S(1)}, bf16[32,4096]{1,0:T(8,128)(2,1)S(1)}, u32[]{:S(2)}, u32[]{:S(2)}) collective-permute-start(bf16[32,4096]{1,0:T(8,128)(2,1)S(1)} %add_convert_fusion.8), channel_id=1, source_target_pairs={{0,4},{1,5},{4,8},{5,9},{8,12},{9,13},{12,14},{13,15},{14,10},{15,... | collective-permute-start | bytes 786440 | tf_op jit(solution)/shard_map/ppermute | solution.py:27
  204.8 16.1 %collective-permute-start.33 = (bf16[32,4096]{1,0:T(8,128)(2,1)S(1)}, bf16[32,4096]{1,0:T(8,128)(2,1)S(1)}, u32[]{:S(2)}, u32[]{:S(2)}) collective-permute-start(bf16[32,4096]{1,0:T(8,128)(2,1)S(1)} %add_convert_fusion.5), channel_id=1, source_target_pairs={{4,0},{5,1},{8,4},{9,5},{12,8},{13,9},{14,12},{15,13},{10,14},{11,... | collective-permute-start | bytes 786440 | tf_op jit(solution)/shard_map/ppermute | solution.py:27
  210.4 8.3 %collective-permute-start.36 = (bf16[32,4096]{1,0:T(8,128)(2,1)S(1)}, bf16[32,4096]{1,0:T(8,128)(2,1)S(1)}, u32[]{:S(2)}, u32[]{:S(2)}) collective-permute-start(bf16[32,4096]{1,0:T(8,128)(2,1)S(1)} %add_convert_fusion.3), channel_id=1, source_target_pairs={{4,0},{5,1},{8,4},{9,5},{12,8},{13,9},{14,12},{15,13},{10,14},{11,... | collective-permute-start | bytes 786440 | tf_op jit(solution)/shard_map/ppermute | solution.py:27
  212.5 8.7 %collective-permute-start.40 = (bf16[32,4096]{1,0:T(8,128)(2,1)S(1)}, bf16[32,4096]{1,0:T(8,128)(2,1)S(1)}, u32[]{:S(2)}, u32[]{:S(2)}) collective-permute-start(bf16[32,4096]{1,0:T(8,128)(2,1)S(1)} %add_convert_fusion), channel_id=1, source_target_pairs={{0,4},{1,5},{4,8},{5,9},{8,12},{9,13},{12,14},{13,15},{14,10},{15,... | collective-permute-start | bytes 786440 | tf_op jit(solution)/shard_map/ppermute | solution.py:27
  215.9 8.2 %collective-permute-start.30 = (bf16[32,4096]{1,0:T(8,128)(2,1)S(1)}, bf16[32,4096]{1,0:T(8,128)(2,1)S(1)}, u32[]{:S(2)}, u32[]{:S(2)}) collective-permute-start(bf16[32,4096]{1,0:T(8,128)(2,1)S(1)} %add_convert_fusion.7), channel_id=1, source_target_pairs={{0,4},{1,5},{4,8},{5,9},{8,12},{9,13},{12,14},{13,15},{14,10},{15,... | collective-permute-start | bytes 786440 | tf_op jit(solution)/shard_map/ppermute | solution.py:27
  218.8 6.4 %collective-permute-start.37 = (bf16[32,4096]{1,0:T(8,128)(2,1)S(1)}, bf16[32,4096]{1,0:T(8,128)(2,1)S(1)}, u32[]{:S(2)}, u32[]{:S(2)}) collective-permute-start(bf16[32,4096]{1,0:T(8,128)(2,1)S(1)} %add_convert_fusion.2), channel_id=1, source_target_pairs={{4,0},{5,1},{8,4},{9,5},{12,8},{13,9},{14,12},{15,13},{10,14},{11,... | collective-permute-start | bytes 786440 | tf_op jit(solution)/shard_map/ppermute | solution.py:27
  (18 other events, 51.9 us)

commit v4 on v3

--- a/solution.py
+++ b/solution.py
@@ -22,9 +22,15 @@
 ATTEND_VMEM = 16 * 2**20
 EXPERT_VMEM = 26 * 2**20
 
+TILE, GROUPS = "tile", "groups"
+LONG = "long"
+SHORT = "short"
+UPPER = "upper"
+LOWER = "lower"
+
 
 def permute(x, pairs):
-    return lax.ppermute(x, "tile", pairs)
+    return lax.ppermute(x, TILE, pairs)
 
 
 def band_pairs(devices):
@@ -145,7 +151,6 @@
             bytes_accessed=(2 * sources + 2) * rows * part * 2,
             transcendentals=rows * rows * sources * part // HEAD_DIM,
         ),
-        name="attend_last" if last else "attend",
     )(flags, *operands)
 
 
@@ -224,7 +229,6 @@
             bytes_accessed=4 * width * hidden,
             transcendentals=count * rows * hidden,
         ),
-        name="experts",
     )(mine, *flat, *weights)
 
 
@@ -265,8 +269,8 @@
 
 def block(queries, key_rows, values, modulation, expert_in, expert_out, routes, gate_fixed):
     _, width = queries.shape
-    devices = lax.axis_size("tile")
-    position = lax.axis_index("tile")
+    devices = lax.axis_size(TILE)
+    position = lax.axis_index(TILE)
     grid_rows = devices // TILE_COLS
     tile = (position + TILE_COLS // 2) % devices
     grid_row, grid_col = tile // TILE_COLS, tile % TILE_COLS
@@ -324,15 +328,15 @@
     mine = (position // SPLIT).astype(jnp.int32).reshape(1)
     add = lambda a, b: (a.astype(jnp.float32) + b.astype(jnp.float32)).astype(jnp.bfloat16)
 
-    rows_of = {("upper", 0): upper, ("lower", 0): lower}
+    rows_of = {(UPPER, 0): upper, (LOWER, 0): lower}
     for s in range(1, far + 1):
         for kind, half, sign, pairs in (
-            ("long", "upper", -1, forward),
-            ("long", "lower", 1, backward),
-            ("short", "lower", -1, forward),
-            ("short", "upper", 1, backward),
+            (LONG, UPPER, -1, forward),
+            (LONG, LOWER, 1, backward),
+            (SHORT, LOWER, -1, forward),
+            (SHORT, UPPER, 1, backward),
         ):
-            if kind == "long" or s < far:
+            if kind == LONG or s < far:
                 rows_of[half, sign * s] = permute(rows_of[half, sign * (s - 1)], pairs)
 
     partial = {}
@@ -341,46 +345,46 @@
         partial.update(zip(keys, run_experts([rows_of[k] for k in keys], weights, mine)))
 
     for s in range(1, far + 1):
-        keys = [("upper", -s), ("lower", s)]
+        keys = [(UPPER, -s), (LOWER, s)]
         if s == 1:
-            keys += [("upper", 0), ("lower", 0)]
+            keys += [(UPPER, 0), (LOWER, 0)]
         elif s < far:
-            keys += [("lower", -(s - 1)), ("upper", s - 1)]
+            keys += [(LOWER, -(s - 1)), (UPPER, s - 1)]
         share(keys)
-    share([("lower", 1 - far), ("upper", far - 1)])
+    share([(LOWER, 1 - far), (UPPER, far - 1)])
 
     def reduce_chain(kind, half, sign, pairs):
-        hops = far if kind == "long" else far - 1
-        x = partial[half, -sign * hops if kind == "long" else sign * hops]
+        hops = far if kind == LONG else far - 1
+        x = partial[half, -sign * hops if kind == LONG else sign * hops]
         for s in range(hops, 0, -1):
             x = permute(x, pairs)
             if s > 1:
                 x = add(x, partial[half, sign * (s - 1)])
         return x
 
-    long_f = reduce_chain("long", "upper", 1, forward)
-    long_b = reduce_chain("long", "lower", -1, backward)
-    short_f = reduce_chain("short", "lower", 1, forward)
-    short_b = reduce_chain("short", "upper", -1, backward)
+    long_f = reduce_chain(LONG, UPPER, 1, forward)
+    long_b = reduce_chain(LONG, LOWER, -1, backward)
+    short_f = reduce_chain(SHORT, LOWER, 1, forward)
+    short_b = reduce_chain(SHORT, UPPER, -1, backward)
     return combine(
         attended,
         modulation,
-        [long_f, short_b, partial["upper", 0]],
-        [long_b, short_f, partial["lower", 0]],
+        [long_f, short_b, partial[UPPER, 0]],
+        [long_b, short_f, partial[LOWER, 0]],
     )
 
 
 def solution(mesh):
     placed = (
-        P(("groups", "tile"), None),
-        P(("groups", "tile"), None),
-        P(("groups", "tile"), None),
-        P("groups", None),
-        P(None, "tile"),
-        P("tile", None),
-        P(("groups", "tile"), None),
-        P(("groups", "tile"), None),
+        P((GROUPS, TILE), None),
+        P((GROUPS, TILE), None),
+        P((GROUPS, TILE), None),
+        P(GROUPS, None),
+        P(None, TILE),
+        P(TILE, None),
+        P((GROUPS, TILE), None),
+        P((GROUPS, TILE), None),
     )
     return jax.shard_map(
-        block, mesh=mesh, in_specs=placed, out_specs=P(("groups", "tile"), None), check_vma=False
+        block, mesh=mesh, in_specs=placed, out_specs=P((GROUPS, TILE), None), check_vma=False
     )

time: 227 us -> 227 us (level)
  no operation moved by 1% of the time
where the time goes in v4:
time: 227 us; the launch traced here: 226 us
  waiting for transfers between devices  105 us (46%)
  starting transfers between devices  68.9 us (30%)
  Pallas kernels  35.6 us (16%)
  local copies, waits for them, and re-layouts  15.2 us (7%)
    ppermute x41, waiting for transfers between devices, permute(): return lax.ppermute(x, TILE, pairs)  105 us
    ppermute x41, starting transfers between devices, permute(): return lax.ppermute(x, TILE, pairs)  68.9 us
    pallas_call x5, Pallas kernels, run_experts(): pl.pallas_call(functools.partial(experts_kernel, count), out_shape=[jax.S...  27.2 us
    unnamed x50, local copies, waits for them, and re-layouts  12.8 us
    pallas_call x3, Pallas kernels, attend_chunk(): pl.pallas_call(functools.partial(attention_kernel, start, part // HEAD_DI...  7.36 us
  transfers between devices with their start and end apart: 41, of which 22 were waited for; matrix products, arithmetic and copies ran while one was open for 1% of the time, Pallas kernels for 15%

profile of v4, /device:TPU:0, one launch (start us, length us, event | category | flops | bytes accessed | tf_op | source)
XLA Modules:
  0.0 226.3 jit_solution(16270656615490747728)
XLA Ops:
  2.0 4.1 %collective-permute-start.2 = (bf16[2,64,1536]{2,1,0:T(8,128)(2,1)S(1)}, bf16[2,64,1536]{2,1,0:T(8,128)(2,1)S(1)}, u32[]{:S(2)}, u32[]{:S(2)}) collective-permute-start(bf16[2,64,1536]{2,1,0:T(8,128)(2,1)S(1)} %pad_maximum_fusion.1), channel_id=1, source_target_pairs={{12,4},{13,5},{14,6},{15,7},{0,8},{1,9},{2,10},{3,11},{4,12},{5,13... | collective-permute-start | bytes 1179656 | tf_op jit(solution)/shard_map/ppermute | solution.py:33
  7.2 3.0 %collective-permute-start.8 = (bf16[2,64,1024]{2,1,0:T(8,128)(2,1)S(1)}, bf16[2,64,1024]{2,1,0:T(8,128)(2,1)}, u32[]{:S(2)}, u32[]{:S(2)}) collective-permute-start(bf16[2,64,1024]{2,1,0:T(8,128)(2,1)S(1)} %pad_maximum_fusion.3), channel_id=1, source_target_pairs={{12,4},{13,5},{14,6},{15,7},{0,8},{1,9},{2,10},{3,11},{4,12},{5,13... | collective-permute-start | bytes 786440 | tf_op jit(solution)/shard_map/ppermute | solution.py:33
  10.2 28.3 %collective-permute-done.2.refs_2_ = bf16[2,64,1536]{2,1,0:T(8,128)(2,1)S(1)} collective-permute-done((bf16[2,64,1536]{2,1,0:T(8,128)(2,1)S(1)}, bf16[2,64,1536]{2,1,0:T(8,128)(2,1)S(1)}, u32[]{:S(2)}, u32[]{:S(2)}) %collective-permute-start.2) | collective-permute-done | bytes 393248 | tf_op jit(solution)/shard_map/ppermute | solution.py:33
  38.6 13.4 %collective-permute-done.8.refs_2_ = bf16[2,64,1024]{2,1,0:T(8,128)(2,1)} collective-permute-done((bf16[2,64,1024]{2,1,0:T(8,128)(2,1)S(1)}, bf16[2,64,1024]{2,1,0:T(8,128)(2,1)}, u32[]{:S(2)}, u32[]{:S(2)}) %collective-permute-start.8) | collective-permute-done | bytes 262176 | tf_op jit(solution)/shard_map/ppermute | solution.py:33
  52.0 3.6 %collective-permute-start.1 = (bf16[2,64,4096]{2,1,0:T(8,128)(2,1)S(1)}, bf16[2,64,4096]{2,1,0:T(8,128)(2,1)S(1)}, u32[]{:S(2)}, u32[]{:S(2)}) collective-permute-start(bf16[2,64,4096]{2,1,0:T(8,128)(2,1)S(1)} %pad_maximum_fusion), channel_id=1, source_target_pairs={{14,13},{13,14},{8,15},{7,0},{2,1},{1,2},{6,5},{5,6},{0,7},{15,8},... | collective-permute-start | bytes 3145736 | tf_op jit(solution)/shard_map/ppermute | solution.py:33
  56.4 2.9 %collective-permute-start.4 = (bf16[2,64,1536]{2,1,0:T(8,128)(2,1)S(1)}, bf16[2,64,1536]{2,1,0:T(8,128)(2,1)S(1)}, u32[]{:S(2)}, u32[]{:S(2)}) collective-permute-start(bf16[2,64,1536]{2,1,0:T(8,128)(2,1)S(1)} %collective-permute-done.2.refs_2_), channel_id=1, source_target_pairs={{14,13},{13,14},{8,15},{7,0},{2,1},{1,2},{6,5},{5,6},{0,7},{15,8},... | collective-permute-start | bytes 1179656 | tf_op jit(solution)/shard_map/ppermute | solution.py:33
  59.3 14.1 %collective-permute-done.4.refs_4_ = bf16[2,64,1536]{2,1,0:T(8,128)(2,1)S(1)} collective-permute-done((bf16[2,64,1536]{2,1,0:T(8,128)(2,1)S(1)}, bf16[2,64,1536]{2,1,0:T(8,128)(2,1)S(1)}, u32[]{:S(2)}, u32[]{:S(2)}) %collective-permute-start.4) | collective-permute-done | bytes 393248 | tf_op jit(solution)/shard_map/ppermute | solution.py:33
  74.1 15.0 %collective-permute-start.6 = (bf16[2,64,1536]{2,1,0:T(8,128)(2,1)}, bf16[2,64,1536]{2,1,0:T(8,128)(2,1)S(1)}, u32[]{:S(2)}, u32[]{:S(2)}) collective-permute-start(bf16[2,64,1536]{2,1,0:T(8,128)(2,1)} %collective-permute-done.5.refs_2_), channel_id=1, source_target_pairs={{0,1},{1,0},{2,3},{3,2},{4,5},{5,4},{6,7},{7,6},{8,9},{9,8},{10,11... | collective-permute-start | bytes 1179656 | tf_op jit(solution)/shard_map/ppermute | solution.py:33
  91.8 3.1 %collective-permute-start.10 = (bf16[2,64,1024]{2,1,0:T(8,128)(2,1)}, bf16[2,64,1024]{2,1,0:T(8,128)(2,1)}, u32[]{:S(2)}, u32[]{:S(2)}) collective-permute-start(bf16[2,64,1024]{2,1,0:T(8,128)(2,1)} %collective-permute-done.8.refs_2_), channel_id=1, source_target_pairs={{14,13},{13,14},{8,15},{7,0},{2,1},{1,2},{6,5},{5,6},{0,7},{15,8},... | collective-permute-start | bytes 786440 | tf_op jit(solution)/shard_map/ppermute | solution.py:33
  94.9 3.3 %collective-permute-start.7 = (bf16[2,64,1536]{2,1,0:T(8,128)(2,1)}, bf16[2,64,1536]{2,1,0:T(8,128)(2,1)}, u32[]{:S(2)}, u32[]{:S(2)}) collective-permute-start(bf16[2,64,1536]{2,1,0:T(8,128)(2,1)} %collective-permute-done.5.refs_2_), channel_id=1, source_target_pairs={{14,13},{13,14},{8,15},{7,0},{2,1},{1,2},{6,5},{5,6},{0,7},{15,8},... | collective-permute-start | bytes 1179656 | tf_op jit(solution)/shard_map/ppermute | solution.py:33
  102.6 2.1 shard_map.82.refs_7_.refs_0_
  105.2 2.7 %shard_map.83.refs_8_.refs_1_ = bf16[64,1536]{1,0:T(8,128)(2,1)S(1)} custom-call(s32[6]{0:T(128)S(1)} %add_convert_fusion.10.flags_ref, bf16[64,4096]{1,0:T(8,128)(2,1)S(1)} %copy-done.6, bf16[64,4096]{1,0:T(8,128)(2,1)S(1)} %copy-done.4, bf16[64,4096]{1,0:T(8,128)(2,1)S(1)} %copy-done.5, bf16[2,64,4096]{2,1,0:T(8,128)(2,1)S(1)} %collective-permute-done.refs_0_, ...), custom_call_target="tpu_custom_call" | custom-call | flops 150994944 | bytes 2752512 | tf_op jit(solution)/shard_map/pallas_call | solution.py:143
  107.9 2.6 %shard_map.84 = (bf16[64,1024]{1,0:T(8,128)(2,1)S(1)}, bf16[32,4224]{1,0:T(8,128)(2,1)S(1)}, bf16[32,4224]{1,0:T(8,128)(2,1)S(1)}) custom-call(s32[6]{0:T(128)S(1)} %add_convert_fusion.10.flags_ref, bf16[64,4096]{1,0:T(8,128)(2,1)S(1)} %copy-done.6, bf16[64,4096]{1,0:T(8,128)(2,1)S(1)} %copy-done.4, bf16[64,4096]{1,0:T(8,128)(2,1)S(1)} %copy-done.5, ...), custom_call_target="tpu_custom_call" | custom-call | flops 100663296 | bytes 1835008 | tf_op jit(solution)/shard_map/pallas_call | solution.py:143
  111.2 5.6 %collective-permute-start.15 = (bf16[32,4224]{1,0:T(8,128)(2,1)S(1)}, bf16[32,4224]{1,0:T(8,128)(2,1)S(1)}, u32[]{:S(2)}, u32[]{:S(2)}) collective-permute-start(bf16[32,4224]{1,0:T(8,128)(2,1)S(1)} %get-tuple-element.26.refs_3_), channel_id=1, source_target_pairs={{4,0},{5,1},{8,4},{9,5},{12,8},{13,9},{14,12},{15,13},{10,14},{11,... | collective-permute-start | bytes 811016 | tf_op jit(solution)/shard_map/ppermute | solution.py:33
  117.6 5.3 %collective-permute-done.11.refs_0_ = bf16[32,4224]{1,0:T(8,128)(2,1)S(1)} collective-permute-done((bf16[32,4224]{1,0:T(8,128)(2,1)S(1)}, bf16[32,4224]{1,0:T(8,128)(2,1)S(1)}, u32[]{:S(2)}, u32[]{:S(2)}) %collective-permute-start.11) | collective-permute-done | bytes 270368 | tf_op jit(solution)/shard_map/ppermute | solution.py:33
  122.8 2.3 %collective-permute-start.25 = (bf16[32,4224]{1,0:T(8,128)(2,1)S(1)}, bf16[32,4224]{1,0:T(8,128)(2,1)S(1)}, u32[]{:S(2)}, u32[]{:S(2)}) collective-permute-start(bf16[32,4224]{1,0:T(8,128)(2,1)S(1)} %get-tuple-element.25.refs_2_), channel_id=1, source_target_pairs={{4,0},{5,1},{8,4},{9,5},{12,8},{13,9},{14,12},{15,13},{10,14},{11,... | collective-permute-start | bytes 811016 | tf_op jit(solution)/shard_map/ppermute | solution.py:33
  125.8 2.8 %collective-permute-done.22.refs_2_ = bf16[32,4224]{1,0:T(8,128)(2,1)S(1)} collective-permute-done((bf16[32,4224]{1,0:T(8,128)(2,1)S(1)}, bf16[32,4224]{1,0:T(8,128)(2,1)S(1)}, u32[]{:S(2)}, u32[]{:S(2)}) %collective-permute-start.22) | collective-permute-done | bytes 270368 | tf_op jit(solution)/shard_map/ppermute | solution.py:33
  129.3 2.7 %collective-permute-done.25.refs_3_ = bf16[32,4224]{1,0:T(8,128)(2,1)S(1)} collective-permute-done((bf16[32,4224]{1,0:T(8,128)(2,1)S(1)}, bf16[32,4224]{1,0:T(8,128)(2,1)S(1)}, u32[]{:S(2)}, u32[]{:S(2)}) %collective-permute-start.25) | collective-permute-done | bytes 270368 | tf_op jit(solution)/shard_map/ppermute | solution.py:33
  132.0 3.2 %collective-permute-done.12.refs_0_ = bf16[32,4224]{1,0:T(8,128)(2,1)S(1)} collective-permute-done((bf16[32,4224]{1,0:T(8,128)(2,1)S(1)}, bf16[32,4224]{1,0:T(8,128)(2,1)S(1)}, u32[]{:S(2)}, u32[]{:S(2)}) %collective-permute-start.12) | collective-permute-done | bytes 270368 | tf_op jit(solution)/shard_map/ppermute | solution.py:33
  135.8 1.8 collective-permute-done.16.refs_1_
  137.6 2.5 %collective-permute-start.17 = (bf16[32,4224]{1,0:T(8,128)(2,1)S(1)}, bf16[32,4224]{1,0:T(8,128)(2,1)S(1)}, u32[]{:S(2)}, u32[]{:S(2)}) collective-permute-start(bf16[32,4224]{1,0:T(8,128)(2,1)S(1)} %collective-permute-done.16.refs_1_), channel_id=1, source_target_pairs={{4,0},{5,1},{8,4},{9,5},{12,8},{13,9},{14,12},{15,13},{10,14},{11,... | collective-permute-start | bytes 811016 | tf_op jit(solution)/shard_map/ppermute | solution.py:33
  140.1 1.7 collective-permute-done.23.refs_2_
  141.8 2.0 collective-permute-start.26
  143.8 3.5 %collective-permute-done.13.refs_0_ = bf16[32,4224]{1,0:T(8,128)(2,1)S(1)} collective-permute-done((bf16[32,4224]{1,0:T(8,128)(2,1)S(1)}, bf16[32,4224]{1,0:T(8,128)(2,1)S(1)}, u32[]{:S(2)}, u32[]{:S(2)}) %collective-permute-start.13) | collective-permute-done | bytes 270368 | tf_op jit(solution)/shard_map/ppermute | solution.py:33
  147.4 2.1 collective-permute-start.18
  149.4 3.3 %collective-permute-done.26.refs_3_ = bf16[32,4224]{1,0:T(8,128)(2,1)S(1)} collective-permute-done((bf16[32,4224]{1,0:T(8,128)(2,1)S(1)}, bf16[32,4224]{1,0:T(8,128)(2,1)S(1)}, u32[]{:S(2)}, u32[]{:S(2)}) %collective-permute-start.26) | collective-permute-done | bytes 270368 | tf_op jit(solution)/shard_map/ppermute | solution.py:33
  152.8 1.7 collective-permute-start.24
  154.4 2.2 collective-permute-done.14.refs_0_
  156.6 2.0 collective-permute-done.18.refs_1_
  158.7 2.2 copy-done
  160.9 2.2 copy-done.2
  163.0 6.2 %shard_map.85 = (bf16[32,4096]{1,0:T(8,128)(2,1)S(1)}, bf16[32,4096]{1,0:T(8,128)(2,1)S(1)}) custom-call(s32[1]{0:T(128)} %bitcast.9.mine_ref, bf16[32,4224]{1,0:T(8,128)(2,1)S(1)} %collective-permute-done.14.refs_0_, bf16[32,4224]{1,0:T(8,128)(2,1)} %collective-permute-done.18.refs_1_, bf16[4096,512]{1,0:T(8,128)(2,1)S(1)} %copy-done, ...), custom_call_target="tpu_custom_call" | custom-call | flops 1073741824 | bytes 16777216 | tf_op jit(solution)/shard_map/pallas_call | solution.py:213
  169.3 5.5 %shard_map.87 = (bf16[32,4096]{1,0:T(8,128)(2,1)S(1)}, bf16[32,4096]{1,0:T(8,128)(2,1)S(1)}, bf16[32,4096]{1,0:T(8,128)(2,1)S(1)}, bf16[32,4096]{1,0:T(8,128)(2,1)S(1)}) custom-call(s32[1]{0:T(128)} %bitcast.9.mine_ref, bf16[32,4224]{1,0:T(8,128)(2,1)S(1)} %collective-permute-done.13.refs_0_, bf16[32,4224]{1,0:T(8,128)(2,1)S(1)} %collective-permute-done.17.refs_1_, ...), custom_call_target="tpu_custom_call" | custom-call | flops 2147483648 | bytes 16777216 | tf_op jit(solution)/shard_map/pallas_call | solution.py:213
  174.8 2.5 %collective-permute-start.31 = (bf16[32,4096]{1,0:T(8,128)(2,1)S(1)}, bf16[32,4096]{1,0:T(8,128)(2,1)S(1)}, u32[]{:S(2)}, u32[]{:S(2)}) collective-permute-start(bf16[32,4096]{1,0:T(8,128)(2,1)S(1)} %get-tuple-element.31), channel_id=1, source_target_pairs={{4,0},{5,1},{8,4},{9,5},{12,8},{13,9},{14,12},{15,13},{10,14},{11,... | collective-permute-start | bytes 786440 | tf_op jit(solution)/shard_map/ppermute | solution.py:33
  177.3 1.7 collective-permute-start.34
  179.0 5.2 %shard_map.88 = (bf16[32,4096]{1,0:T(8,128)(2,1)S(1)}, bf16[32,4096]{1,0:T(8,128)(2,1)S(1)}, bf16[32,4096]{1,0:T(8,128)(2,1)S(1)}, bf16[32,4096]{1,0:T(8,128)(2,1)S(1)}) custom-call(s32[1]{0:T(128)} %bitcast.9.mine_ref, bf16[32,4224]{1,0:T(8,128)(2,1)S(1)} %collective-permute-done.12.refs_0_, bf16[32,4224]{1,0:T(8,128)(2,1)S(1)} %collective-permute-done.16.refs_1_, ...), custom_call_target="tpu_custom_call" | custom-call | flops 2147483648 | bytes 16777216 | tf_op jit(solution)/shard_map/pallas_call | solution.py:213
  184.8 5.2 %shard_map.86 = (bf16[32,4096]{1,0:T(8,128)(2,1)S(1)}, bf16[32,4096]{1,0:T(8,128)(2,1)S(1)}) custom-call(s32[1]{0:T(128)} %bitcast.9.mine_ref, bf16[32,4224]{1,0:T(8,128)(2,1)S(1)} %collective-permute-done.24.refs_0_, bf16[32,4224]{1,0:T(8,128)(2,1)S(1)} %collective-permute-done.27.refs_1_, bf16[4096,512]{1,0:T(8,128)(2,1)S(1)} %copy-done.1, ...), custom_call_target="tpu_custom_call" | custom-call | flops 1073741824 | bytes 16777216 | tf_op jit(solution)/shard_map/pallas_call | solution.py:213
  190.0 5.2 %shard_map.89 = (bf16[32,4096]{1,0:T(8,128)(2,1)S(1)}, bf16[32,4096]{1,0:T(8,128)(2,1)S(1)}, bf16[32,4096]{1,0:T(8,128)(2,1)S(1)}, bf16[32,4096]{1,0:T(8,128)(2,1)S(1)}) custom-call(s32[1]{0:T(128)} %bitcast.9.mine_ref, bf16[32,4224]{1,0:T(8,128)(2,1)S(1)} %collective-permute-done.11.refs_0_, bf16[32,4224]{1,0:T(8,128)(2,1)S(1)} %collective-permute-done.15.refs_1_, ...), custom_call_target="tpu_custom_call" | custom-call | flops 2147483648 | bytes 16777216 | tf_op jit(solution)/shard_map/pallas_call | solution.py:213
  195.5 2.1 collective-permute-start.32
  197.6 1.8 collective-permute-start.35
  199.8 4.8 %collective-permute-done.28 = bf16[32,4096]{1,0:T(8,128)(2,1)S(1)} collective-permute-done((bf16[32,4096]{1,0:T(8,128)(2,1)S(1)}, bf16[32,4096]{1,0:T(8,128)(2,1)S(1)}, u32[]{:S(2)}, u32[]{:S(2)}) %collective-permute-start.28) | collective-permute-done | bytes 262176 | tf_op jit(solution)/shard_map/ppermute | solution.py:33
  204.8 2.1 collective-permute-start.33
  206.8 3.5 %collective-permute-done.35 = bf16[32,4096]{1,0:T(8,128)(2,1)S(1)} collective-permute-done((bf16[32,4096]{1,0:T(8,128)(2,1)S(1)}, bf16[32,4096]{1,0:T(8,128)(2,1)S(1)}, u32[]{:S(2)}, u32[]{:S(2)}) %collective-permute-start.35) | collective-permute-done | bytes 262176 | tf_op jit(solution)/shard_map/ppermute | solution.py:33
  210.4 2.0 collective-permute-start.36
  212.6 3.2 %collective-permute-done.29 = bf16[32,4096]{1,0:T(8,128)(2,1)S(1)} collective-permute-done((bf16[32,4096]{1,0:T(8,128)(2,1)S(1)}, bf16[32,4096]{1,0:T(8,128)(2,1)S(1)}, u32[]{:S(2)}, u32[]{:S(2)}) %collective-permute-start.29) | collective-permute-done | bytes 262176 | tf_op jit(solution)/shard_map/ppermute | solution.py:33
  215.9 2.8 %collective-permute-done.36 = bf16[32,4096]{1,0:T(8,128)(2,1)S(1)} collective-permute-done((bf16[32,4096]{1,0:T(8,128)(2,1)S(1)}, bf16[32,4096]{1,0:T(8,128)(2,1)S(1)}, u32[]{:S(2)}, u32[]{:S(2)}) %collective-permute-start.36) | collective-permute-done | bytes 262176 | tf_op jit(solution)/shard_map/ppermute | solution.py:33
  218.8 2.0 collective-permute-start.37
  221.2 2.8 %collective-permute-done.30.refs_3_ = bf16[32,4096]{1,0:T(8,128)(2,1)S(1)} collective-permute-done((bf16[32,4096]{1,0:T(8,128)(2,1)S(1)}, bf16[32,4096]{1,0:T(8,128)(2,1)S(1)}, u32[]{:S(2)}, u32[]{:S(2)}) %collective-permute-start.30) | collective-permute-done | bytes 262176 | tf_op jit(solution)/shard_map/ppermute | solution.py:33
  (116 shorter events, 20.2 us)
Async XLA Ops:
  0.0 38.5 %copy-start.4 = (bf16[64,4096]{1,0:T(8,128)(2,1)S(1)}, bf16[64,4096]{1,0:T(8,128)(2,1)}, u32[]{:S(2)}) copy-start(bf16[64,4096]{1,0:T(8,128)(2,1)} %k_ref.5) | copy-start | bytes 1572868
  0.0 38.5 %copy-start.5 = (bf16[64,4096]{1,0:T(8,128)(2,1)S(1)}, bf16[64,4096]{1,0:T(8,128)(2,1)}, u32[]{:S(2)}) copy-start(bf16[64,4096]{1,0:T(8,128)(2,1)} %v_ref.5) | copy-start | bytes 1572868
  0.0 98.3 %copy-start.23 = (s32[64,2]{0,1:T(2,128)S(1)}, s32[64,2]{0,1:T(2,128)}, u32[]{:S(2)}) copy-start(s32[64,2]{0,1:T(2,128)} %param.15) | copy-start | bytes 1540
  0.0 98.3 %copy-start.24 = (s32[64,2]{0,1:T(2,128)S(1)}, s32[64,2]{0,1:T(2,128)}, u32[]{:S(2)}) copy-start(s32[64,2]{0,1:T(2,128)} %param.14) | copy-start | bytes 1540
  0.0 158.6 %collective-permute-start.19 = (bf16[4096,512]{1,0:T(8,128)(2,1)}, bf16[4096,512]{1,0:T(8,128)(2,1)}, u32[]{:S(2)}, u32[]{:S(2)}) collective-permute-start(bf16[4096,512]{1,0:T(8,128)(2,1)} %refs_4_.9), channel_id=1, source_target_pairs={{0,1},{1,0},{2,3},{3,2},{4,5},{5,4},{6,7},{7,6},{8,9},{9,8},{10,11... | collective-permute-start | bytes 12582920 | tf_op jit(solution)/shard_map/ppermute | solution.py:33
  0.6 158.1 %collective-permute-start.20 = (bf16[512,4096]{1,0:T(8,128)(2,1)}, bf16[512,4096]{1,0:T(8,128)(2,1)}, u32[]{:S(2)}, u32[]{:S(2)}) collective-permute-start(bf16[512,4096]{1,0:T(8,128)(2,1)} %refs_6_.5), channel_id=1, source_target_pairs={{0,1},{1,0},{2,3},{3,2},{4,5},{5,4},{6,7},{7,6},{8,9},{9,8},{10,11... | collective-permute-start | bytes 12582920 | tf_op jit(solution)/shard_map/ppermute | solution.py:33
  2.0 36.5 %collective-permute-start.2 = (bf16[2,64,1536]{2,1,0:T(8,128)(2,1)S(1)}, bf16[2,64,1536]{2,1,0:T(8,128)(2,1)S(1)}, u32[]{:S(2)}, u32[]{:S(2)}) collective-permute-start(bf16[2,64,1536]{2,1,0:T(8,128)(2,1)S(1)} %pad_maximum_fusion.1), channel_id=1, source_target_pairs={{12,4},{13,5},{14,6},{15,7},{0,8},{1,9},{2,10},{3,11},{4,12},{5,13... | collective-permute-start | bytes 1179656 | tf_op jit(solution)/shard_map/ppermute | solution.py:33
  6.1 45.9 %collective-permute-start.5 = (bf16[2,64,1536]{2,1,0:T(8,128)(2,1)S(1)}, bf16[2,64,1536]{2,1,0:T(8,128)(2,1)}, u32[]{:S(2)}, u32[]{:S(2)}) collective-permute-start(bf16[2,64,1536]{2,1,0:T(8,128)(2,1)S(1)} %pad_maximum_fusion.2), channel_id=1, source_target_pairs={{12,4},{13,5},{14,6},{15,7},{0,8},{1,9},{2,10},{3,11},{4,12},{5,13... | collective-permute-start | bytes 1179656 | tf_op jit(solution)/shard_map/ppermute | solution.py:33
  7.2 44.8 %collective-permute-start.8 = (bf16[2,64,1024]{2,1,0:T(8,128)(2,1)S(1)}, bf16[2,64,1024]{2,1,0:T(8,128)(2,1)}, u32[]{:S(2)}, u32[]{:S(2)}) collective-permute-start(bf16[2,64,1024]{2,1,0:T(8,128)(2,1)S(1)} %pad_maximum_fusion.3), channel_id=1, source_target_pairs={{12,4},{13,5},{14,6},{15,7},{0,8},{1,9},{2,10},{3,11},{4,12},{5,13... | collective-permute-start | bytes 786440 | tf_op jit(solution)/shard_map/ppermute | solution.py:33
  38.5 56.4 %copy-start.7 = (bf16[2,64,1536]{2,1,0:T(8,128)(2,1)}, bf16[2,64,1536]{2,1,0:T(8,128)(2,1)S(1)}, u32[]{:S(2)}) copy-start(bf16[2,64,1536]{2,1,0:T(8,128)(2,1)S(1)} %collective-permute-done.2.refs_2_) | copy-start | bytes 1179652
  38.5 17.1 %collective-permute-start.3 = (bf16[2,64,1536]{2,1,0:T(8,128)(2,1)S(1)}, bf16[2,64,1536]{2,1,0:T(8,128)(2,1)S(1)}, u32[]{:S(2)}, u32[]{:S(2)}) collective-permute-start(bf16[2,64,1536]{2,1,0:T(8,128)(2,1)S(1)} %collective-permute-done.2.refs_2_), channel_id=1, source_target_pairs={{0,1},{1,0},{2,3},{3,2},{4,5},{5,4},{6,7},{7,6},{8,9},{9,8},{10,11... | collective-permute-start | bytes 1179656 | tf_op jit(solution)/shard_map/ppermute | solution.py:33
  52.0 39.7 %collective-permute-start = (bf16[2,64,4096]{2,1,0:T(8,128)(2,1)S(1)}, bf16[2,64,4096]{2,1,0:T(8,128)(2,1)S(1)}, u32[]{:S(2)}, u32[]{:S(2)}) collective-permute-start(bf16[2,64,4096]{2,1,0:T(8,128)(2,1)S(1)} %pad_maximum_fusion), channel_id=1, source_target_pairs={{0,1},{1,0},{2,3},{3,2},{4,5},{5,4},{6,7},{7,6},{8,9},{9,8},{10,11... | collective-permute-start | bytes 3145736 | tf_op jit(solution)/shard_map/ppermute | solution.py:33
  52.0 42.9 %collective-permute-start.1 = (bf16[2,64,4096]{2,1,0:T(8,128)(2,1)S(1)}, bf16[2,64,4096]{2,1,0:T(8,128)(2,1)S(1)}, u32[]{:S(2)}, u32[]{:S(2)}) collective-permute-start(bf16[2,64,4096]{2,1,0:T(8,128)(2,1)S(1)} %pad_maximum_fusion), channel_id=1, source_target_pairs={{14,13},{13,14},{8,15},{7,0},{2,1},{1,2},{6,5},{5,6},{0,7},{15,8},... | collective-permute-start | bytes 3145736 | tf_op jit(solution)/shard_map/ppermute | solution.py:33
  56.4 17.0 %collective-permute-start.4 = (bf16[2,64,1536]{2,1,0:T(8,128)(2,1)S(1)}, bf16[2,64,1536]{2,1,0:T(8,128)(2,1)S(1)}, u32[]{:S(2)}, u32[]{:S(2)}) collective-permute-start(bf16[2,64,1536]{2,1,0:T(8,128)(2,1)S(1)} %collective-permute-done.2.refs_2_), channel_id=1, source_target_pairs={{14,13},{13,14},{8,15},{7,0},{2,1},{1,2},{6,5},{5,6},{0,7},{15,8},... | collective-permute-start | bytes 1179656 | tf_op jit(solution)/shard_map/ppermute | solution.py:33
  74.1 16.5 %collective-permute-start.6 = (bf16[2,64,1536]{2,1,0:T(8,128)(2,1)}, bf16[2,64,1536]{2,1,0:T(8,128)(2,1)S(1)}, u32[]{:S(2)}, u32[]{:S(2)}) collective-permute-start(bf16[2,64,1536]{2,1,0:T(8,128)(2,1)} %collective-permute-done.5.refs_2_), channel_id=1, source_target_pairs={{0,1},{1,0},{2,3},{3,2},{4,5},{5,4},{6,7},{7,6},{8,9},{9,8},{10,11... | collective-permute-start | bytes 1179656 | tf_op jit(solution)/shard_map/ppermute | solution.py:33
  91.4 16.5 %collective-permute-start.9 = (bf16[2,64,1024]{2,1,0:T(8,128)(2,1)}, bf16[2,64,1024]{2,1,0:T(8,128)(2,1)}, u32[]{:S(2)}, u32[]{:S(2)}) collective-permute-start(bf16[2,64,1024]{2,1,0:T(8,128)(2,1)} %collective-permute-done.8.refs_2_), channel_id=1, source_target_pairs={{0,1},{1,0},{2,3},{3,2},{4,5},{5,4},{6,7},{7,6},{8,9},{9,8},{10,11... | collective-permute-start | bytes 786440 | tf_op jit(solution)/shard_map/ppermute | solution.py:33
  91.8 16.1 %collective-permute-start.10 = (bf16[2,64,1024]{2,1,0:T(8,128)(2,1)}, bf16[2,64,1024]{2,1,0:T(8,128)(2,1)}, u32[]{:S(2)}, u32[]{:S(2)}) collective-permute-start(bf16[2,64,1024]{2,1,0:T(8,128)(2,1)} %collective-permute-done.8.refs_2_), channel_id=1, source_target_pairs={{14,13},{13,14},{8,15},{7,0},{2,1},{1,2},{6,5},{5,6},{0,7},{15,8},... | collective-permute-start | bytes 786440 | tf_op jit(solution)/shard_map/ppermute | solution.py:33
  94.9 10.3 %collective-permute-start.7 = (bf16[2,64,1536]{2,1,0:T(8,128)(2,1)}, bf16[2,64,1536]{2,1,0:T(8,128)(2,1)}, u32[]{:S(2)}, u32[]{:S(2)}) collective-permute-start(bf16[2,64,1536]{2,1,0:T(8,128)(2,1)} %collective-permute-done.5.refs_2_), channel_id=1, source_target_pairs={{14,13},{13,14},{8,15},{7,0},{2,1},{1,2},{6,5},{5,6},{0,7},{15,8},... | collective-permute-start | bytes 1179656 | tf_op jit(solution)/shard_map/ppermute | solution.py:33
  111.2 11.6 %collective-permute-start.11 = (bf16[32,4224]{1,0:T(8,128)(2,1)S(1)}, bf16[32,4224]{1,0:T(8,128)(2,1)S(1)}, u32[]{:S(2)}, u32[]{:S(2)}) collective-permute-start(bf16[32,4224]{1,0:T(8,128)(2,1)S(1)} %get-tuple-element.25.refs_2_), channel_id=1, source_target_pairs={{0,4},{1,5},{4,8},{5,9},{8,12},{9,13},{12,14},{13,15},{14,10},{15,... | collective-permute-start | bytes 811016 | tf_op jit(solution)/shard_map/ppermute | solution.py:33
  111.2 14.6 %collective-permute-start.15 = (bf16[32,4224]{1,0:T(8,128)(2,1)S(1)}, bf16[32,4224]{1,0:T(8,128)(2,1)S(1)}, u32[]{:S(2)}, u32[]{:S(2)}) collective-permute-start(bf16[32,4224]{1,0:T(8,128)(2,1)S(1)} %get-tuple-element.26.refs_3_), channel_id=1, source_target_pairs={{4,0},{5,1},{8,4},{9,5},{12,8},{13,9},{14,12},{15,13},{10,14},{11,... | collective-permute-start | bytes 811016 | tf_op jit(solution)/shard_map/ppermute | solution.py:33
  116.8 11.8 %collective-permute-start.22 = (bf16[32,4224]{1,0:T(8,128)(2,1)S(1)}, bf16[32,4224]{1,0:T(8,128)(2,1)S(1)}, u32[]{:S(2)}, u32[]{:S(2)}) collective-permute-start(bf16[32,4224]{1,0:T(8,128)(2,1)S(1)} %get-tuple-element.26.refs_3_), channel_id=1, source_target_pairs={{0,4},{1,5},{4,8},{5,9},{8,12},{9,13},{12,14},{13,15},{14,10},{15,... | collective-permute-start | bytes 811016 | tf_op jit(solution)/shard_map/ppermute | solution.py:33
  122.8 9.2 %collective-permute-start.25 = (bf16[32,4224]{1,0:T(8,128)(2,1)S(1)}, bf16[32,4224]{1,0:T(8,128)(2,1)S(1)}, u32[]{:S(2)}, u32[]{:S(2)}) collective-permute-start(bf16[32,4224]{1,0:T(8,128)(2,1)S(1)} %get-tuple-element.25.refs_2_), channel_id=1, source_target_pairs={{4,0},{5,1},{8,4},{9,5},{12,8},{13,9},{14,12},{15,13},{10,14},{11,... | collective-permute-start | bytes 811016 | tf_op jit(solution)/shard_map/ppermute | solution.py:33
  125.8 9.4 %collective-permute-start.12 = (bf16[32,4224]{1,0:T(8,128)(2,1)S(1)}, bf16[32,4224]{1,0:T(8,128)(2,1)S(1)}, u32[]{:S(2)}, u32[]{:S(2)}) collective-permute-start(bf16[32,4224]{1,0:T(8,128)(2,1)S(1)} %collective-permute-done.11.refs_0_), channel_id=1, source_target_pairs={{0,4},{1,5},{4,8},{5,9},{8,12},{9,13},{12,14},{13,15},{14,10},{15,... | collective-permute-start | bytes 811016 | tf_op jit(solution)/shard_map/ppermute | solution.py:33
  128.6 9.0 %collective-permute-start.16 = (bf16[32,4224]{1,0:T(8,128)(2,1)S(1)}, bf16[32,4224]{1,0:T(8,128)(2,1)S(1)}, u32[]{:S(2)}, u32[]{:S(2)}) collective-permute-start(bf16[32,4224]{1,0:T(8,128)(2,1)S(1)} %collective-permute-done.15.refs_1_), channel_id=1, source_target_pairs={{4,0},{5,1},{8,4},{9,5},{12,8},{13,9},{14,12},{15,13},{10,14},{11,... | collective-permute-start | bytes 811016 | tf_op jit(solution)/shard_map/ppermute | solution.py:33
  132.0 9.8 %collective-permute-start.23 = (bf16[32,4224]{1,0:T(8,128)(2,1)S(1)}, bf16[32,4224]{1,0:T(8,128)(2,1)S(1)}, u32[]{:S(2)}, u32[]{:S(2)}) collective-permute-start(bf16[32,4224]{1,0:T(8,128)(2,1)S(1)} %collective-permute-done.22.refs_2_), channel_id=1, source_target_pairs={{0,4},{1,5},{4,8},{5,9},{8,12},{9,13},{12,14},{13,15},{14,10},{15,... | collective-permute-start | bytes 811016 | tf_op jit(solution)/shard_map/ppermute | solution.py:33
  135.2 12.2 %collective-permute-start.13 = (bf16[32,4224]{1,0:T(8,128)(2,1)S(1)}, bf16[32,4224]{1,0:T(8,128)(2,1)S(1)}, u32[]{:S(2)}, u32[]{:S(2)}) collective-permute-start(bf16[32,4224]{1,0:T(8,128)(2,1)S(1)} %collective-permute-done.12.refs_0_), channel_id=1, source_target_pairs={{0,4},{1,5},{4,8},{5,9},{8,12},{9,13},{12,14},{13,15},{14,10},{15,... | collective-permute-start | bytes 811016 | tf_op jit(solution)/shard_map/ppermute | solution.py:33
  137.6 9.7 %collective-permute-start.17 = (bf16[32,4224]{1,0:T(8,128)(2,1)S(1)}, bf16[32,4224]{1,0:T(8,128)(2,1)S(1)}, u32[]{:S(2)}, u32[]{:S(2)}) collective-permute-start(bf16[32,4224]{1,0:T(8,128)(2,1)S(1)} %collective-permute-done.16.refs_1_), channel_id=1, source_target_pairs={{4,0},{5,1},{8,4},{9,5},{12,8},{13,9},{14,12},{15,13},{10,14},{11,... | collective-permute-start | bytes 811016 | tf_op jit(solution)/shard_map/ppermute | solution.py:33
  141.8 10.9 %collective-permute-start.26 = (bf16[32,4224]{1,0:T(8,128)(2,1)S(1)}, bf16[32,4224]{1,0:T(8,128)(2,1)S(1)}, u32[]{:S(2)}, u32[]{:S(2)}) collective-permute-start(bf16[32,4224]{1,0:T(8,128)(2,1)S(1)} %collective-permute-done.25.refs_3_), channel_id=1, source_target_pairs={{4,0},{5,1},{8,4},{9,5},{12,8},{13,9},{14,12},{15,13},{10,14},{11,... | collective-permute-start | bytes 811016 | tf_op jit(solution)/shard_map/ppermute | solution.py:33
  147.3 9.3 %collective-permute-start.14 = (bf16[32,4224]{1,0:T(8,128)(2,1)S(1)}, bf16[32,4224]{1,0:T(8,128)(2,1)S(1)}, u32[]{:S(2)}, u32[]{:S(2)}) collective-permute-start(bf16[32,4224]{1,0:T(8,128)(2,1)S(1)} %collective-permute-done.13.refs_0_), channel_id=1, source_target_pairs={{0,4},{1,5},{4,8},{5,9},{8,12},{9,13},{12,14},{13,15},{14,10},{15,... | collective-permute-start | bytes 811016 | tf_op jit(solution)/shard_map/ppermute | solution.py:33
  147.4 11.3 %collective-permute-start.18 = (bf16[32,4224]{1,0:T(8,128)(2,1)S(1)}, bf16[32,4224]{1,0:T(8,128)(2,1)}, u32[]{:S(2)}, u32[]{:S(2)}) collective-permute-start(bf16[32,4224]{1,0:T(8,128)(2,1)S(1)} %collective-permute-done.17.refs_1_), channel_id=1, source_target_pairs={{4,0},{5,1},{8,4},{9,5},{12,8},{13,9},{14,12},{15,13},{10,14},{11,... | collective-permute-start | bytes 811016 | tf_op jit(solution)/shard_map/ppermute | solution.py:33
  152.8 31.4 %collective-permute-start.24 = (bf16[32,4224]{1,0:T(8,128)(2,1)S(1)}, bf16[32,4224]{1,0:T(8,128)(2,1)S(1)}, u32[]{:S(2)}, u32[]{:S(2)}) collective-permute-start(bf16[32,4224]{1,0:T(8,128)(2,1)S(1)} %collective-permute-done.23.refs_2_), channel_id=1, source_target_pairs={{0,4},{1,5},{4,8},{5,9},{8,12},{9,13},{12,14},{13,15},{14,10},{15,... | collective-permute-start | bytes 811016 | tf_op jit(solution)/shard_map/ppermute | solution.py:33
  156.6 28.1 %collective-permute-start.27 = (bf16[32,4224]{1,0:T(8,128)(2,1)S(1)}, bf16[32,4224]{1,0:T(8,128)(2,1)S(1)}, u32[]{:S(2)}, u32[]{:S(2)}) collective-permute-start(bf16[32,4224]{1,0:T(8,128)(2,1)S(1)} %collective-permute-done.26.refs_3_), channel_id=1, source_target_pairs={{4,0},{5,1},{8,4},{9,5},{12,8},{13,9},{14,12},{15,13},{10,14},{11,... | collective-permute-start | bytes 811016 | tf_op jit(solution)/shard_map/ppermute | solution.py:33
  169.2 26.0 %collective-permute-start.21 = (bf16[32,4096]{1,0:T(8,128)(2,1)S(1)}, bf16[32,4096]{1,0:T(8,128)(2,1)S(1)}, u32[]{:S(2)}, u32[]{:S(2)}) collective-permute-start(bf16[32,4096]{1,0:T(8,128)(2,1)S(1)} %get-tuple-element.27), channel_id=1, source_target_pairs={{0,4},{1,5},{4,8},{5,9},{8,12},{9,13},{12,14},{13,15},{14,10},{15,... | collective-permute-start | bytes 786440 | tf_op jit(solution)/shard_map/ppermute | solution.py:33
  174.8 20.6 %collective-permute-start.31 = (bf16[32,4096]{1,0:T(8,128)(2,1)S(1)}, bf16[32,4096]{1,0:T(8,128)(2,1)S(1)}, u32[]{:S(2)}, u32[]{:S(2)}) collective-permute-start(bf16[32,4096]{1,0:T(8,128)(2,1)S(1)} %get-tuple-element.31), channel_id=1, source_target_pairs={{4,0},{5,1},{8,4},{9,5},{12,8},{13,9},{14,12},{15,13},{10,14},{11,... | collective-permute-start | bytes 786440 | tf_op jit(solution)/shard_map/ppermute | solution.py:33
  177.3 20.2 %collective-permute-start.34 = (bf16[32,4096]{1,0:T(8,128)(2,1)S(1)}, bf16[32,4096]{1,0:T(8,128)(2,1)S(1)}, u32[]{:S(2)}, u32[]{:S(2)}) collective-permute-start(bf16[32,4096]{1,0:T(8,128)(2,1)S(1)} %get-tuple-element.35), channel_id=1, source_target_pairs={{4,0},{5,1},{8,4},{9,5},{12,8},{13,9},{14,12},{15,13},{10,14},{11,... | collective-permute-start | bytes 786440 | tf_op jit(solution)/shard_map/ppermute | solution.py:33
  184.2 15.1 %collective-permute-start.38 = (bf16[32,4096]{1,0:T(8,128)(2,1)S(1)}, bf16[32,4096]{1,0:T(8,128)(2,1)S(1)}, u32[]{:S(2)}, u32[]{:S(2)}) collective-permute-start(bf16[32,4096]{1,0:T(8,128)(2,1)S(1)} %get-tuple-element.39), channel_id=1, source_target_pairs={{0,4},{1,5},{4,8},{5,9},{8,12},{9,13},{12,14},{13,15},{14,10},{15,... | collective-permute-start | bytes 786440 | tf_op jit(solution)/shard_map/ppermute | solution.py:33
  195.2 30.0 %copy-start.20 = (f32[3,4096]{1,0:T(4,128)S(1)}, f32[3,4096]{1,0:T(4,128)}, u32[]{:S(2)}) copy-start(f32[3,4096]{1,0:T(4,128)} %modulation_ref.1) | copy-start | bytes 147460
  195.2 30.0 %copy-start.22 = (bf16[64,1024]{1,0:T(8,128)(2,1)S(1)}, bf16[64,1024]{1,0:T(8,128)(2,1)}, u32[]{:S(2)}) copy-start(bf16[64,1024]{1,0:T(8,128)(2,1)} %copy-done.21) | copy-start | bytes 393220
  195.3 9.2 %collective-permute-start.28 = (bf16[32,4096]{1,0:T(8,128)(2,1)S(1)}, bf16[32,4096]{1,0:T(8,128)(2,1)S(1)}, u32[]{:S(2)}, u32[]{:S(2)}) collective-permute-start(bf16[32,4096]{1,0:T(8,128)(2,1)S(1)} %add_convert_fusion.9), channel_id=1, source_target_pairs={{0,4},{1,5},{4,8},{5,9},{8,12},{9,13},{12,14},{13,15},{14,10},{15,... | collective-permute-start | bytes 786440 | tf_op jit(solution)/shard_map/ppermute | solution.py:33
  195.5 9.2 %collective-permute-start.32 = (bf16[32,4096]{1,0:T(8,128)(2,1)S(1)}, bf16[32,4096]{1,0:T(8,128)(2,1)S(1)}, u32[]{:S(2)}, u32[]{:S(2)}) collective-permute-start(bf16[32,4096]{1,0:T(8,128)(2,1)S(1)} %add_convert_fusion.6), channel_id=1, source_target_pairs={{4,0},{5,1},{8,4},{9,5},{12,8},{13,9},{14,12},{15,13},{10,14},{11,... | collective-permute-start | bytes 786440 | tf_op jit(solution)/shard_map/ppermute | solution.py:33
  197.6 12.7 %collective-permute-start.35 = (bf16[32,4096]{1,0:T(8,128)(2,1)S(1)}, bf16[32,4096]{1,0:T(8,128)(2,1)S(1)}, u32[]{:S(2)}, u32[]{:S(2)}) collective-permute-start(bf16[32,4096]{1,0:T(8,128)(2,1)S(1)} %add_convert_fusion.4), channel_id=1, source_target_pairs={{4,0},{5,1},{8,4},{9,5},{12,8},{13,9},{14,12},{15,13},{10,14},{11,... | collective-permute-start | bytes 786440 | tf_op jit(solution)/shard_map/ppermute | solution.py:33
  199.4 13.0 %collective-permute-start.39 = (bf16[32,4096]{1,0:T(8,128)(2,1)S(1)}, bf16[32,4096]{1,0:T(8,128)(2,1)S(1)}, u32[]{:S(2)}, u32[]{:S(2)}) collective-permute-start(bf16[32,4096]{1,0:T(8,128)(2,1)S(1)} %add_convert_fusion.1), channel_id=1, source_target_pairs={{0,4},{1,5},{4,8},{5,9},{8,12},{9,13},{12,14},{13,15},{14,10},{15,... | collective-permute-start | bytes 786440 | tf_op jit(solution)/shard_map/ppermute | solution.py:33
  204.6 11.2 %collective-permute-start.29 = (bf16[32,4096]{1,0:T(8,128)(2,1)S(1)}, bf16[32,4096]{1,0:T(8,128)(2,1)S(1)}, u32[]{:S(2)}, u32[]{:S(2)}) collective-permute-start(bf16[32,4096]{1,0:T(8,128)(2,1)S(1)} %add_convert_fusion.8), channel_id=1, source_target_pairs={{0,4},{1,5},{4,8},{5,9},{8,12},{9,13},{12,14},{13,15},{14,10},{15,... | collective-permute-start | bytes 786440 | tf_op jit(solution)/shard_map/ppermute | solution.py:33
  204.8 16.1 %collective-permute-start.33 = (bf16[32,4096]{1,0:T(8,128)(2,1)S(1)}, bf16[32,4096]{1,0:T(8,128)(2,1)S(1)}, u32[]{:S(2)}, u32[]{:S(2)}) collective-permute-start(bf16[32,4096]{1,0:T(8,128)(2,1)S(1)} %add_convert_fusion.5), channel_id=1, source_target_pairs={{4,0},{5,1},{8,4},{9,5},{12,8},{13,9},{14,12},{15,13},{10,14},{11,... | collective-permute-start | bytes 786440 | tf_op jit(solution)/shard_map/ppermute | solution.py:33
  210.4 8.3 %collective-permute-start.36 = (bf16[32,4096]{1,0:T(8,128)(2,1)S(1)}, bf16[32,4096]{1,0:T(8,128)(2,1)S(1)}, u32[]{:S(2)}, u32[]{:S(2)}) collective-permute-start(bf16[32,4096]{1,0:T(8,128)(2,1)S(1)} %add_convert_fusion.3), channel_id=1, source_target_pairs={{4,0},{5,1},{8,4},{9,5},{12,8},{13,9},{14,12},{15,13},{10,14},{11,... | collective-permute-start | bytes 786440 | tf_op jit(solution)/shard_map/ppermute | solution.py:33
  212.5 8.7 %collective-permute-start.40 = (bf16[32,4096]{1,0:T(8,128)(2,1)S(1)}, bf16[32,4096]{1,0:T(8,128)(2,1)S(1)}, u32[]{:S(2)}, u32[]{:S(2)}) collective-permute-start(bf16[32,4096]{1,0:T(8,128)(2,1)S(1)} %add_convert_fusion), channel_id=1, source_target_pairs={{0,4},{1,5},{4,8},{5,9},{8,12},{9,13},{12,14},{13,15},{14,10},{15,... | collective-permute-start | bytes 786440 | tf_op jit(solution)/shard_map/ppermute | solution.py:33
  215.9 8.2 %collective-permute-start.30 = (bf16[32,4096]{1,0:T(8,128)(2,1)S(1)}, bf16[32,4096]{1,0:T(8,128)(2,1)S(1)}, u32[]{:S(2)}, u32[]{:S(2)}) collective-permute-start(bf16[32,4096]{1,0:T(8,128)(2,1)S(1)} %add_convert_fusion.7), channel_id=1, source_target_pairs={{0,4},{1,5},{4,8},{5,9},{8,12},{9,13},{12,14},{13,15},{14,10},{15,... | collective-permute-start | bytes 786440 | tf_op jit(solution)/shard_map/ppermute | solution.py:33
  218.8 6.4 %collective-permute-start.37 = (bf16[32,4096]{1,0:T(8,128)(2,1)S(1)}, bf16[32,4096]{1,0:T(8,128)(2,1)S(1)}, u32[]{:S(2)}, u32[]{:S(2)}) collective-permute-start(bf16[32,4096]{1,0:T(8,128)(2,1)S(1)} %add_convert_fusion.2), channel_id=1, source_target_pairs={{4,0},{5,1},{8,4},{9,5},{12,8},{13,9},{14,12},{15,13},{10,14},{11,... | collective-permute-start | bytes 786440 | tf_op jit(solution)/shard_map/ppermute | solution.py:33
  (18 other events, 51.9 us)

commit v5 on v4

--- a/solution.py
+++ b/solution.py
@@ -15,12 +15,12 @@
 CORES = 2
 EPSILON = 1e-06
 MASKED = -1e30
-HEADS = (12, 12, 8)
-HEAD_GROUP = 4
+HEADS = (8, 12, 12)
+HEAD_GROUP = 12
 HIDDEN_STEP = 512
 LANES = 128
 ATTEND_VMEM = 16 * 2**20
-EXPERT_VMEM = 26 * 2**20
+EXPERT_VMEM = 32 * 2**20
 
 TILE, GROUPS = "tile", "groups"
 LONG = "long"
@@ -344,14 +344,18 @@
     def share(keys):
         partial.update(zip(keys, run_experts([rows_of[k] for k in keys], weights, mine)))
 
-    for s in range(1, far + 1):
-        keys = [(UPPER, -s), (LOWER, s)]
-        if s == 1:
-            keys += [(UPPER, 0), (LOWER, 0)]
-        elif s < far:
-            keys += [(LOWER, -(s - 1)), (UPPER, s - 1)]
+    long = lambda s: [(UPPER, -s), (LOWER, s)]
+    short = lambda s: [(LOWER, -s), (UPPER, s)]
+    calls = [long(1) + [(UPPER, 0), (LOWER, 0)]]
+    for s in range(3, far, 2):
+        calls.append(long(s - 1) + long(s) + short(s - 2) + (short(s - 3) if s > 3 else []))
+    end = short(far - 1)
+    assigned = end + [key for keys in calls for key in keys]
+    calls.append([key for key in rows_of if key not in assigned])
+    if end:
+        calls.append(end)
+    for keys in calls:
         share(keys)
-    share([(LOWER, 1 - far), (UPPER, far - 1)])
 
     def reduce_chain(kind, half, sign, pairs):
         hops = far if kind == LONG else far - 1

time: 227 us -> 207 us (0.912)
  waiting for transfers between devices: 105 us -> 97.3 us
  Pallas kernels: 35.6 us -> 28.6 us
  starting transfers between devices: 68.9 us -> 62.5 us
    ppermute x41, waiting for transfers between devices: 105 us -> 97.3 us  [permute(): return lax.ppermute(x, TILE, pairs)]
    ppermute x41, starting transfers between devices: 68.9 us -> 62.5 us  [permute(): return lax.ppermute(x, TILE, pairs)]
    pallas_call x5 -> x4, Pallas kernels: 27.2 us -> 21.3 us  [run_experts(): pl.pallas_call(functools.partial(experts_kernel, count), out_shape=[jax.S...]
    unnamed x50 -> x48, local copies, waits for them, and re-layouts: 12.8 us -> 13.2 us
  transfers between devices with their start and end apart: 41 -> 41, of which waited for: 22 -> 21; matrix products, arithmetic and copies ran while one was open for 1% -> 2% of each run, Pallas kernels for 15% -> 13%
where the time goes in v5:
time: 207 us; the launch traced here: 206 us
  waiting for transfers between devices  97.3 us (47%)
  starting transfers between devices  62.5 us (30%)
  Pallas kernels  28.6 us (14%)
  local copies, waits for them, and re-layouts  15.6 us (8%)
    ppermute x41, waiting for transfers between devices, permute(): return lax.ppermute(x, TILE, pairs)  97.3 us
    ppermute x41, starting transfers between devices, permute(): return lax.ppermute(x, TILE, pairs)  62.5 us
    pallas_call x4, Pallas kernels, run_experts(): pl.pallas_call(functools.partial(experts_kernel, count), out_shape=[jax.S...  21.3 us
    unnamed x48, local copies, waits for them, and re-layouts  13.2 us
    pallas_call x3, Pallas kernels, attend_chunk(): pl.pallas_call(functools.partial(attention_kernel, start, part // HEAD_DI...  6.18 us
  transfers between devices with their start and end apart: 41, of which 21 were waited for; matrix products, arithmetic and copies ran while one was open for 2% of the time, Pallas kernels for 13%

profile of v5, /device:TPU:0, one launch (start us, length us, event | category | flops | bytes accessed | tf_op | source)
XLA Modules:
  0.0 206.2 jit_solution(13475000312658599107)
XLA Ops:
  0.7 1.3 slice_bitcast_fusion
  2.0 4.1 %collective-permute-start.5 = (bf16[2,64,1536]{2,1,0:T(8,128)(2,1)S(1)}, bf16[2,64,1536]{2,1,0:T(8,128)(2,1)}, u32[]{:S(2)}, u32[]{:S(2)}) collective-permute-start(bf16[2,64,1536]{2,1,0:T(8,128)(2,1)S(1)} %pad_maximum_fusion.1), channel_id=1, source_target_pairs={{12,4},{13,5},{14,6},{15,7},{0,8},{1,9},{2,10},{3,11},{4,12},{5,13... | collective-permute-start | bytes 1179656 | tf_op jit(solution)/shard_map/ppermute | solution.py:33
  7.2 3.0 %collective-permute-start.8 = (bf16[2,64,1536]{2,1,0:T(8,128)(2,1)S(1)}, bf16[2,64,1536]{2,1,0:T(8,128)(2,1)}, u32[]{:S(2)}, u32[]{:S(2)}) collective-permute-start(bf16[2,64,1536]{2,1,0:T(8,128)(2,1)S(1)} %pad_maximum_fusion.2), channel_id=1, source_target_pairs={{12,4},{13,5},{14,6},{15,7},{0,8},{1,9},{2,10},{3,11},{4,12},{5,13... | collective-permute-start | bytes 1179656 | tf_op jit(solution)/shard_map/ppermute | solution.py:33
  11.2 32.9 %collective-permute-done.2.refs_2_ = bf16[2,64,1024]{2,1,0:T(8,128)(2,1)S(1)} collective-permute-done((bf16[2,64,1024]{2,1,0:T(8,128)(2,1)S(1)}, bf16[2,64,1024]{2,1,0:T(8,128)(2,1)S(1)}, u32[]{:S(2)}, u32[]{:S(2)}) %collective-permute-start.2) | collective-permute-done | bytes 262176 | tf_op jit(solution)/shard_map/ppermute | solution.py:33
  44.1 3.2 %collective-permute-start.1 = (bf16[2,64,4096]{2,1,0:T(8,128)(2,1)}, bf16[2,64,4096]{2,1,0:T(8,128)(2,1)S(1)}, u32[]{:S(2)}, u32[]{:S(2)}) collective-permute-start(bf16[2,64,4096]{2,1,0:T(8,128)(2,1)} %pad_maximum_fusion), channel_id=1, source_target_pairs={{14,13},{13,14},{8,15},{7,0},{2,1},{1,2},{6,5},{5,6},{0,7},{15,8},... | collective-permute-start | bytes 3145736 | tf_op jit(solution)/shard_map/ppermute | solution.py:33
  47.3 4.7 %collective-permute-done.8.refs_2_ = bf16[2,64,1536]{2,1,0:T(8,128)(2,1)} collective-permute-done((bf16[2,64,1536]{2,1,0:T(8,128)(2,1)S(1)}, bf16[2,64,1536]{2,1,0:T(8,128)(2,1)}, u32[]{:S(2)}, u32[]{:S(2)}) %collective-permute-start.8) | collective-permute-done | bytes 393248 | tf_op jit(solution)/shard_map/ppermute | solution.py:33
  52.0 1.5 collective-permute-done.3.refs_3_
  54.3 3.2 %collective-permute-start.4 = (bf16[2,64,1024]{2,1,0:T(8,128)(2,1)S(1)}, bf16[2,64,1024]{2,1,0:T(8,128)(2,1)S(1)}, u32[]{:S(2)}, u32[]{:S(2)}) collective-permute-start(bf16[2,64,1024]{2,1,0:T(8,128)(2,1)S(1)} %collective-permute-done.2.refs_2_), channel_id=1, source_target_pairs={{14,13},{13,14},{8,15},{7,0},{2,1},{1,2},{6,5},{5,6},{0,7},{15,8},... | collective-permute-start | bytes 786440 | tf_op jit(solution)/shard_map/ppermute | solution.py:33
  58.2 8.9 %collective-permute-done.4.refs_4_ = bf16[2,64,1024]{2,1,0:T(8,128)(2,1)S(1)} collective-permute-done((bf16[2,64,1024]{2,1,0:T(8,128)(2,1)S(1)}, bf16[2,64,1024]{2,1,0:T(8,128)(2,1)S(1)}, u32[]{:S(2)}, u32[]{:S(2)}) %collective-permute-start.4) | collective-permute-done | bytes 262176 | tf_op jit(solution)/shard_map/ppermute | solution.py:33
  67.8 10.7 %collective-permute-start.6 = (bf16[2,64,1536]{2,1,0:T(8,128)(2,1)}, bf16[2,64,1536]{2,1,0:T(8,128)(2,1)S(1)}, u32[]{:S(2)}, u32[]{:S(2)}) collective-permute-start(bf16[2,64,1536]{2,1,0:T(8,128)(2,1)} %collective-permute-done.5.refs_2_), channel_id=1, source_target_pairs={{0,1},{1,0},{2,3},{3,2},{4,5},{5,4},{6,7},{7,6},{8,9},{9,8},{10,11... | collective-permute-start | bytes 1179656 | tf_op jit(solution)/shard_map/ppermute | solution.py:33
  78.5 1.6 collective-permute-done.6.refs_3_
  80.8 2.7 %collective-permute-start.7 = (bf16[2,64,1536]{2,1,0:T(8,128)(2,1)}, bf16[2,64,1536]{2,1,0:T(8,128)(2,1)}, u32[]{:S(2)}, u32[]{:S(2)}) collective-permute-start(bf16[2,64,1536]{2,1,0:T(8,128)(2,1)} %collective-permute-done.5.refs_2_), channel_id=1, source_target_pairs={{14,13},{13,14},{8,15},{7,0},{2,1},{1,2},{6,5},{5,6},{0,7},{15,8},... | collective-permute-start | bytes 1179656 | tf_op jit(solution)/shard_map/ppermute | solution.py:33
  83.5 3.8 %collective-permute-start.10 = (bf16[2,64,1536]{2,1,0:T(8,128)(2,1)}, bf16[2,64,1536]{2,1,0:T(8,128)(2,1)}, u32[]{:S(2)}, u32[]{:S(2)}) collective-permute-start(bf16[2,64,1536]{2,1,0:T(8,128)(2,1)} %collective-permute-done.8.refs_2_), channel_id=1, source_target_pairs={{14,13},{13,14},{8,15},{7,0},{2,1},{1,2},{6,5},{5,6},{0,7},{15,8},... | collective-permute-start | bytes 1179656 | tf_op jit(solution)/shard_map/ppermute | solution.py:33
  91.5 1.4 shard_map.82.refs_7_.refs_0_
  92.9 2.1 %shard_map.83.refs_8_.refs_1_ = bf16[64,1536]{1,0:T(8,128)(2,1)S(1)} custom-call(s32[6]{0:T(128)S(1)} %add_convert_fusion.10.flags_ref, bf16[64,4096]{1,0:T(8,128)(2,1)S(1)} %copy-done.6, bf16[64,4096]{1,0:T(8,128)(2,1)S(1)} %copy-done.4, bf16[64,4096]{1,0:T(8,128)(2,1)S(1)} %copy-done.5, bf16[2,64,4096]{2,1,0:T(8,128)(2,1)S(1)} %collective-permute-done.refs_0_, ...), custom_call_target="tpu_custom_call" | custom-call | flops 150994944 | bytes 2752512 | tf_op jit(solution)/shard_map/pallas_call | solution.py:143
  95.4 2.7 %shard_map.84 = (bf16[64,1536]{1,0:T(8,128)(2,1)S(1)}, bf16[32,4224]{1,0:T(8,128)(2,1)S(1)}, bf16[32,4224]{1,0:T(8,128)(2,1)S(1)}) custom-call(s32[6]{0:T(128)S(1)} %add_convert_fusion.10.flags_ref, bf16[64,4096]{1,0:T(8,128)(2,1)S(1)} %copy-done.6, bf16[64,4096]{1,0:T(8,128)(2,1)S(1)} %copy-done.4, bf16[64,4096]{1,0:T(8,128)(2,1)S(1)} %copy-done.5, ...), custom_call_target="tpu_custom_call" | custom-call | flops 150994944 | bytes 2752512 | tf_op jit(solution)/shard_map/pallas_call | solution.py:143
  98.8 7.5 %collective-permute-start.19 = (bf16[32,4224]{1,0:T(8,128)(2,1)S(1)}, bf16[32,4224]{1,0:T(8,128)(2,1)S(1)}, u32[]{:S(2)}, u32[]{:S(2)}) collective-permute-start(bf16[32,4224]{1,0:T(8,128)(2,1)S(1)} %get-tuple-element.25.refs_3_), channel_id=1, source_target_pairs={{4,0},{5,1},{8,4},{9,5},{12,8},{13,9},{14,12},{15,13},{10,14},{11,... | collective-permute-start | bytes 811016 | tf_op jit(solution)/shard_map/ppermute | solution.py:33
  107.0 5.1 %collective-permute-done.15.refs_0_ = bf16[32,4224]{1,0:T(8,128)(2,1)S(1)} collective-permute-done((bf16[32,4224]{1,0:T(8,128)(2,1)S(1)}, bf16[32,4224]{1,0:T(8,128)(2,1)S(1)}, u32[]{:S(2)}, u32[]{:S(2)}) %collective-permute-start.15) | collective-permute-done | bytes 270368 | tf_op jit(solution)/shard_map/ppermute | solution.py:33
  112.1 2.3 %collective-permute-start.13 = (bf16[32,4224]{1,0:T(8,128)(2,1)S(1)}, bf16[32,4224]{1,0:T(8,128)(2,1)S(1)}, u32[]{:S(2)}, u32[]{:S(2)}) collective-permute-start(bf16[32,4224]{1,0:T(8,128)(2,1)S(1)} %get-tuple-element.26.refs_2_), channel_id=1, source_target_pairs={{4,0},{5,1},{8,4},{9,5},{12,8},{13,9},{14,12},{15,13},{10,14},{11,... | collective-permute-start | bytes 811016 | tf_op jit(solution)/shard_map/ppermute | solution.py:33
  115.1 2.8 %collective-permute-done.11.refs_4_ = bf16[32,4224]{1,0:T(8,128)(2,1)S(1)} collective-permute-done((bf16[32,4224]{1,0:T(8,128)(2,1)S(1)}, bf16[32,4224]{1,0:T(8,128)(2,1)S(1)}, u32[]{:S(2)}, u32[]{:S(2)}) %collective-permute-start.11) | collective-permute-done | bytes 270368 | tf_op jit(solution)/shard_map/ppermute | solution.py:33
  118.7 2.4 %collective-permute-done.13.refs_5_ = bf16[32,4224]{1,0:T(8,128)(2,1)S(1)} collective-permute-done((bf16[32,4224]{1,0:T(8,128)(2,1)S(1)}, bf16[32,4224]{1,0:T(8,128)(2,1)S(1)}, u32[]{:S(2)}, u32[]{:S(2)}) %collective-permute-start.13) | collective-permute-done | bytes 270368 | tf_op jit(solution)/shard_map/ppermute | solution.py:33
  121.1 3.4 %collective-permute-done.16.refs_0_ = bf16[32,4224]{1,0:T(8,128)(2,1)S(1)} collective-permute-done((bf16[32,4224]{1,0:T(8,128)(2,1)S(1)}, bf16[32,4224]{1,0:T(8,128)(2,1)S(1)}, u32[]{:S(2)}, u32[]{:S(2)}) %collective-permute-start.16) | collective-permute-done | bytes 270368 | tf_op jit(solution)/shard_map/ppermute | solution.py:33
  124.5 2.4 %collective-permute-done.20.refs_1_ = bf16[32,4224]{1,0:T(8,128)(2,1)S(1)} collective-permute-done((bf16[32,4224]{1,0:T(8,128)(2,1)S(1)}, bf16[32,4224]{1,0:T(8,128)(2,1)S(1)}, u32[]{:S(2)}, u32[]{:S(2)}) %collective-permute-start.20) | collective-permute-done | bytes 270368 | tf_op jit(solution)/shard_map/ppermute | solution.py:33
  126.9 4.0 %collective-permute-done.12.refs_0_ = bf16[32,4224]{1,0:T(8,128)(2,1)S(1)} collective-permute-done((bf16[32,4224]{1,0:T(8,128)(2,1)S(1)}, bf16[32,4224]{1,0:T(8,128)(2,1)S(1)}, u32[]{:S(2)}, u32[]{:S(2)}) %collective-permute-start.12) | collective-permute-done | bytes 270368 | tf_op jit(solution)/shard_map/ppermute | solution.py:33
  130.9 1.5 collective-permute-start.21
  132.4 1.4 collective-permute-done.14.refs_1_
  133.8 2.9 %collective-permute-done.17.refs_2_ = bf16[32,4224]{1,0:T(8,128)(2,1)S(1)} collective-permute-done((bf16[32,4224]{1,0:T(8,128)(2,1)S(1)}, bf16[32,4224]{1,0:T(8,128)(2,1)S(1)}, u32[]{:S(2)}, u32[]{:S(2)}) %collective-permute-start.17) | collective-permute-done | bytes 270368 | tf_op jit(solution)/shard_map/ppermute | solution.py:33
  136.7 1.7 collective-permute-start.27
  138.4 1.3 collective-permute-done.21.refs_3_
  139.7 2.1 %collective-permute-start.22 = (bf16[32,4224]{1,0:T(8,128)(2,1)S(1)}, bf16[32,4224]{1,0:T(8,128)(2,1)S(1)}, u32[]{:S(2)}, u32[]{:S(2)}) collective-permute-start(bf16[32,4224]{1,0:T(8,128)(2,1)S(1)} %collective-permute-done.21.refs_3_), channel_id=1, source_target_pairs={{4,0},{5,1},{8,4},{9,5},{12,8},{13,9},{14,12},{15,13},{10,14},{11,... | collective-permute-start | bytes 811016 | tf_op jit(solution)/shard_map/ppermute | solution.py:33
  141.8 2.2 %copy-done = bf16[4096,512]{1,0:T(8,128)(2,1)S(1)} copy-done((bf16[4096,512]{1,0:T(8,128)(2,1)S(1)}, bf16[4096,512]{1,0:T(8,128)(2,1)}, u32[]{:S(2)}) %copy-start) | copy-done | bytes 4194328
  144.0 2.2 %copy-done.2 = bf16[512,4096]{1,0:T(8,128)(2,1)S(1)} copy-done((bf16[512,4096]{1,0:T(8,128)(2,1)S(1)}, bf16[512,4096]{1,0:T(8,128)(2,1)}, u32[]{:S(2)}) %copy-start.2) | copy-done | bytes 4194328
  146.2 5.7 %shard_map.87 = (bf16[32,4096]{1,0:T(8,128)(2,1)S(1)}, bf16[32,4096]{1,0:T(8,128)(2,1)S(1)}, bf16[32,4096]{1,0:T(8,128)(2,1)S(1)}, bf16[32,4096]{1,0:T(8,128)(2,...) custom-call(s32[1]{0:T(128)} %bitcast.9.mine_ref, ...), custom_call_target="tpu_custom_call" | custom-call | flops 3221225472 | bytes 16777216 | tf_op jit(solution)/shard_map/pallas_call | solution.py:213
  151.9 2.5 %collective-permute-start.38 = (bf16[32,4096]{1,0:T(8,128)(2,1)S(1)}, bf16[32,4096]{1,0:T(8,128)(2,1)S(1)}, u32[]{:S(2)}, u32[]{:S(2)}) collective-permute-start(bf16[32,4096]{1,0:T(8,128)(2,1)S(1)} %get-tuple-element.39), channel_id=1, source_target_pairs={{0,4},{1,5},{4,8},{5,9},{8,12},{9,13},{12,14},{13,15},{14,10},{15,... | collective-permute-start | bytes 786440 | tf_op jit(solution)/shard_map/ppermute | solution.py:33
  154.5 5.2 %shard_map.85 = (bf16[32,4096]{1,0:T(8,128)(2,1)S(1)}, bf16[32,4096]{1,0:T(8,128)(2,1)S(1)}, bf16[32,4096]{1,0:T(8,128)(2,1)S(1)}, bf16[32,4096]{1,0:T(8,128)(2,1)S(1)}) custom-call(s32[1]{0:T(128)} %bitcast.9.mine_ref, bf16[32,4224]{1,0:T(8,128)(2,1)S(1)} %collective-permute-done.12.refs_0_, bf16[32,4224]{1,0:T(8,128)(2,1)S(1)} %collective-permute-done.14.refs_1_, ...), custom_call_target="tpu_custom_call" | custom-call | flops 2147483648 | bytes 16777216 | tf_op jit(solution)/shard_map/pallas_call | solution.py:213
  159.7 1.6 collective-permute-start.31
  162.1 5.2 %shard_map.86 = (bf16[32,4096]{1,0:T(8,128)(2,1)S(1)}, bf16[32,4096]{1,0:T(8,128)(2,1)S(1)}) custom-call(s32[1]{0:T(128)} %bitcast.9.mine_ref, bf16[32,4224]{1,0:T(8,128)(2,1)S(1)} %collective-permute-done.26.refs_0_, bf16[32,4224]{1,0:T(8,128)(2,1)S(1)} %collective-permute-done.27.refs_1_, bf16[4096,512]{1,0:T(8,128)(2,1)S(1)} %copy-done.1, ...), custom_call_target="tpu_custom_call" | custom-call | flops 1073741824 | bytes 16777216 | tf_op jit(solution)/shard_map/pallas_call | solution.py:213
  167.3 5.2 %shard_map.88 = (bf16[32,4096]{1,0:T(8,128)(2,1)S(1)}, bf16[32,4096]{1,0:T(8,128)(2,1)S(1)}, bf16[32,4096]{1,0:T(8,128)(2,1)S(1)}, bf16[32,4096]{1,0:T(8,128)(2,1)S(1)}) custom-call(s32[1]{0:T(128)} %bitcast.9.mine_ref, bf16[32,4224]{1,0:T(8,128)(2,1)S(1)} %collective-permute-done.15.refs_0_, bf16[32,4224]{1,0:T(8,128)(2,1)S(1)} %collective-permute-done.19.refs_1_, ...), custom_call_target="tpu_custom_call" | custom-call | flops 2147483648 | bytes 16777216 | tf_op jit(solution)/shard_map/pallas_call | solution.py:213
  172.6 2.1 %collective-permute-start.39 = (bf16[32,4096]{1,0:T(8,128)(2,1)S(1)}, bf16[32,4096]{1,0:T(8,128)(2,1)S(1)}, u32[]{:S(2)}, u32[]{:S(2)}) collective-permute-start(bf16[32,4096]{1,0:T(8,128)(2,1)S(1)} %add_convert_fusion.1), channel_id=1, source_target_pairs={{0,4},{1,5},{4,8},{5,9},{8,12},{9,13},{12,14},{13,15},{14,10},{15,... | collective-permute-start | bytes 786440 | tf_op jit(solution)/shard_map/ppermute | solution.py:33
  174.9 1.5 collective-permute-start.32
  177.1 4.7 %collective-permute-done.39 = bf16[32,4096]{1,0:T(8,128)(2,1)S(1)} collective-permute-done((bf16[32,4096]{1,0:T(8,128)(2,1)S(1)}, bf16[32,4096]{1,0:T(8,128)(2,1)S(1)}, u32[]{:S(2)}, u32[]{:S(2)}) %collective-permute-start.39) | collective-permute-done | bytes 262176 | tf_op jit(solution)/shard_map/ppermute | solution.py:33
  181.9 2.1 %collective-permute-start.40 = (bf16[32,4096]{1,0:T(8,128)(2,1)S(1)}, bf16[32,4096]{1,0:T(8,128)(2,1)S(1)}, u32[]{:S(2)}, u32[]{:S(2)}) collective-permute-start(bf16[32,4096]{1,0:T(8,128)(2,1)S(1)} %add_convert_fusion), channel_id=1, source_target_pairs={{0,4},{1,5},{4,8},{5,9},{8,12},{9,13},{12,14},{13,15},{14,10},{15,... | collective-permute-start | bytes 786440 | tf_op jit(solution)/shard_map/ppermute | solution.py:33
  184.1 5.5 %collective-permute-done.32 = bf16[32,4096]{1,0:T(8,128)(2,1)S(1)} collective-permute-done((bf16[32,4096]{1,0:T(8,128)(2,1)S(1)}, bf16[32,4096]{1,0:T(8,128)(2,1)S(1)}, u32[]{:S(2)}, u32[]{:S(2)}) %collective-permute-start.32) | collective-permute-done | bytes 262176 | tf_op jit(solution)/shard_map/ppermute | solution.py:33
  189.8 2.1 collective-permute-start.29
  191.9 2.9 %collective-permute-done.36 = bf16[32,4096]{1,0:T(8,128)(2,1)S(1)} collective-permute-done((bf16[32,4096]{1,0:T(8,128)(2,1)S(1)}, bf16[32,4096]{1,0:T(8,128)(2,1)S(1)}, u32[]{:S(2)}, u32[]{:S(2)}) %collective-permute-start.36) | collective-permute-done | bytes 262176 | tf_op jit(solution)/shard_map/ppermute | solution.py:33
  195.3 3.3 %collective-permute-done.29 = bf16[32,4096]{1,0:T(8,128)(2,1)S(1)} collective-permute-done((bf16[32,4096]{1,0:T(8,128)(2,1)S(1)}, bf16[32,4096]{1,0:T(8,128)(2,1)S(1)}, u32[]{:S(2)}, u32[]{:S(2)}) %collective-permute-start.29) | collective-permute-done | bytes 262176 | tf_op jit(solution)/shard_map/ppermute | solution.py:33
  199.8 1.4 collective-permute-done.37.refs_6_
  201.2 3.9 %collective-permute-done.30.refs_3_ = bf16[32,4096]{1,0:T(8,128)(2,1)S(1)} collective-permute-done((bf16[32,4096]{1,0:T(8,128)(2,1)S(1)}, bf16[32,4096]{1,0:T(8,128)(2,1)S(1)}, u32[]{:S(2)}, u32[]{:S(2)}) %collective-permute-start.30) | collective-permute-done | bytes 262176 | tf_op jit(solution)/shard_map/ppermute | solution.py:33
  (113 shorter events, 18.3 us)
Async XLA Ops:
  0.0 10.2 %copy-start.5 = (bf16[64,4096]{1,0:T(8,128)(2,1)S(1)}, bf16[64,4096]{1,0:T(8,128)(2,1)}, u32[]{:S(2)}) copy-start(bf16[64,4096]{1,0:T(8,128)(2,1)} %v_ref.5) | copy-start | bytes 1572868
  0.0 10.2 %copy-start.4 = (bf16[64,4096]{1,0:T(8,128)(2,1)S(1)}, bf16[64,4096]{1,0:T(8,128)(2,1)}, u32[]{:S(2)}) copy-start(bf16[64,4096]{1,0:T(8,128)(2,1)} %k_ref.5) | copy-start | bytes 1572868
  0.0 78.5 %copy-start.23 = (s32[64,2]{0,1:T(2,128)S(1)}, s32[64,2]{0,1:T(2,128)}, u32[]{:S(2)}) copy-start(s32[64,2]{0,1:T(2,128)} %param.14) | copy-start | bytes 1540
  0.0 87.4 %copy-start.22 = (s32[64,2]{0,1:T(2,128)S(1)}, s32[64,2]{0,1:T(2,128)}, u32[]{:S(2)}) copy-start(s32[64,2]{0,1:T(2,128)} %param.15) | copy-start | bytes 1540
  0.0 139.7 %collective-permute-start.23 = (bf16[4096,512]{1,0:T(8,128)(2,1)}, bf16[4096,512]{1,0:T(8,128)(2,1)}, u32[]{:S(2)}, u32[]{:S(2)}) collective-permute-start(bf16[4096,512]{1,0:T(8,128)(2,1)} %refs_4_.5), channel_id=1, source_target_pairs={{0,1},{1,0},{2,3},{3,2},{4,5},{5,4},{6,7},{7,6},{8,9},{9,8},{10,11... | collective-permute-start | bytes 12582920 | tf_op jit(solution)/shard_map/ppermute | solution.py:33
  0.6 141.2 %collective-permute-start.24 = (bf16[512,4096]{1,0:T(8,128)(2,1)}, bf16[512,4096]{1,0:T(8,128)(2,1)}, u32[]{:S(2)}, u32[]{:S(2)}) collective-permute-start(bf16[512,4096]{1,0:T(8,128)(2,1)} %refs_6_.5), channel_id=1, source_target_pairs={{0,1},{1,0},{2,3},{3,2},{4,5},{5,4},{6,7},{7,6},{8,9},{9,8},{10,11... | collective-permute-start | bytes 12582920 | tf_op jit(solution)/shard_map/ppermute | solution.py:33
  2.0 42.1 %collective-permute-start.5 = (bf16[2,64,1536]{2,1,0:T(8,128)(2,1)S(1)}, bf16[2,64,1536]{2,1,0:T(8,128)(2,1)}, u32[]{:S(2)}, u32[]{:S(2)}) collective-permute-start(bf16[2,64,1536]{2,1,0:T(8,128)(2,1)S(1)} %pad_maximum_fusion.1), channel_id=1, source_target_pairs={{12,4},{13,5},{14,6},{15,7},{0,8},{1,9},{2,10},{3,11},{4,12},{5,13... | collective-permute-start | bytes 1179656 | tf_op jit(solution)/shard_map/ppermute | solution.py:33
  7.1 37.0 %collective-permute-start.2 = (bf16[2,64,1024]{2,1,0:T(8,128)(2,1)S(1)}, bf16[2,64,1024]{2,1,0:T(8,128)(2,1)S(1)}, u32[]{:S(2)}, u32[]{:S(2)}) collective-permute-start(bf16[2,64,1024]{2,1,0:T(8,128)(2,1)S(1)} %pad_maximum_fusion.3), channel_id=1, source_target_pairs={{12,4},{13,5},{14,6},{15,7},{0,8},{1,9},{2,10},{3,11},{4,12},{5,13... | collective-permute-start | bytes 786440 | tf_op jit(solution)/shard_map/ppermute | solution.py:33
  7.2 44.8 %collective-permute-start.8 = (bf16[2,64,1536]{2,1,0:T(8,128)(2,1)S(1)}, bf16[2,64,1536]{2,1,0:T(8,128)(2,1)}, u32[]{:S(2)}, u32[]{:S(2)}) collective-permute-start(bf16[2,64,1536]{2,1,0:T(8,128)(2,1)S(1)} %pad_maximum_fusion.2), channel_id=1, source_target_pairs={{12,4},{13,5},{14,6},{15,7},{0,8},{1,9},{2,10},{3,11},{4,12},{5,13... | collective-permute-start | bytes 1179656 | tf_op jit(solution)/shard_map/ppermute | solution.py:33
  44.1 39.4 %collective-permute-start = (bf16[2,64,4096]{2,1,0:T(8,128)(2,1)}, bf16[2,64,4096]{2,1,0:T(8,128)(2,1)S(1)}, u32[]{:S(2)}, u32[]{:S(2)}) collective-permute-start(bf16[2,64,4096]{2,1,0:T(8,128)(2,1)} %pad_maximum_fusion), channel_id=1, source_target_pairs={{0,1},{1,0},{2,3},{3,2},{4,5},{5,4},{6,7},{7,6},{8,9},{9,8},{10,11... | collective-permute-start | bytes 3145736 | tf_op jit(solution)/shard_map/ppermute | solution.py:33
  44.1 43.2 %collective-permute-start.1 = (bf16[2,64,4096]{2,1,0:T(8,128)(2,1)}, bf16[2,64,4096]{2,1,0:T(8,128)(2,1)S(1)}, u32[]{:S(2)}, u32[]{:S(2)}) collective-permute-start(bf16[2,64,4096]{2,1,0:T(8,128)(2,1)} %pad_maximum_fusion), channel_id=1, source_target_pairs={{14,13},{13,14},{8,15},{7,0},{2,1},{1,2},{6,5},{5,6},{0,7},{15,8},... | collective-permute-start | bytes 3145736 | tf_op jit(solution)/shard_map/ppermute | solution.py:33
  52.0 1.5 collective-permute-start.3
  54.3 12.8 %collective-permute-start.4 = (bf16[2,64,1024]{2,1,0:T(8,128)(2,1)S(1)}, bf16[2,64,1024]{2,1,0:T(8,128)(2,1)S(1)}, u32[]{:S(2)}, u32[]{:S(2)}) collective-permute-start(bf16[2,64,1024]{2,1,0:T(8,128)(2,1)S(1)} %collective-permute-done.2.refs_2_), channel_id=1, source_target_pairs={{14,13},{13,14},{8,15},{7,0},{2,1},{1,2},{6,5},{5,6},{0,7},{15,8},... | collective-permute-start | bytes 786440 | tf_op jit(solution)/shard_map/ppermute | solution.py:33
  67.8 12.3 %collective-permute-start.6 = (bf16[2,64,1536]{2,1,0:T(8,128)(2,1)}, bf16[2,64,1536]{2,1,0:T(8,128)(2,1)S(1)}, u32[]{:S(2)}, u32[]{:S(2)}) collective-permute-start(bf16[2,64,1536]{2,1,0:T(8,128)(2,1)} %collective-permute-done.5.refs_2_), channel_id=1, source_target_pairs={{0,1},{1,0},{2,3},{3,2},{4,5},{5,4},{6,7},{7,6},{8,9},{9,8},{10,11... | collective-permute-start | bytes 1179656 | tf_op jit(solution)/shard_map/ppermute | solution.py:33
  80.8 12.1 %collective-permute-start.7 = (bf16[2,64,1536]{2,1,0:T(8,128)(2,1)}, bf16[2,64,1536]{2,1,0:T(8,128)(2,1)}, u32[]{:S(2)}, u32[]{:S(2)}) collective-permute-start(bf16[2,64,1536]{2,1,0:T(8,128)(2,1)} %collective-permute-done.5.refs_2_), channel_id=1, source_target_pairs={{14,13},{13,14},{8,15},{7,0},{2,1},{1,2},{6,5},{5,6},{0,7},{15,8},... | collective-permute-start | bytes 1179656 | tf_op jit(solution)/shard_map/ppermute | solution.py:33
  83.5 11.9 %collective-permute-start.10 = (bf16[2,64,1536]{2,1,0:T(8,128)(2,1)}, bf16[2,64,1536]{2,1,0:T(8,128)(2,1)}, u32[]{:S(2)}, u32[]{:S(2)}) collective-permute-start(bf16[2,64,1536]{2,1,0:T(8,128)(2,1)} %collective-permute-done.8.refs_2_), channel_id=1, source_target_pairs={{14,13},{13,14},{8,15},{7,0},{2,1},{1,2},{6,5},{5,6},{0,7},{15,8},... | collective-permute-start | bytes 1179656 | tf_op jit(solution)/shard_map/ppermute | solution.py:33
  87.3 8.1 %collective-permute-start.9 = (bf16[2,64,1536]{2,1,0:T(8,128)(2,1)}, bf16[2,64,1536]{2,1,0:T(8,128)(2,1)}, u32[]{:S(2)}, u32[]{:S(2)}) collective-permute-start(bf16[2,64,1536]{2,1,0:T(8,128)(2,1)} %collective-permute-done.8.refs_2_), channel_id=1, source_target_pairs={{0,1},{1,0},{2,3},{3,2},{4,5},{5,4},{6,7},{7,6},{8,9},{9,8},{10,11... | collective-permute-start | bytes 1179656 | tf_op jit(solution)/shard_map/ppermute | solution.py:33
  98.8 13.3 %collective-permute-start.15 = (bf16[32,4224]{1,0:T(8,128)(2,1)S(1)}, bf16[32,4224]{1,0:T(8,128)(2,1)S(1)}, u32[]{:S(2)}, u32[]{:S(2)}) collective-permute-start(bf16[32,4224]{1,0:T(8,128)(2,1)S(1)} %get-tuple-element.26.refs_2_), channel_id=1, source_target_pairs={{0,4},{1,5},{4,8},{5,9},{8,12},{9,13},{12,14},{13,15},{14,10},{15,... | collective-permute-start | bytes 811016 | tf_op jit(solution)/shard_map/ppermute | solution.py:33
  98.8 16.3 %collective-permute-start.19 = (bf16[32,4224]{1,0:T(8,128)(2,1)S(1)}, bf16[32,4224]{1,0:T(8,128)(2,1)S(1)}, u32[]{:S(2)}, u32[]{:S(2)}) collective-permute-start(bf16[32,4224]{1,0:T(8,128)(2,1)S(1)} %get-tuple-element.25.refs_3_), channel_id=1, source_target_pairs={{4,0},{5,1},{8,4},{9,5},{12,8},{13,9},{14,12},{15,13},{10,14},{11,... | collective-permute-start | bytes 811016 | tf_op jit(solution)/shard_map/ppermute | solution.py:33
  106.3 11.6 %collective-permute-start.11 = (bf16[32,4224]{1,0:T(8,128)(2,1)S(1)}, bf16[32,4224]{1,0:T(8,128)(2,1)S(1)}, u32[]{:S(2)}, u32[]{:S(2)}) collective-permute-start(bf16[32,4224]{1,0:T(8,128)(2,1)S(1)} %get-tuple-element.25.refs_3_), channel_id=1, source_target_pairs={{0,4},{1,5},{4,8},{5,9},{8,12},{9,13},{12,14},{13,15},{14,10},{15,... | collective-permute-start | bytes 811016 | tf_op jit(solution)/shard_map/ppermute | solution.py:33
  112.1 9.0 %collective-permute-start.13 = (bf16[32,4224]{1,0:T(8,128)(2,1)S(1)}, bf16[32,4224]{1,0:T(8,128)(2,1)S(1)}, u32[]{:S(2)}, u32[]{:S(2)}) collective-permute-start(bf16[32,4224]{1,0:T(8,128)(2,1)S(1)} %get-tuple-element.26.refs_2_), channel_id=1, source_target_pairs={{4,0},{5,1},{8,4},{9,5},{12,8},{13,9},{14,12},{15,13},{10,14},{11,... | collective-permute-start | bytes 811016 | tf_op jit(solution)/shard_map/ppermute | solution.py:33
  115.1 9.4 %collective-permute-start.16 = (bf16[32,4224]{1,0:T(8,128)(2,1)S(1)}, bf16[32,4224]{1,0:T(8,128)(2,1)S(1)}, u32[]{:S(2)}, u32[]{:S(2)}) collective-permute-start(bf16[32,4224]{1,0:T(8,128)(2,1)S(1)} %collective-permute-done.15.refs_0_), channel_id=1, source_target_pairs={{0,4},{1,5},{4,8},{5,9},{8,12},{9,13},{12,14},{13,15},{14,10},{15,... | collective-permute-start | bytes 811016 | tf_op jit(solution)/shard_map/ppermute | solution.py:33
  117.9 9.0 %collective-permute-start.20 = (bf16[32,4224]{1,0:T(8,128)(2,1)S(1)}, bf16[32,4224]{1,0:T(8,128)(2,1)S(1)}, u32[]{:S(2)}, u32[]{:S(2)}) collective-permute-start(bf16[32,4224]{1,0:T(8,128)(2,1)S(1)} %collective-permute-done.19.refs_1_), channel_id=1, source_target_pairs={{4,0},{5,1},{8,4},{9,5},{12,8},{13,9},{14,12},{15,13},{10,14},{11,... | collective-permute-start | bytes 811016 | tf_op jit(solution)/shard_map/ppermute | solution.py:33
  121.1 9.8 %collective-permute-start.12 = (bf16[32,4224]{1,0:T(8,128)(2,1)S(1)}, bf16[32,4224]{1,0:T(8,128)(2,1)S(1)}, u32[]{:S(2)}, u32[]{:S(2)}) collective-permute-start(bf16[32,4224]{1,0:T(8,128)(2,1)S(1)} %collective-permute-done.11.refs_4_), channel_id=1, source_target_pairs={{0,4},{1,5},{4,8},{5,9},{8,12},{9,13},{12,14},{13,15},{14,10},{15,... | collective-permute-start | bytes 811016 | tf_op jit(solution)/shard_map/ppermute | solution.py:33
  124.4 9.3 %collective-permute-start.14 = (bf16[32,4224]{1,0:T(8,128)(2,1)S(1)}, bf16[32,4224]{1,0:T(8,128)(2,1)S(1)}, u32[]{:S(2)}, u32[]{:S(2)}) collective-permute-start(bf16[32,4224]{1,0:T(8,128)(2,1)S(1)} %collective-permute-done.13.refs_5_), channel_id=1, source_target_pairs={{4,0},{5,1},{8,4},{9,5},{12,8},{13,9},{14,12},{15,13},{10,14},{11,... | collective-permute-start | bytes 811016 | tf_op jit(solution)/shard_map/ppermute | solution.py:33
  126.9 9.8 %collective-permute-start.17 = (bf16[32,4224]{1,0:T(8,128)(2,1)S(1)}, bf16[32,4224]{1,0:T(8,128)(2,1)S(1)}, u32[]{:S(2)}, u32[]{:S(2)}) collective-permute-start(bf16[32,4224]{1,0:T(8,128)(2,1)S(1)} %collective-permute-done.16.refs_0_), channel_id=1, source_target_pairs={{0,4},{1,5},{4,8},{5,9},{8,12},{9,13},{12,14},{13,15},{14,10},{15,... | collective-permute-start | bytes 811016 | tf_op jit(solution)/shard_map/ppermute | solution.py:33
  130.9 8.8 %collective-permute-start.21 = (bf16[32,4224]{1,0:T(8,128)(2,1)S(1)}, bf16[32,4224]{1,0:T(8,128)(2,1)S(1)}, u32[]{:S(2)}, u32[]{:S(2)}) collective-permute-start(bf16[32,4224]{1,0:T(8,128)(2,1)S(1)} %collective-permute-done.20.refs_1_), channel_id=1, source_target_pairs={{4,0},{5,1},{8,4},{9,5},{12,8},{13,9},{14,12},{15,13},{10,14},{11,... | collective-permute-start | bytes 811016 | tf_op jit(solution)/shard_map/ppermute | solution.py:33
  133.8 27.5 %collective-permute-start.26 = (bf16[32,4224]{1,0:T(8,128)(2,1)S(1)}, bf16[32,4224]{1,0:T(8,128)(2,1)S(1)}, u32[]{:S(2)}, u32[]{:S(2)}) collective-permute-start(bf16[32,4224]{1,0:T(8,128)(2,1)S(1)} %collective-permute-done.12.refs_0_), channel_id=1, source_target_pairs={{0,4},{1,5},{4,8},{5,9},{8,12},{9,13},{12,14},{13,15},{14,10},{15,... | collective-permute-start | bytes 811016 | tf_op jit(solution)/shard_map/ppermute | solution.py:33
  136.7 25.4 %collective-permute-start.27 = (bf16[32,4224]{1,0:T(8,128)(2,1)S(1)}, bf16[32,4224]{1,0:T(8,128)(2,1)S(1)}, u32[]{:S(2)}, u32[]{:S(2)}) collective-permute-start(bf16[32,4224]{1,0:T(8,128)(2,1)S(1)} %collective-permute-done.14.refs_1_), channel_id=1, source_target_pairs={{4,0},{5,1},{8,4},{9,5},{12,8},{13,9},{14,12},{15,13},{10,14},{11,... | collective-permute-start | bytes 811016 | tf_op jit(solution)/shard_map/ppermute | solution.py:33
  139.7 14.8 %collective-permute-start.18 = (bf16[32,4224]{1,0:T(8,128)(2,1)S(1)}, bf16[32,4224]{1,0:T(8,128)(2,1)S(1)}, u32[]{:S(2)}, u32[]{:S(2)}) collective-permute-start(bf16[32,4224]{1,0:T(8,128)(2,1)S(1)} %collective-permute-done.17.refs_2_), channel_id=1, source_target_pairs={{0,4},{1,5},{4,8},{5,9},{8,12},{9,13},{12,14},{13,15},{14,10},{15,... | collective-permute-start | bytes 811016 | tf_op jit(solution)/shard_map/ppermute | solution.py:33
  139.7 14.8 %collective-permute-start.22 = (bf16[32,4224]{1,0:T(8,128)(2,1)S(1)}, bf16[32,4224]{1,0:T(8,128)(2,1)S(1)}, u32[]{:S(2)}, u32[]{:S(2)}) collective-permute-start(bf16[32,4224]{1,0:T(8,128)(2,1)S(1)} %collective-permute-done.21.refs_3_), channel_id=1, source_target_pairs={{4,0},{5,1},{8,4},{9,5},{12,8},{13,9},{14,12},{15,13},{10,14},{11,... | collective-permute-start | bytes 811016 | tf_op jit(solution)/shard_map/ppermute | solution.py:33
  146.2 8.3 %copy-start.1 = (bf16[4096,512]{1,0:T(8,128)(2,1)S(1)}, bf16[4096,512]{1,0:T(8,128)(2,1)}, u32[]{:S(2)}) copy-start(bf16[4096,512]{1,0:T(8,128)(2,1)} %refs_4_.5) | copy-start | bytes 12582916
  146.2 8.3 %copy-start.3 = (bf16[512,4096]{1,0:T(8,128)(2,1)S(1)}, bf16[512,4096]{1,0:T(8,128)(2,1)}, u32[]{:S(2)}) copy-start(bf16[512,4096]{1,0:T(8,128)(2,1)} %refs_6_.5) | copy-start | bytes 12582916
  151.9 20.6 %collective-permute-start.38 = (bf16[32,4096]{1,0:T(8,128)(2,1)S(1)}, bf16[32,4096]{1,0:T(8,128)(2,1)S(1)}, u32[]{:S(2)}, u32[]{:S(2)}) collective-permute-start(bf16[32,4096]{1,0:T(8,128)(2,1)S(1)} %get-tuple-element.39), channel_id=1, source_target_pairs={{0,4},{1,5},{4,8},{5,9},{8,12},{9,13},{12,14},{13,15},{14,10},{15,... | collective-permute-start | bytes 786440 | tf_op jit(solution)/shard_map/ppermute | solution.py:33
  159.6 15.0 %collective-permute-start.34 = (bf16[32,4096]{1,0:T(8,128)(2,1)S(1)}, bf16[32,4096]{1,0:T(8,128)(2,1)S(1)}, u32[]{:S(2)}, u32[]{:S(2)}) collective-permute-start(bf16[32,4096]{1,0:T(8,128)(2,1)S(1)} %get-tuple-element.35), channel_id=1, source_target_pairs={{4,0},{5,1},{8,4},{9,5},{12,8},{13,9},{14,12},{15,13},{10,14},{11,... | collective-permute-start | bytes 786440 | tf_op jit(solution)/shard_map/ppermute | solution.py:33
  159.7 15.1 %collective-permute-start.31 = (bf16[32,4096]{1,0:T(8,128)(2,1)S(1)}, bf16[32,4096]{1,0:T(8,128)(2,1)S(1)}, u32[]{:S(2)}, u32[]{:S(2)}) collective-permute-start(bf16[32,4096]{1,0:T(8,128)(2,1)S(1)} %get-tuple-element.31), channel_id=1, source_target_pairs={{4,0},{5,1},{8,4},{9,5},{12,8},{13,9},{14,12},{15,13},{10,14},{11,... | collective-permute-start | bytes 786440 | tf_op jit(solution)/shard_map/ppermute | solution.py:33
  161.3 15.1 %collective-permute-start.25 = (bf16[32,4096]{1,0:T(8,128)(2,1)S(1)}, bf16[32,4096]{1,0:T(8,128)(2,1)S(1)}, u32[]{:S(2)}, u32[]{:S(2)}) collective-permute-start(bf16[32,4096]{1,0:T(8,128)(2,1)S(1)} %get-tuple-element.27), channel_id=1, source_target_pairs={{0,4},{1,5},{4,8},{5,9},{8,12},{9,13},{12,14},{13,15},{14,10},{15,... | collective-permute-start | bytes 786440 | tf_op jit(solution)/shard_map/ppermute | solution.py:33
  172.5 32.6 %copy-start.21 = (bf16[64,1536]{1,0:T(8,128)(2,1)S(1)}, bf16[64,1536]{1,0:T(8,128)(2,1)}, u32[]{:S(2)}) copy-start(bf16[64,1536]{1,0:T(8,128)(2,1)} %copy-done.20) | copy-start | bytes 589828
  172.6 9.2 %collective-permute-start.39 = (bf16[32,4096]{1,0:T(8,128)(2,1)S(1)}, bf16[32,4096]{1,0:T(8,128)(2,1)S(1)}, u32[]{:S(2)}, u32[]{:S(2)}) collective-permute-start(bf16[32,4096]{1,0:T(8,128)(2,1)S(1)} %add_convert_fusion.1), channel_id=1, source_target_pairs={{0,4},{1,5},{4,8},{5,9},{8,12},{9,13},{12,14},{13,15},{14,10},{15,... | collective-permute-start | bytes 786440 | tf_op jit(solution)/shard_map/ppermute | solution.py:33
  174.7 9.2 %collective-permute-start.35 = (bf16[32,4096]{1,0:T(8,128)(2,1)S(1)}, bf16[32,4096]{1,0:T(8,128)(2,1)S(1)}, u32[]{:S(2)}, u32[]{:S(2)}) collective-permute-start(bf16[32,4096]{1,0:T(8,128)(2,1)S(1)} %add_convert_fusion.4), channel_id=1, source_target_pairs={{4,0},{5,1},{8,4},{9,5},{12,8},{13,9},{14,12},{15,13},{10,14},{11,... | collective-permute-start | bytes 786440 | tf_op jit(solution)/shard_map/ppermute | solution.py:33
  174.9 14.7 %collective-permute-start.32 = (bf16[32,4096]{1,0:T(8,128)(2,1)S(1)}, bf16[32,4096]{1,0:T(8,128)(2,1)S(1)}, u32[]{:S(2)}, u32[]{:S(2)}) collective-permute-start(bf16[32,4096]{1,0:T(8,128)(2,1)S(1)} %add_convert_fusion.6), channel_id=1, source_target_pairs={{4,0},{5,1},{8,4},{9,5},{12,8},{13,9},{14,12},{15,13},{10,14},{11,... | collective-permute-start | bytes 786440 | tf_op jit(solution)/shard_map/ppermute | solution.py:33
  176.5 13.2 %collective-permute-start.28 = (bf16[32,4096]{1,0:T(8,128)(2,1)S(1)}, bf16[32,4096]{1,0:T(8,128)(2,1)S(1)}, u32[]{:S(2)}, u32[]{:S(2)}) collective-permute-start(bf16[32,4096]{1,0:T(8,128)(2,1)S(1)} %add_convert_fusion.9), channel_id=1, source_target_pairs={{0,4},{1,5},{4,8},{5,9},{8,12},{9,13},{12,14},{13,15},{14,10},{15,... | collective-permute-start | bytes 786440 | tf_op jit(solution)/shard_map/ppermute | solution.py:33
  181.9 18.0 %collective-permute-start.40 = (bf16[32,4096]{1,0:T(8,128)(2,1)S(1)}, bf16[32,4096]{1,0:T(8,128)(2,1)S(1)}, u32[]{:S(2)}, u32[]{:S(2)}) collective-permute-start(bf16[32,4096]{1,0:T(8,128)(2,1)S(1)} %add_convert_fusion), channel_id=1, source_target_pairs={{0,4},{1,5},{4,8},{5,9},{8,12},{9,13},{12,14},{13,15},{14,10},{15,... | collective-permute-start | bytes 786440 | tf_op jit(solution)/shard_map/ppermute | solution.py:33
  184.0 10.7 %collective-permute-start.36 = (bf16[32,4096]{1,0:T(8,128)(2,1)S(1)}, bf16[32,4096]{1,0:T(8,128)(2,1)S(1)}, u32[]{:S(2)}, u32[]{:S(2)}) collective-permute-start(bf16[32,4096]{1,0:T(8,128)(2,1)S(1)} %add_convert_fusion.3), channel_id=1, source_target_pairs={{4,0},{5,1},{8,4},{9,5},{12,8},{13,9},{14,12},{15,13},{10,14},{11,... | collective-permute-start | bytes 786440 | tf_op jit(solution)/shard_map/ppermute | solution.py:33
  189.7 10.2 %collective-permute-start.33 = (bf16[32,4096]{1,0:T(8,128)(2,1)S(1)}, bf16[32,4096]{1,0:T(8,128)(2,1)S(1)}, u32[]{:S(2)}, u32[]{:S(2)}) collective-permute-start(bf16[32,4096]{1,0:T(8,128)(2,1)S(1)} %add_convert_fusion.5), channel_id=1, source_target_pairs={{4,0},{5,1},{8,4},{9,5},{12,8},{13,9},{14,12},{15,13},{10,14},{11,... | collective-permute-start | bytes 786440 | tf_op jit(solution)/shard_map/ppermute | solution.py:33
  189.8 8.8 %collective-permute-start.29 = (bf16[32,4096]{1,0:T(8,128)(2,1)S(1)}, bf16[32,4096]{1,0:T(8,128)(2,1)S(1)}, u32[]{:S(2)}, u32[]{:S(2)}) collective-permute-start(bf16[32,4096]{1,0:T(8,128)(2,1)S(1)} %add_convert_fusion.8), channel_id=1, source_target_pairs={{0,4},{1,5},{4,8},{5,9},{8,12},{9,13},{12,14},{13,15},{14,10},{15,... | collective-permute-start | bytes 786440 | tf_op jit(solution)/shard_map/ppermute | solution.py:33
  194.8 6.4 %collective-permute-start.37 = (bf16[32,4096]{1,0:T(8,128)(2,1)S(1)}, bf16[32,4096]{1,0:T(8,128)(2,1)S(1)}, u32[]{:S(2)}, u32[]{:S(2)}) collective-permute-start(bf16[32,4096]{1,0:T(8,128)(2,1)S(1)} %add_convert_fusion.2), channel_id=1, source_target_pairs={{4,0},{5,1},{8,4},{9,5},{12,8},{13,9},{14,12},{15,13},{10,14},{11,... | collective-permute-start | bytes 786440 | tf_op jit(solution)/shard_map/ppermute | solution.py:33
  198.7 6.4 %collective-permute-start.30 = (bf16[32,4096]{1,0:T(8,128)(2,1)S(1)}, bf16[32,4096]{1,0:T(8,128)(2,1)S(1)}, u32[]{:S(2)}, u32[]{:S(2)}) collective-permute-start(bf16[32,4096]{1,0:T(8,128)(2,1)S(1)} %add_convert_fusion.7), channel_id=1, source_target_pairs={{0,4},{1,5},{4,8},{5,9},{8,12},{9,13},{12,14},{13,15},{14,10},{15,... | collective-permute-start | bytes 786440 | tf_op jit(solution)/shard_map/ppermute | solution.py:33
  (17 other events, 30.5 us)
